TPU v7x, 128 devices: a whole 4x4x4 slice. The times are simulated.
128 devices in a mesh: pts: 32 (over z, x, core), rep: 4 (over y).
Axes of the slice: x: 4, y: 4, z: 4, core: 2. Of those that a mesh axis runs over, the one named last changes fastest.
Arguments:
- target_xyz: float32 [3, 32768], P(None, 'pts'), may hold values from 0 to 1
- source_xyz: float32 [3, 65536], P(None, ('pts', 'rep')), may hold values from 0 to 1
- target_count: int32 [32], P('pts'), may hold values from 1 to 1024, as said below
- source_count: int32 [128], P(('pts', 'rep')), may hold values from 1 to 512, as said below
- psi: bfloat16 [32768, 256], P('pts'), may hold values from -6 to 6
- omega: bfloat16 [65536, 256], P(('pts', 'rep')), may hold values from -6 to 6
Outputs:
- range_sketch: float32 [32768, 256], P('pts')
- corange_sketch: float32 [65536, 256], P(('pts', 'rep'))
- core: float32 [256, 256], replicated
- range_gram: float32 [256, 256], replicated
- corange_gram: float32 [256, 256], replicated
Inputs may be any that keep to these rules, and one draw needn't show every extreme that they name: `target_count`: each group holds 1 to 1024 live targets; some group holds exactly 1024. `source_count`: each shard holds 1 to 512 live sources; some shard holds exactly 512.
All inputs are finite; a program needn't handle non-finite values.
Results may differ from a plain program's by a relative error of at most 0.0003.
The roundings to bfloat16 on the way count: a program that leaves them out, or rounds other values in their place, can miss the bound.
Values may be sent and summed in bfloat16 or wider, within the bound.
No kernel may reach another device: no remote copies, remote signals or barrier semaphores. Data moves between devices by JAX's collectives and lax.ppermute only.
A program may use at most 64 MiB of HBM per device.

v0:
```python
import math

import jax
import jax.numpy as jnp
from jax import lax
from jax.experimental import pallas as pl
from jax.experimental.pallas import tpu as pltpu
from jax.sharding import Mesh, PartitionSpec as P


SHIFT = 1.05
SPREAD = 8.0
ZN, XN, CN, YN = 4, 4, 2, 4
ALL = ("z", "x", "c", "y")
R = 256
TCAP, SCAP = 1024, 512
TQ = TCAP // YN
GRAN = 16
NT = ZN * XN
NS = CN * YN
TC = 256
SC = 512
TH = TQ // 2
TPAY = TH + 32
SPAY = SCAP + 64
FAR = 4.0
F32 = jnp.float32
BF16 = jnp.bfloat16


def three_pieces(v):
    hi = v.astype(BF16)
    rest = v - hi.astype(F32)
    mid = rest.astype(BF16)
    low = (rest - mid.astype(F32)).astype(BF16)
    return hi, mid, low


def pack_kernel(where_ref, txyz_ref, sxyz_ref, psi_ref, omega_ref, apay_ref, bpay_ref, spay_ref, cols, quarter):
    yq = where_ref[0]
    tcount = where_ref[1]
    scount = where_ref[2]
    rows16 = lax.broadcasted_iota(jnp.int32, (GRAN, R), 0)
    cols[...] = jnp.concatenate(
        [txyz_ref[...], jnp.zeros((5, TCAP), F32)], axis=0
    ).T
    for a in range(TQ // GRAN):
        start = pl.multiple_of((a * YN + yq) * GRAN, GRAN)
        block = psi_ref[pl.ds(start, GRAN), :]
        half = (apay_ref, bpay_ref)[a * GRAN // TH]
        at = a * GRAN % TH
        half[at:at + GRAN, :] = jnp.where(
            rows16 + start < tcount, block, jnp.zeros_like(block)
        )
        quarter[a * GRAN:(a + 1) * GRAN, :] = cols[pl.ds(start, GRAN), :]
    step = GRAN * YN
    tlive = (tcount // step) * GRAN + jnp.clip(tcount % step - yq * GRAN, 0, GRAN)
    sub = lax.broadcasted_iota(jnp.int32, (8, TQ), 0)
    tpos = quarter[...].T
    tpos = jnp.where((sub == 1) | (sub == 2), tpos * SPREAD, tpos)
    tpos = jnp.where(sub == 3, tlive.astype(F32), tpos)
    tail = jnp.zeros((8, R), BF16)
    apay_ref[TH:TPAY, :] = jnp.concatenate([*three_pieces(tpos), tail], axis=0)
    srow = lax.broadcasted_iota(jnp.int32, (SCAP, R), 0)
    om = omega_ref[...]
    spay_ref[0:SCAP, :] = jnp.where(srow < scount, om, jnp.zeros_like(om))
    for h in range(SCAP // R):
        part = jnp.concatenate(
            [sxyz_ref[:, h * R:(h + 1) * R], jnp.zeros((5, R), F32)], axis=0
        )
        part = jnp.where((sub == 1) | (sub == 2), part * SPREAD, part)
        part = jnp.where(sub == 0, part + SHIFT, part)
        part = jnp.where(sub == 3, (scount - h * R).clip(0, R).astype(F32), part)
        base = SCAP + 32 * h
        spay_ref[base:base + 32, :] = jnp.concatenate([*three_pieces(part), tail], axis=0)


def pack(where, txyz, sxyz, psi, omega):
    vm = pl.BlockSpec(memory_space=pltpu.VMEM)
    return pl.pallas_call(
        pack_kernel,
        out_shape=(
            jax.ShapeDtypeStruct((TPAY, R), BF16),
            jax.ShapeDtypeStruct((TH, R), BF16),
            jax.ShapeDtypeStruct((SPAY, R), BF16),
        ),
        in_specs=[pl.BlockSpec(memory_space=pltpu.SMEM), vm, vm, vm, vm],
        out_specs=(vm, vm, vm),
        scratch_shapes=[pltpu.VMEM((TCAP, 8), F32), pltpu.VMEM((TQ, 8), F32)],
    )(where, txyz, sxyz, psi, omega)


def join(ref, *at):
    lo = at[-1]
    lead = at[:-1]
    v = ref[(*lead, slice(lo, lo + 32), slice(None))].astype(F32)
    return v[0:8] + v[8:16] + v[16:24]


def ceil16(n):
    return ((n + GRAN - 1) // GRAN) * GRAN


def sketch_kernel(a0, a1, a2, a3, b0, b1, b2, b3, s0, s1, ya0, ya1, ya2, ya3,
                  yb0, yb1, yb2, yb3, z0, z1, psic, tpos, omc, spos, srow,
                  bcx, bcy, bcz, yc, zc, cntv, cnts, sem):
    ain, bin_, sin = (a0, a1, a2, a3), (b0, b1, b2, b3), (s0, s1)
    yas, ybs, zouts = (ya0, ya1, ya2, ya3), (yb0, yb1, yb2, yb3), (z0, z1)
    for k in range(NT):
        cntv[k:k + 1, :] = join(ain[k // ZN], k % ZN, TH)[3:4, 0:128].astype(jnp.int32)
    for k in range(NS):
        both = [join(sin[k // YN], k % YN, SCAP + 32 * h)[3:4, 0:128] for h in range(SCAP // R)]
        cntv[NT + k:NT + k + 1, :] = sum(both).astype(jnp.int32)
    fetch_counts = pltpu.make_async_copy(cntv, cnts, sem)
    fetch_counts.start()
    fetch_counts.wait()
    toff = [jnp.int32(0)]
    for k in range(NT):
        dx, dz = k // ZN, k % ZN
        off = pl.multiple_of(toff[k], GRAN)
        psic[pl.ds(off, TH), :] = ain[dx][dz, 0:TH, :]
        psic[pl.ds(off + TH, TH), :] = bin_[dz][dx]
        tpos[pl.ds(off, TQ), :] = join(ain[dx], dz, TH).T
        toff.append(toff[k] + ceil16(cnts[k, 0]))
    tend = pl.multiple_of(toff[NT], GRAN)
    psic[pl.ds(tend, TC), :] = jnp.zeros((TC, R), BF16)
    tpos[pl.ds(tend, TC), :] = jnp.zeros((TC, 8), F32)
    soff = [jnp.int32(0)]
    for k in range(NS):
        ref, d = sin[k // YN], k % YN
        off = pl.multiple_of(soff[k], GRAN)
        omc[pl.ds(off, SCAP), :] = ref[d, 0:SCAP, :]
        for h in range(SCAP // R):
            spos[pl.ds(off + h * R, R), :] = join(ref, d, SCAP + 32 * h).T
        soff.append(soff[k] + ceil16(cnts[NT + k, 0]))
    send = pl.multiple_of(soff[NS], GRAN)
    omc[pl.ds(send, SC), :] = jnp.zeros((SC, R), BF16)
    spos[pl.ds(send, SC), :] = jnp.full((SC, 8), FAR, F32)
    nt = (toff[NT] + TC - 1) // TC
    ns = (soff[NS] + SC - 1) // SC

    def prepare(si, carry):
        at = pl.multiple_of(si * SC, SC)
        srow[si] = spos[pl.ds(at, SC), :].T
        zc[pl.ds(at, SC), :] = jnp.zeros((SC, R), F32)
        return carry

    lax.fori_loop(0, ns, prepare, 0)

    def over_targets(ti, carry):
        ta = pl.multiple_of(ti * TC, TC)
        tp = tpos[pl.ds(ta, TC), :]
        bcx[...] = jnp.broadcast_to(tp[:, 0:1], (TC, 128))
        bcy[...] = jnp.broadcast_to(tp[:, 1:2], (TC, 128))
        bcz[...] = jnp.broadcast_to(tp[:, 2:3], (TC, 128))
        yc[pl.ds(ta, TC), :] = jnp.zeros((TC, R), F32)

        def over_sources(si, inner):
            sa = pl.multiple_of(si * SC, SC)
            pieces = []
            for j in range(SC // 128):
                lanes = slice(j * 128, (j + 1) * 128)
                dx = bcx[...] - srow[si, 0:1, lanes]
                dy = bcy[...] - srow[si, 1:2, lanes]
                dz = bcz[...] - srow[si, 2:3, lanes]
                pieces.append(lax.rsqrt(dx * dx + dy * dy + dz * dz).astype(BF16))
            tile = jnp.concatenate(pieces, axis=1)
            yc[pl.ds(ta, TC), :] += jnp.dot(
                tile, omc[pl.ds(sa, SC), :], preferred_element_type=F32
            )
            zc[pl.ds(sa, SC), :] += lax.dot_general(
                tile, psic[pl.ds(ta, TC), :], (((0,), (0,)), ((), ())),
                preferred_element_type=F32,
            )
            return inner

        lax.fori_loop(0, ns, over_sources, 0)
        return carry

    lax.fori_loop(0, nt, over_targets, 0)
    for k in range(NT):
        dx, dz = k // ZN, k % ZN
        off = pl.multiple_of(toff[k], GRAN)
        yas[dx][dz] = yc[pl.ds(off, TH), :]
        ybs[dz][dx] = yc[pl.ds(off + TH, TH), :]
    for k in range(NS):
        off = pl.multiple_of(soff[k], GRAN)
        zouts[k // YN][k % YN] = zc[pl.ds(off, SCAP), :]


def sketch(ain, bin_, sin):
    vm = pl.BlockSpec(memory_space=pltpu.VMEM)
    trows = NT * TQ + 2 * TC
    srows = NS * SCAP + 2 * SC
    return pl.pallas_call(
        sketch_kernel,
        out_shape=(
            *[jax.ShapeDtypeStruct((ZN, TH, R), F32)] * (2 * XN),
            *[jax.ShapeDtypeStruct((YN, SCAP, R), F32)] * CN,
        ),
        in_specs=[vm] * 10,
        out_specs=(vm,) * 10,
        scratch_shapes=[
            pltpu.VMEM((trows, R), BF16),
            pltpu.VMEM((trows, 8), F32),
            pltpu.VMEM((srows, R), BF16),
            pltpu.VMEM((srows, 8), F32),
            pltpu.VMEM((srows // SC, 8, SC), F32),
            pltpu.VMEM((TC, 128), F32),
            pltpu.VMEM((TC, 128), F32),
            pltpu.VMEM((TC, 128), F32),
            pltpu.VMEM((trows, R), F32),
            pltpu.VMEM((srows, R), F32),
            pltpu.VMEM((NT + NS, 128), jnp.int32),
            pltpu.SMEM((NT + NS, 128), jnp.int32),
            pltpu.SemaphoreType.DMA(()),
        ],
    )(*ain, *bin_, *sin)


def finish_kernel(where_ref, a0, a1, a2, a3, b0, b1, b2, b3, z0, z1, z2, z3, pa, pb,
                  yfin_ref, zfin_ref, keep_ref, send_ref, *, yscale, zscale, tn, sn):
    yq, tcount, scount, core = where_ref[0], where_ref[1], where_ref[2], where_ref[3]
    row = lax.broadcasted_iota(jnp.int32, (TH, R), 0)
    for h, part in enumerate(((a0, a1, a2, a3), (b0, b1, b2, b3))):
        total = (part[0][...] + part[1][...]) + (part[2][...] + part[3][...])
        q = row + h * TH
        slot = (q // GRAN) * (GRAN * YN) + yq * GRAN + q % GRAN
        yfin_ref[h * TH:(h + 1) * TH, :] = jnp.where(slot < tcount, total * yscale, 0.0)
    srow = lax.broadcasted_iota(jnp.int32, (SCAP, R), 0)
    total = (z0[...] + z1[...]) + (z2[...] + z3[...])
    zfin_ref[...] = jnp.where(srow < scount, total * zscale, 0.0)
    psi = jnp.concatenate([pa[0:TH, :], pb[...]], axis=0).astype(F32)
    y, z = yfin_ref[...], zfin_ref[...]
    hi = lax.Precision.HIGHEST
    dims = (((0,), (0,)), ((), ()))
    parts = (
        lax.dot_general(psi, y, dims, precision=hi, preferred_element_type=F32) / math.sqrt(tn),
        lax.dot_general(y, y, dims, precision=hi, preferred_element_type=F32) / tn,
        lax.dot_general(z, z, dims, precision=hi, preferred_element_type=F32) / sn,
    )
    first = core == 0
    for k in range(3):
        top, low = parts[k][0:R // 2, :], parts[k][R // 2:, :]
        keep_ref[k] = jnp.where(first, top, low)
        send_ref[k] = jnp.where(first, low, top)


def finish(where, a, b, z, pa, pb):
    tn, sn = TCAP * NT * CN, SCAP * NT * NS
    vm = pl.BlockSpec(memory_space=pltpu.VMEM)
    half = jax.ShapeDtypeStruct((3, R // 2, R), F32)

    def body(*refs):
        finish_kernel(
            *refs, yscale=2.0 / math.sqrt(sn), zscale=2.0 / math.sqrt(tn), tn=tn, sn=sn
        )

    return pl.pallas_call(
        body,
        out_shape=(
            jax.ShapeDtypeStruct((TQ, R), F32),
            jax.ShapeDtypeStruct((SCAP, R), F32),
            half,
            half,
        ),
        in_specs=[pl.BlockSpec(memory_space=pltpu.SMEM)] + [vm] * 14,
        out_specs=(vm,) * 4,
    )(where, *a, *b, *z, pa, pb)


def place_kernel(where_ref, *refs):
    ys, own, other = refs[0:YN], refs[YN:YN + ZN], refs[YN + ZN]
    yout, outs = refs[YN + ZN + 1], refs[YN + ZN + 2:]
    yq, core, z = where_ref[0], where_ref[3], where_ref[4]
    for d in range(YN):
        q = lax.rem(yq + d, YN)
        for a in range(TQ // GRAN):
            at = pl.multiple_of((a * YN + q) * GRAN, GRAN)
            yout[pl.ds(at, GRAN), :] = ys[d][a * GRAN:(a + 1) * GRAN, :]
    share = R // CN // ZN
    for d in range(ZN):
        q = lax.rem(z + d, ZN)
        at = pl.multiple_of((core * ZN + q) * share, share)
        far = pl.multiple_of(((1 - core) * ZN + q) * share, share)
        for k in range(3):
            outs[k][pl.ds(at, share), :] = own[d][k]
            outs[k][pl.ds(far, share), :] = other[d, k]


def place(where, ys, own, other):
    vm = pl.BlockSpec(memory_space=pltpu.VMEM)
    return pl.pallas_call(
        place_kernel,
        out_shape=(
            jax.ShapeDtypeStruct((TCAP, R), F32),
            *[jax.ShapeDtypeStruct((R, R), F32)] * 3,
        ),
        in_specs=[pl.BlockSpec(memory_space=pltpu.SMEM)] + [vm] * (YN + ZN + 1),
        out_specs=(vm,) * 4,
    )(where, *ys, *own, other)


def fetch(v, axis, d):
    n = lax.axis_size(axis)
    return lax.ppermute(v, axis, [((i + d) % n, i) for i in range(n)])


def give(v, axis, d):
    n = lax.axis_size(axis)
    return lax.ppermute(v, axis, [(i, (i + d) % n) for i in range(n)])


def ring(v, axis):
    return [v] + [fetch(v, axis, d) for d in range(1, lax.axis_size(axis))]


def gathered_sum(v, axis):
    p = ring(v, axis)
    return (p[0] + p[2]) + (p[1] + p[3])


def returned(vs, axis):
    return [vs[0]] + [give(vs[d], axis, d) for d in range(1, len(vs))]


def steps(target_xyz, source_xyz, target_count, source_count, psi, omega):
    yq, core, z = (lax.axis_index(n) for n in ("y", "c", "z"))
    where = jnp.stack([yq, target_count[0], source_count[0], core, z]).astype(jnp.int32)
    apay, bpay, spay = pack(where, target_xyz, source_xyz, psi, omega)
    arow = ring(apay, "z")
    brow = ring(bpay, "x")
    srow = ring(spay, "y")
    ain = ring(jnp.stack(arow), "x")
    bin_ = ring(jnp.stack(brow), "z")
    srep = jnp.stack(srow)
    sfar = fetch(srep, "c", 1)
    parts = sketch(ain, bin_, [srep, sfar])
    ya, yb, (z0, z1) = parts[0:4], parts[4:8], parts[8:10]
    zfar = give(z1, "c", 1)
    ax = returned(ya, "x")
    bz = returned(yb, "z")
    zmine = [z0[d] + zfar[d] for d in range(YN)]
    zs = returned(zmine, "y")
    ax = [(ax[0][d] + ax[1][d]) + (ax[2][d] + ax[3][d]) for d in range(ZN)]
    bz = [(bz[0][d] + bz[1][d]) + (bz[2][d] + bz[3][d]) for d in range(XN)]
    a = returned(ax, "z")
    b = returned(bz, "x")
    yfin, zfin, keep, send = finish(where, a, b, zs, apay, bpay)
    ys = ring(yfin, "y")
    half = keep + fetch(send, "c", 1)
    half = half.reshape(3, ZN, R // CN // ZN, R)
    chunks = [
        lax.dynamic_index_in_dim(half, lax.rem(z + d, ZN), 1, keepdims=False)
        for d in range(ZN)
    ]
    p = returned(chunks, "z")
    mine = (p[0] + p[1]) + (p[2] + p[3])
    mine = gathered_sum(gathered_sum(mine, "x"), "y")
    own = ring(mine, "z")
    other = fetch(jnp.stack(own), "c", 1)
    y, g0, g1, g2 = place(where, ys, own, other)
    return (y, zfin, g0, g1, g2)


def solution(mesh):
    grid = Mesh(mesh.devices.reshape(ZN, XN, CN, YN), ALL)
    pts = ("z", "x", "c")
    return jax.shard_map(
        steps,
        mesh=grid,
        in_specs=(P(None, pts), P(None, ALL), P(pts), P(ALL), P(pts, None), P(ALL, None)),
        out_specs=(P(pts, None), P(ALL, None), P(), P(), P()),
        check_vma=False,
    )
```

profile of v0, /device:TPU:1, one launch (start us, length us, event | category | flops | bytes accessed | tf_op | source)
XLA Modules:
  0.0 228.9 jit_solution(3118290242855449730)
XLA Ops:
  4.8 3.6 %collective-permute-start.12 = (bf16[576,256]{1,0:T(8,128)(2,1)}, bf16[576,256]{1,0:T(8,128)(2,1)S(1)}, u32[]{:S(2)}, u32[]{:S(2)}) collective-permute-start(bf16[576,256]{1,0:T(8,128)(2,1)} %get-tuple-element.28), channel_id=1, source_target_pairs={{1,0},{2,1},{3,2},{0,3},{5,4},{6,5},{7,6},{4,7},{9,8},{10,9},{11,1... | collective-permute-start | bytes 884744 | tf_op jit(solution)/shard_map/ppermute | solution.py:306
  9.3 11.1 %collective-permute-done.12 = bf16[576,256]{1,0:T(8,128)(2,1)S(1)} collective-permute-done((bf16[576,256]{1,0:T(8,128)(2,1)}, bf16[576,256]{1,0:T(8,128)(2,1)S(1)}, u32[]{:S(2)}, u32[]{:S(2)}) %collective-permute-start.12) | collective-permute-done | bytes 294944 | tf_op jit(solution)/shard_map/ppermute | solution.py:306
  20.5 4.8 %collective-permute-done.14 = bf16[576,256]{1,0:T(8,128)(2,1)S(1)} collective-permute-done((bf16[576,256]{1,0:T(8,128)(2,1)}, bf16[576,256]{1,0:T(8,128)(2,1)S(1)}, u32[]{:S(2)}, u32[]{:S(2)}) %collective-permute-start.14) | collective-permute-done | bytes 294944 | tf_op jit(solution)/shard_map/ppermute | solution.py:306
  31.2 3.8 %collective-permute-start = (bf16[160,256]{1,0:T(8,128)(2,1)S(1)}, bf16[160,256]{1,0:T(8,128)(2,1)S(1)}, u32[]{:S(2)}, u32[]{:S(2)}) collective-permute-start(bf16[160,256]{1,0:T(8,128)(2,1)S(1)} %copy-done.17), channel_id=1, source_target_pairs={{32,0},{64,32},{96,64},{0,96},{33,1},{65,33},{97,65},{1,97},{34,2}... | collective-permute-start | bytes 245768 | tf_op jit(solution)/shard_map/ppermute | solution.py:306
  35.1 3.0 %collective-permute-start.10 = (bf16[4,128,256]{2,1,0:T(8,128)(2,1)S(1)}, bf16[4,128,256]{2,1,0:T(8,128)(2,1)S(1)}, u32[]{:S(2)}, u32[]{:S(2)}) collective-permute-start(bf16[4,128,256]{2,1,0:T(8,128)(2,1)S(1)} %pad_maximum_fusion.3.b0), channel_id=1, source_target_pairs={{64,0},{96,32},{0,64},{32,96},{65,1},{97,33},{1,65},{33,97},{66,2}... | collective-permute-start | bytes 786440 | tf_op jit(solution)/shard_map/ppermute | solution.py:306
  40.7 4.1 %collective-permute-done.1 = bf16[160,256]{1,0:T(8,128)(2,1)S(1)} collective-permute-done((bf16[160,256]{1,0:T(8,128)(2,1)S(1)}, bf16[160,256]{1,0:T(8,128)(2,1)S(1)}, u32[]{:S(2)}, u32[]{:S(2)}) %collective-permute-start.1) | collective-permute-done | bytes 81952 | tf_op jit(solution)/shard_map/ppermute | solution.py:306
  44.8 3.2 %collective-permute-done.2 = bf16[160,256]{1,0:T(8,128)(2,1)S(1)} collective-permute-done((bf16[160,256]{1,0:T(8,128)(2,1)S(1)}, bf16[160,256]{1,0:T(8,128)(2,1)S(1)}, u32[]{:S(2)}, u32[]{:S(2)}) %collective-permute-start.2) | collective-permute-done | bytes 81952 | tf_op jit(solution)/shard_map/ppermute | solution.py:306
  50.6 3.4 %collective-permute-done.11.b3 = bf16[4,128,256]{2,1,0:T(8,128)(2,1)S(1)} collective-permute-done((bf16[4,128,256]{2,1,0:T(8,128)(2,1)S(1)}, bf16[4,128,256]{2,1,0:T(8,128)(2,1)S(1)}, u32[]{:S(2)}, u32[]{:S(2)}) %collective-permute-start.11) | collective-permute-done | bytes 262176 | tf_op jit(solution)/shard_map/ppermute | solution.py:306
  54.0 7.4 %collective-permute-done.9.b1 = bf16[4,128,256]{2,1,0:T(8,128)(2,1)S(1)} collective-permute-done((bf16[4,128,256]{2,1,0:T(8,128)(2,1)S(1)}, bf16[4,128,256]{2,1,0:T(8,128)(2,1)S(1)}, u32[]{:S(2)}, u32[]{:S(2)}) %collective-permute-start.9) | collective-permute-done | bytes 262176 | tf_op jit(solution)/shard_map/ppermute | solution.py:306
  61.4 6.0 %collective-permute-done.5.a3 = bf16[4,160,256]{2,1,0:T(8,128)(2,1)S(1)} collective-permute-done((bf16[4,160,256]{2,1,0:T(8,128)(2,1)S(1)}, bf16[4,160,256]{2,1,0:T(8,128)(2,1)S(1)}, u32[]{:S(2)}, u32[]{:S(2)}) %collective-permute-start.5) | collective-permute-done | bytes 327712 | tf_op jit(solution)/shard_map/ppermute | solution.py:306
  69.2 20.5 %shard_map.102 = (f32[4,128,256]{2,1,0:T(8,128)}, f32[4,128,256]{2,1,0:T(8,128)}, f32[4,128,256]{2,1,0:T(8,128)}, f32[4,128,256]{2,1,0:T(8,128)}, f32[4,128,256]...) custom-call(bf16[4,160,256]{2,1,0:T(8,128)(2,1)} %copy-done.1, ...), custom_call_target="tpu_custom_call" | custom-call | tf_op jit(solution)/shard_map/pallas_call | solution.py:195
  93.0 23.4 %collective-permute-done.22 = f32[4,128,256]{2,1,0:T(8,128)S(1)} collective-permute-done((f32[4,128,256]{2,1,0:T(8,128)}, f32[4,128,256]{2,1,0:T(8,128)S(1)}, u32[]{:S(2)}, u32[]{:S(2)}) %collective-permute-start.22) | collective-permute-done | bytes 524320 | tf_op jit(solution)/shard_map/ppermute | solution.py:311
  118.7 2.8 %fusion = (f32[512,256]{1,0:T(8,128)S(1)}, f32[512,256]{1,0:T(8,128)S(1)}, f32[512,256]{1,0:T(8,128)S(1)}, f32[512,256]{1,0:T(8,128)}) fusion(f32[4,512,256]{2,1,0:T(8,128)S(1)} %collective-permute-done.28, f32[4,512,256]{2,1,0:T(8,128)} %get-tuple-element.37), kind=kLoop, calls=%fused_computation.2 | loop fusion | flops 524288 | bytes 6291456 | tf_op jit(solution)/shard_map/add | solution.py:343
  121.9 2.5 %collective-permute-start.31 = (f32[512,256]{1,0:T(8,128)S(1)}, f32[512,256]{1,0:T(8,128)S(1)}, u32[]{:S(2)}, u32[]{:S(2)}) collective-permute-start(f32[512,256]{1,0:T(8,128)S(1)} %get-tuple-element.47), channel_id=1, source_target_pairs={{0,3},{1,0},{2,1},{3,2},{4,7},{5,4},{6,5},{7,6},{8,11},{9,8},{10,9... | collective-permute-start | bytes 1572872 | tf_op jit(solution)/shard_map/ppermute | solution.py:311
  125.2 5.4 %collective-permute-done.17 = f32[4,128,256]{2,1,0:T(8,128)S(1)} collective-permute-done((f32[4,128,256]{2,1,0:T(8,128)}, f32[4,128,256]{2,1,0:T(8,128)S(1)}, u32[]{:S(2)}, u32[]{:S(2)}) %collective-permute-start.17) | collective-permute-done | bytes 524320 | tf_op jit(solution)/shard_map/ppermute | solution.py:311
  130.6 8.6 %collective-permute-done.18 = f32[4,128,256]{2,1,0:T(8,128)S(1)} collective-permute-done((f32[4,128,256]{2,1,0:T(8,128)}, f32[4,128,256]{2,1,0:T(8,128)S(1)}, u32[]{:S(2)}, u32[]{:S(2)}) %collective-permute-start.18) | collective-permute-done | bytes 524320 | tf_op jit(solution)/shard_map/ppermute | solution.py:311
  139.2 3.3 %collective-permute-start.26 = (f32[128,256]{1,0:T(8,128)S(1)}, f32[128,256]{1,0:T(8,128)S(1)}, u32[]{:S(2)}, u32[]{:S(2)}) collective-permute-start(f32[128,256]{1,0:T(8,128)S(1)} %get-tuple-element.52), channel_id=1, source_target_pairs={{0,16},{8,24},{16,0},{24,8},{1,17},{9,25},{17,1},{25,9},{2,18},{10... | collective-permute-start | bytes 393224 | tf_op jit(solution)/shard_map/ppermute | solution.py:311
  143.3 2.5 %collective-permute-start.27 = (f32[128,256]{1,0:T(8,128)S(1)}, f32[128,256]{1,0:T(8,128)S(1)}, u32[]{:S(2)}, u32[]{:S(2)}) collective-permute-start(f32[128,256]{1,0:T(8,128)S(1)} %get-tuple-element.51), channel_id=1, source_target_pairs={{0,24},{8,0},{16,8},{24,16},{1,25},{9,1},{17,9},{25,17},{2,26},{10... | collective-permute-start | bytes 393224 | tf_op jit(solution)/shard_map/ppermute | solution.py:311
  145.8 2.8 %collective-permute-done.27.refs_8_ = f32[128,256]{1,0:T(8,128)S(1)} collective-permute-done((f32[128,256]{1,0:T(8,128)S(1)}, f32[128,256]{1,0:T(8,128)S(1)}, u32[]{:S(2)}, u32[]{:S(2)}) %collective-permute-start.27) | collective-permute-done | bytes 131104 | tf_op jit(solution)/shard_map/ppermute | solution.py:311
  148.6 3.0 %collective-permute-start.20 = (f32[128,256]{1,0:T(8,128)S(1)}, f32[128,256]{1,0:T(8,128)S(1)}, u32[]{:S(2)}, u32[]{:S(2)}) collective-permute-start(f32[128,256]{1,0:T(8,128)S(1)} %get-tuple-element.56), channel_id=1, source_target_pairs={{0,64},{32,96},{64,0},{96,32},{1,65},{33,97},{65,1},{97,33},{2,66}... | collective-permute-start | bytes 393224 | tf_op jit(solution)/shard_map/ppermute | solution.py:311
  157.0 4.1 %shard_map.103 = (f32[256,256]{1,0:T(8,128)}, f32[512,256]{1,0:T(8,128)}, f32[3,128,256]{2,1,0:T(8,128)}, f32[3,128,256]{2,1,0:T(8,128)}) custom-call(s32[5]{0:T(128)} %stack.75.where_ref.refs_0_, f32[128,256]{1,0:T(8,128)} %get-tuple-element.58.refs_1_, f32[128,256]{1,0:T(8,128)} %copy-done.29, f32[128,256]{1,0:T(8,128)} %copy-done.30, ...), custom_call_target="tpu_custom_call" | custom-call | tf_op jit(solution)/shard_map/pallas_call | solution.py:259
  161.1 4.2 %collective-permute-start.35 = (f32[3,128,256]{2,1,0:T(8,128)}, f32[3,128,256]{2,1,0:T(8,128)S(1)}, u32[]{:S(2)}, u32[]{:S(2)}) collective-permute-start(f32[3,128,256]{2,1,0:T(8,128)} %get-tuple-element.41), channel_id=1, source_target_pairs={{4,0},{0,4},{5,1},{1,5},{6,2},{2,6},{7,3},{3,7},{12,8},{8,12},{13,... | collective-permute-start | bytes 1179656 | tf_op jit(solution)/shard_map/ppermute | solution.py:306
  170.7 3.2 %collective-permute-done.36 = f32[3,32,256]{2,1,0:T(8,128)S(1)} collective-permute-done((f32[3,32,256]{2,1,0:T(8,128)S(1)}, f32[3,32,256]{2,1,0:T(8,128)S(1)}, u32[]{:S(2)}, u32[]{:S(2)}) %collective-permute-start.36) | collective-permute-done | bytes 98336 | tf_op jit(solution)/shard_map/ppermute | solution.py:311
  175.7 3.3 %collective-permute-start.39 = (f32[3,32,256]{2,1,0:T(8,128)S(1)}, f32[3,32,256]{2,1,0:T(8,128)S(1)}, u32[]{:S(2)}, u32[]{:S(2)}) collective-permute-start(f32[3,32,256]{2,1,0:T(8,128)S(1)} %fusion.20), channel_id=1, source_target_pairs={{16,0},{24,8},{0,16},{8,24},{17,1},{25,9},{1,17},{9,25},{18,2},{26... | collective-permute-start | bytes 294920 | tf_op jit(solution)/shard_map/ppermute | solution.py:306
  179.1 4.3 %collective-permute-start.40 = (f32[3,32,256]{2,1,0:T(8,128)S(1)}, f32[3,32,256]{2,1,0:T(8,128)S(1)}, u32[]{:S(2)}, u32[]{:S(2)}) collective-permute-start(f32[3,32,256]{2,1,0:T(8,128)S(1)} %fusion.20), channel_id=1, source_target_pairs={{8,0},{16,8},{24,16},{0,24},{9,1},{17,9},{25,17},{1,25},{10,2},{18... | collective-permute-start | bytes 294920 | tf_op jit(solution)/shard_map/ppermute | solution.py:306
  190.0 3.2 %collective-permute-done.42 = f32[3,32,256]{2,1,0:T(8,128)S(1)} collective-permute-done((f32[3,32,256]{2,1,0:T(8,128)S(1)}, f32[3,32,256]{2,1,0:T(8,128)S(1)}, u32[]{:S(2)}, u32[]{:S(2)}) %collective-permute-start.42) | collective-permute-done | bytes 98336 | tf_op jit(solution)/shard_map/ppermute | solution.py:306
  194.2 2.8 %collective-permute-start.45 = (f32[3,32,256]{2,1,0:T(8,128)S(1)}, f32[3,32,256]{2,1,0:T(8,128)S(1)}, u32[]{:S(2)}, u32[]{:S(2)}) collective-permute-start(f32[3,32,256]{2,1,0:T(8,128)S(1)} %add_add_fusion.refs_4_), channel_id=1, source_target_pairs={{32,0},{64,32},{96,64},{0,96},{33,1},{65,33},{97,65},{1,97},{34,2}... | collective-permute-start | bytes 294920 | tf_op jit(solution)/shard_map/ppermute | solution.py:306
  199.7 2.5 %collective-permute-done.46.refs_6_ = f32[3,32,256]{2,1,0:T(8,128)S(1)} collective-permute-done((f32[3,32,256]{2,1,0:T(8,128)S(1)}, f32[3,32,256]{2,1,0:T(8,128)S(1)}, u32[]{:S(2)}, u32[]{:S(2)}) %collective-permute-start.46) | collective-permute-done | bytes 98336 | tf_op jit(solution)/shard_map/ppermute | solution.py:306
  202.8 5.7 %collective-permute-start.48 = (f32[4,3,32,256]{3,2,1,0:T(8,128)S(1)}, f32[4,3,32,256]{3,2,1,0:T(8,128)S(1)}, u32[]{:S(2)}, u32[]{:S(2)}) collective-permute-start(f32[4,3,32,256]{3,2,1,0:T(8,128)S(1)} %pad_maximum_fusion.1), channel_id=1, source_target_pairs={{4,0},{0,4},{5,1},{1,5},{6,2},{2,6},{7,3},{3,7},{12,8},{8,12},{13,... | collective-permute-start | bytes 1179656 | tf_op jit(solution)/shard_map/ppermute | solution.py:306
  210.0 6.3 %collective-permute-done.32.refs_1_ = f32[256,256]{1,0:T(8,128)S(1)} collective-permute-done((f32[256,256]{1,0:T(8,128)S(1)}, f32[256,256]{1,0:T(8,128)S(1)}, u32[]{:S(2)}, u32[]{:S(2)}) %collective-permute-start.32) | collective-permute-done | bytes 262176 | tf_op jit(solution)/shard_map/ppermute | solution.py:306
  218.3 6.3 %collective-permute-done.34.refs_3_ = f32[256,256]{1,0:T(8,128)S(1)} collective-permute-done((f32[256,256]{1,0:T(8,128)S(1)}, f32[256,256]{1,0:T(8,128)S(1)}, u32[]{:S(2)}, u32[]{:S(2)}) %collective-permute-start.34) | collective-permute-done | bytes 262176 | tf_op jit(solution)/shard_map/ppermute | solution.py:306
  226.1 2.8 %shard_map.104 = (f32[1024,256]{1,0:T(8,128)}, f32[256,256]{1,0:T(8,128)}, f32[256,256]{1,0:T(8,128)}, f32[256,256]{1,0:T(8,128)}) custom-call(s32[5]{0:T(128)} %stack.75.where_ref.refs_0_, f32[256,256]{1,0:T(8,128)} %get-tuple-element.39.refs_0_, f32[256,256]{1,0:T(8,128)} %copy-done.22, f32[256,256]{1,0:T(8,128)} %copy-done.23, f32[256,256]{1,0:T(8,128)} %copy-done.24, ...), custom_call_target="tpu_custom_call" | custom-call | tf_op jit(solution)/shard_map/pallas_call | solution.py:293
  (147 shorter events, 52.8 us)
Async XLA Ops:
  4.8 15.7 %collective-permute-start.12 = (bf16[576,256]{1,0:T(8,128)(2,1)}, bf16[576,256]{1,0:T(8,128)(2,1)S(1)}, u32[]{:S(2)}, u32[]{:S(2)}) collective-permute-start(bf16[576,256]{1,0:T(8,128)(2,1)} %get-tuple-element.28), channel_id=1, source_target_pairs={{1,0},{2,1},{3,2},{0,3},{5,4},{6,5},{7,6},{4,7},{9,8},{10,9},{11,1... | collective-permute-start | bytes 884744 | tf_op jit(solution)/shard_map/ppermute | solution.py:306
  8.3 12.2 %collective-permute-start.13 = (bf16[576,256]{1,0:T(8,128)(2,1)}, bf16[576,256]{1,0:T(8,128)(2,1)S(1)}, u32[]{:S(2)}, u32[]{:S(2)}) collective-permute-start(bf16[576,256]{1,0:T(8,128)(2,1)} %get-tuple-element.28), channel_id=1, source_target_pairs={{2,0},{3,1},{0,2},{1,3},{6,4},{7,5},{4,6},{5,7},{10,8},{11,9},{8,1... | collective-permute-start | bytes 884744 | tf_op jit(solution)/shard_map/ppermute | solution.py:306
  8.7 16.6 %collective-permute-start.14 = (bf16[576,256]{1,0:T(8,128)(2,1)}, bf16[576,256]{1,0:T(8,128)(2,1)S(1)}, u32[]{:S(2)}, u32[]{:S(2)}) collective-permute-start(bf16[576,256]{1,0:T(8,128)(2,1)} %get-tuple-element.28), channel_id=1, source_target_pairs={{3,0},{0,1},{1,2},{2,3},{7,4},{4,5},{5,6},{6,7},{11,8},{8,9},{9,10... | collective-permute-start | bytes 884744 | tf_op jit(solution)/shard_map/ppermute | solution.py:306
  26.4 41.7 %collective-permute-start.15 = (bf16[4,576,256]{2,1,0:T(8,128)(2,1)S(1)}, bf16[4,576,256]{2,1,0:T(8,128)(2,1)S(1)}, u32[]{:S(2)}, u32[]{:S(2)}) collective-permute-start(bf16[4,576,256]{2,1,0:T(8,128)(2,1)S(1)} %pad_maximum_fusion.s0), channel_id=1, source_target_pairs={{4,0},{0,4},{5,1},{1,5},{6,2},{2,6},{7,3},{3,7},{12,8},{8,12},{13,... | collective-permute-start | bytes 3538952 | tf_op jit(solution)/shard_map/ppermute | solution.py:306
  27.0 8.0 %collective-permute-start.8 = (bf16[128,256]{1,0:T(8,128)(2,1)S(1)}, bf16[128,256]{1,0:T(8,128)(2,1)S(1)}, u32[]{:S(2)}, u32[]{:S(2)}) collective-permute-start(bf16[128,256]{1,0:T(8,128)(2,1)S(1)} %copy-done.25), channel_id=1, source_target_pairs={{24,0},{0,8},{8,16},{16,24},{25,1},{1,9},{9,17},{17,25},{26,2},{2,... | collective-permute-start | bytes 196616 | tf_op jit(solution)/shard_map/ppermute | solution.py:306
  28.2 6.8 %collective-permute-start.6 = (bf16[128,256]{1,0:T(8,128)(2,1)S(1)}, bf16[128,256]{1,0:T(8,128)(2,1)S(1)}, u32[]{:S(2)}, u32[]{:S(2)}) collective-permute-start(bf16[128,256]{1,0:T(8,128)(2,1)S(1)} %copy-done.25), channel_id=1, source_target_pairs={{8,0},{16,8},{24,16},{0,24},{9,1},{17,9},{25,17},{1,25},{10,2},{18... | collective-permute-start | bytes 196616 | tf_op jit(solution)/shard_map/ppermute | solution.py:306
  31.2 7.8 %collective-permute-start = (bf16[160,256]{1,0:T(8,128)(2,1)S(1)}, bf16[160,256]{1,0:T(8,128)(2,1)S(1)}, u32[]{:S(2)}, u32[]{:S(2)}) collective-permute-start(bf16[160,256]{1,0:T(8,128)(2,1)S(1)} %copy-done.17), channel_id=1, source_target_pairs={{32,0},{64,32},{96,64},{0,96},{33,1},{65,33},{97,65},{1,97},{34,2}... | collective-permute-start | bytes 245768 | tf_op jit(solution)/shard_map/ppermute | solution.py:306
  35.1 15.6 %collective-permute-start.10 = (bf16[4,128,256]{2,1,0:T(8,128)(2,1)S(1)}, bf16[4,128,256]{2,1,0:T(8,128)(2,1)S(1)}, u32[]{:S(2)}, u32[]{:S(2)}) collective-permute-start(bf16[4,128,256]{2,1,0:T(8,128)(2,1)S(1)} %pad_maximum_fusion.3.b0), channel_id=1, source_target_pairs={{64,0},{96,32},{0,64},{32,96},{65,1},{97,33},{1,65},{33,97},{66,2}... | collective-permute-start | bytes 786440 | tf_op jit(solution)/shard_map/ppermute | solution.py:306
  38.0 6.8 %collective-permute-start.1 = (bf16[160,256]{1,0:T(8,128)(2,1)S(1)}, bf16[160,256]{1,0:T(8,128)(2,1)S(1)}, u32[]{:S(2)}, u32[]{:S(2)}) collective-permute-start(bf16[160,256]{1,0:T(8,128)(2,1)S(1)} %copy-done.17), channel_id=1, source_target_pairs={{64,0},{96,32},{0,64},{32,96},{65,1},{97,33},{1,65},{33,97},{66,2}... | collective-permute-start | bytes 245768 | tf_op jit(solution)/shard_map/ppermute | solution.py:306
  38.1 9.9 %collective-permute-start.2 = (bf16[160,256]{1,0:T(8,128)(2,1)S(1)}, bf16[160,256]{1,0:T(8,128)(2,1)S(1)}, u32[]{:S(2)}, u32[]{:S(2)}) collective-permute-start(bf16[160,256]{1,0:T(8,128)(2,1)S(1)} %copy-done.17), channel_id=1, source_target_pairs={{96,0},{0,32},{32,64},{64,96},{97,1},{1,33},{33,65},{65,97},{98,2}... | collective-permute-start | bytes 245768 | tf_op jit(solution)/shard_map/ppermute | solution.py:306
  39.1 14.9 %collective-permute-start.11 = (bf16[4,128,256]{2,1,0:T(8,128)(2,1)S(1)}, bf16[4,128,256]{2,1,0:T(8,128)(2,1)S(1)}, u32[]{:S(2)}, u32[]{:S(2)}) collective-permute-start(bf16[4,128,256]{2,1,0:T(8,128)(2,1)S(1)} %pad_maximum_fusion.3.b0), channel_id=1, source_target_pairs={{96,0},{0,32},{32,64},{64,96},{97,1},{1,33},{33,65},{65,97},{98,2}... | collective-permute-start | bytes 786440 | tf_op jit(solution)/shard_map/ppermute | solution.py:306
  48.1 13.3 %collective-permute-start.3 = (bf16[4,160,256]{2,1,0:T(8,128)(2,1)S(1)}, bf16[4,160,256]{2,1,0:T(8,128)(2,1)S(1)}, u32[]{:S(2)}, u32[]{:S(2)}) collective-permute-start(bf16[4,160,256]{2,1,0:T(8,128)(2,1)S(1)} %pad_maximum_fusion.2.a0), channel_id=1, source_target_pairs={{8,0},{16,8},{24,16},{0,24},{9,1},{17,9},{25,17},{1,25},{10,2},{18... | collective-permute-start | bytes 983048 | tf_op jit(solution)/shard_map/ppermute | solution.py:306
  49.2 12.1 %collective-permute-start.4 = (bf16[4,160,256]{2,1,0:T(8,128)(2,1)S(1)}, bf16[4,160,256]{2,1,0:T(8,128)(2,1)S(1)}, u32[]{:S(2)}, u32[]{:S(2)}) collective-permute-start(bf16[4,160,256]{2,1,0:T(8,128)(2,1)S(1)} %pad_maximum_fusion.2.a0), channel_id=1, source_target_pairs={{16,0},{24,8},{0,16},{8,24},{17,1},{25,9},{1,17},{9,25},{18,2},{26... | collective-permute-start | bytes 983048 | tf_op jit(solution)/shard_map/ppermute | solution.py:306
  50.6 16.8 %collective-permute-start.5 = (bf16[4,160,256]{2,1,0:T(8,128)(2,1)S(1)}, bf16[4,160,256]{2,1,0:T(8,128)(2,1)S(1)}, u32[]{:S(2)}, u32[]{:S(2)}) collective-permute-start(bf16[4,160,256]{2,1,0:T(8,128)(2,1)S(1)} %pad_maximum_fusion.2.a0), channel_id=1, source_target_pairs={{24,0},{0,8},{8,16},{16,24},{25,1},{1,9},{9,17},{17,25},{26,2},{2,... | collective-permute-start | bytes 983048 | tf_op jit(solution)/shard_map/ppermute | solution.py:306
  54.0 7.4 %collective-permute-start.9 = (bf16[4,128,256]{2,1,0:T(8,128)(2,1)S(1)}, bf16[4,128,256]{2,1,0:T(8,128)(2,1)S(1)}, u32[]{:S(2)}, u32[]{:S(2)}) collective-permute-start(bf16[4,128,256]{2,1,0:T(8,128)(2,1)S(1)} %pad_maximum_fusion.3.b0), channel_id=1, source_target_pairs={{32,0},{64,32},{96,64},{0,96},{33,1},{65,33},{97,65},{1,97},{34,2}... | collective-permute-start | bytes 786440 | tf_op jit(solution)/shard_map/ppermute | solution.py:306
  89.7 26.6 %collective-permute-start.28 = (f32[4,512,256]{2,1,0:T(8,128)}, f32[4,512,256]{2,1,0:T(8,128)S(1)}, u32[]{:S(2)}, u32[]{:S(2)}) collective-permute-start(f32[4,512,256]{2,1,0:T(8,128)} %get-tuple-element.38), channel_id=1, source_target_pairs={{0,4},{4,0},{1,5},{5,1},{2,6},{6,2},{3,7},{7,3},{8,12},{12,8},{9,1... | collective-permute-start | bytes 6291464 | tf_op jit(solution)/shard_map/ppermute | solution.py:311
  90.3 26.1 %collective-permute-start.22 = (f32[4,128,256]{2,1,0:T(8,128)}, f32[4,128,256]{2,1,0:T(8,128)S(1)}, u32[]{:S(2)}, u32[]{:S(2)}) collective-permute-start(f32[4,128,256]{2,1,0:T(8,128)} %get-tuple-element.34), channel_id=1, source_target_pairs={{0,32},{32,64},{64,96},{96,0},{1,33},{33,65},{65,97},{97,1},{2,34}... | collective-permute-start | bytes 1572872 | tf_op jit(solution)/shard_map/ppermute | solution.py:311
  90.3 31.2 %collective-permute-start.23 = (f32[4,128,256]{2,1,0:T(8,128)}, f32[4,128,256]{2,1,0:T(8,128)S(1)}, u32[]{:S(2)}, u32[]{:S(2)}) collective-permute-start(f32[4,128,256]{2,1,0:T(8,128)} %get-tuple-element.35), channel_id=1, source_target_pairs={{0,64},{32,96},{64,0},{96,32},{1,65},{33,97},{65,1},{97,33},{2,66}... | collective-permute-start | bytes 1572872 | tf_op jit(solution)/shard_map/ppermute | solution.py:311
  91.2 30.3 %collective-permute-start.24 = (f32[4,128,256]{2,1,0:T(8,128)}, f32[4,128,256]{2,1,0:T(8,128)S(1)}, u32[]{:S(2)}, u32[]{:S(2)}) collective-permute-start(f32[4,128,256]{2,1,0:T(8,128)} %get-tuple-element.36), channel_id=1, source_target_pairs={{0,96},{32,0},{64,32},{96,64},{1,97},{33,1},{65,33},{97,65},{2,98}... | collective-permute-start | bytes 1572872 | tf_op jit(solution)/shard_map/ppermute | solution.py:311
  93.0 28.9 %collective-permute-start.16 = (f32[4,128,256]{2,1,0:T(8,128)}, f32[4,128,256]{2,1,0:T(8,128)S(1)}, u32[]{:S(2)}, u32[]{:S(2)}) collective-permute-start(f32[4,128,256]{2,1,0:T(8,128)} %get-tuple-element.30), channel_id=1, source_target_pairs={{0,8},{8,16},{16,24},{24,0},{1,9},{9,17},{17,25},{25,1},{2,10},{10... | collective-permute-start | bytes 1572872 | tf_op jit(solution)/shard_map/ppermute | solution.py:311
  116.3 14.3 %collective-permute-start.17 = (f32[4,128,256]{2,1,0:T(8,128)}, f32[4,128,256]{2,1,0:T(8,128)S(1)}, u32[]{:S(2)}, u32[]{:S(2)}) collective-permute-start(f32[4,128,256]{2,1,0:T(8,128)} %get-tuple-element.31), channel_id=1, source_target_pairs={{0,16},{8,24},{16,0},{24,8},{1,17},{9,25},{17,1},{25,9},{2,18},{10... | collective-permute-start | bytes 1572872 | tf_op jit(solution)/shard_map/ppermute | solution.py:311
  116.4 22.8 %collective-permute-start.18 = (f32[4,128,256]{2,1,0:T(8,128)}, f32[4,128,256]{2,1,0:T(8,128)S(1)}, u32[]{:S(2)}, u32[]{:S(2)}) collective-permute-start(f32[4,128,256]{2,1,0:T(8,128)} %get-tuple-element.32), channel_id=1, source_target_pairs={{0,24},{8,0},{16,8},{24,16},{1,25},{9,1},{17,9},{25,17},{2,26},{10... | collective-permute-start | bytes 1572872 | tf_op jit(solution)/shard_map/ppermute | solution.py:311
  121.4 34.3 %collective-permute-start.29 = (f32[512,256]{1,0:T(8,128)S(1)}, f32[512,256]{1,0:T(8,128)S(1)}, u32[]{:S(2)}, u32[]{:S(2)}) collective-permute-start(f32[512,256]{1,0:T(8,128)S(1)} %get-tuple-element.49), channel_id=1, source_target_pairs={{0,1},{1,2},{2,3},{3,0},{4,5},{5,6},{6,7},{7,4},{8,9},{9,10},{10,1... | collective-permute-start | bytes 1572872 | tf_op jit(solution)/shard_map/ppermute | solution.py:311
  121.5 34.3 %collective-permute-start.30 = (f32[512,256]{1,0:T(8,128)S(1)}, f32[512,256]{1,0:T(8,128)S(1)}, u32[]{:S(2)}, u32[]{:S(2)}) collective-permute-start(f32[512,256]{1,0:T(8,128)S(1)} %get-tuple-element.48), channel_id=1, source_target_pairs={{0,2},{1,3},{2,0},{3,1},{4,6},{5,7},{6,4},{7,5},{8,10},{9,11},{10,... | collective-permute-start | bytes 1572872 | tf_op jit(solution)/shard_map/ppermute | solution.py:311
  121.9 33.9 %collective-permute-start.31 = (f32[512,256]{1,0:T(8,128)S(1)}, f32[512,256]{1,0:T(8,128)S(1)}, u32[]{:S(2)}, u32[]{:S(2)}) collective-permute-start(f32[512,256]{1,0:T(8,128)S(1)} %get-tuple-element.47), channel_id=1, source_target_pairs={{0,3},{1,0},{2,1},{3,2},{4,7},{5,4},{6,5},{7,6},{8,11},{9,8},{10,9... | collective-permute-start | bytes 1572872 | tf_op jit(solution)/shard_map/ppermute | solution.py:311
  130.6 12.7 %collective-permute-start.25 = (f32[128,256]{1,0:T(8,128)S(1)}, f32[128,256]{1,0:T(8,128)S(1)}, u32[]{:S(2)}, u32[]{:S(2)}) collective-permute-start(f32[128,256]{1,0:T(8,128)S(1)} %get-tuple-element.53), channel_id=1, source_target_pairs={{0,8},{8,16},{16,24},{24,0},{1,9},{9,17},{17,25},{25,1},{2,10},{10... | collective-permute-start | bytes 393224 | tf_op jit(solution)/shard_map/ppermute | solution.py:311
  168.0 6.7 %collective-permute-start.37 = (f32[3,32,256]{2,1,0:T(8,128)S(1)}, f32[3,32,256]{2,1,0:T(8,128)S(1)}, u32[]{:S(2)}, u32[]{:S(2)}) collective-permute-start(f32[3,32,256]{2,1,0:T(8,128)S(1)} %get-tuple-element.60), channel_id=1, source_target_pairs={{0,64},{32,96},{64,0},{96,32},{1,65},{33,97},{65,1},{97,33},{2,66}... | collective-permute-start | bytes 294920 | tf_op jit(solution)/shard_map/ppermute | solution.py:311
  175.7 7.6 %collective-permute-start.39 = (f32[3,32,256]{2,1,0:T(8,128)S(1)}, f32[3,32,256]{2,1,0:T(8,128)S(1)}, u32[]{:S(2)}, u32[]{:S(2)}) collective-permute-start(f32[3,32,256]{2,1,0:T(8,128)S(1)} %fusion.20), channel_id=1, source_target_pairs={{16,0},{24,8},{0,16},{8,24},{17,1},{25,9},{1,17},{9,25},{18,2},{26... | collective-permute-start | bytes 294920 | tf_op jit(solution)/shard_map/ppermute | solution.py:306
  202.8 21.8 %collective-permute-start.48 = (f32[4,3,32,256]{3,2,1,0:T(8,128)S(1)}, f32[4,3,32,256]{3,2,1,0:T(8,128)S(1)}, u32[]{:S(2)}, u32[]{:S(2)}) collective-permute-start(f32[4,3,32,256]{3,2,1,0:T(8,128)S(1)} %pad_maximum_fusion.1), channel_id=1, source_target_pairs={{4,0},{0,4},{5,1},{1,5},{6,2},{2,6},{7,3},{3,7},{12,8},{8,12},{13,... | collective-permute-start | bytes 1179656 | tf_op jit(solution)/shard_map/ppermute | solution.py:306
  208.5 7.8 %collective-permute-start.32 = (f32[256,256]{1,0:T(8,128)S(1)}, f32[256,256]{1,0:T(8,128)S(1)}, u32[]{:S(2)}, u32[]{:S(2)}) collective-permute-start(f32[256,256]{1,0:T(8,128)S(1)} %copy-done.21), channel_id=1, source_target_pairs={{1,0},{2,1},{3,2},{0,3},{5,4},{6,5},{7,6},{4,7},{9,8},{10,9},{11,1... | collective-permute-start | bytes 786440 | tf_op jit(solution)/shard_map/ppermute | solution.py:306
  209.3 9.0 %collective-permute-start.33 = (f32[256,256]{1,0:T(8,128)S(1)}, f32[256,256]{1,0:T(8,128)S(1)}, u32[]{:S(2)}, u32[]{:S(2)}) collective-permute-start(f32[256,256]{1,0:T(8,128)S(1)} %copy-done.21), channel_id=1, source_target_pairs={{2,0},{3,1},{0,2},{1,3},{6,4},{7,5},{4,6},{5,7},{10,8},{11,9},{8,1... | collective-permute-start | bytes 786440 | tf_op jit(solution)/shard_map/ppermute | solution.py:306
  209.6 15.0 %collective-permute-start.34 = (f32[256,256]{1,0:T(8,128)S(1)}, f32[256,256]{1,0:T(8,128)S(1)}, u32[]{:S(2)}, u32[]{:S(2)}) collective-permute-start(f32[256,256]{1,0:T(8,128)S(1)} %copy-done.21), channel_id=1, source_target_pairs={{3,0},{0,1},{1,2},{2,3},{7,4},{4,5},{5,6},{6,7},{11,8},{8,9},{9,10... | collective-permute-start | bytes 786440 | tf_op jit(solution)/shard_map/ppermute | solution.py:306
  (49 other events, 465.7 us)
where the time goes:
time: 229 us
  waiting for transfers between devices  119 us (52%)
  starting transfers between devices  65.8 us (29%)
  Pallas kernels  29.6 us (13%)
  other arithmetic  6.74 us (3%)
  local copies, waits for them, and re-layouts  5.04 us (2%)
    ppermute x30, waiting for transfers between devices, fetch(): return lax.ppermute(v, axis, [((i + d) % n, i) for i in range(n)])  70.2 us
    ppermute x19, waiting for transfers between devices, give(): return lax.ppermute(v, axis, [(i, (i + d) % n) for i in range(n)])  49.3 us
    ppermute x30, starting transfers between devices, fetch(): return lax.ppermute(v, axis, [((i + d) % n, i) for i in range(n)])  45.7 us
    pallas_call x1, Pallas kernels, sketch(): pl.pallas_call(sketch_kernel, out_shape=(*[jax.ShapeDtypeStruct((ZN, TH,...  20.5 us
    ppermute x19, starting transfers between devices, give(): return lax.ppermute(v, axis, [(i, (i + d) % n) for i in range(n)])  20.1 us
  transfers between devices with their start and end apart: 49, of which 27 were waited for; matrix products, arithmetic and copies ran while one was open for 2% of the time, Pallas kernels for 0%

commit v1 on v0

--- a/solution.py
+++ b/solution.py
@@ -26,6 +26,10 @@
 FAR = 4.0
 F32 = jnp.float32
 BF16 = jnp.bfloat16
+
+
+def inside(*arrays):
+    return [pltpu.with_memory_space_constraint(v, pltpu.VMEM) for v in arrays]
 
 
 def three_pieces(v):
@@ -87,6 +91,7 @@
         in_specs=[pl.BlockSpec(memory_space=pltpu.SMEM), vm, vm, vm, vm],
         out_specs=(vm, vm, vm),
         scratch_shapes=[pltpu.VMEM((TCAP, 8), F32), pltpu.VMEM((TQ, 8), F32)],
+        compiler_params=pltpu.CompilerParams(vmem_limit_bytes=8 << 20),
     )(where, txyz, sxyz, psi, omega)
 
 
@@ -103,7 +108,7 @@
 
 def sketch_kernel(a0, a1, a2, a3, b0, b1, b2, b3, s0, s1, ya0, ya1, ya2, ya3,
                   yb0, yb1, yb2, yb3, z0, z1, psic, tpos, omc, spos, srow,
-                  bcx, bcy, bcz, yc, zc, cntv, cnts, sem):
+                  bcx, bcy, bcz, yc, zc, tile0, tile1, cntv, cnts, sem):
     ain, bin_, sin = (a0, a1, a2, a3), (b0, b1, b2, b3), (s0, s1)
     yas, ybs, zouts = (ya0, ya1, ya2, ya3), (yb0, yb1, yb2, yb3), (z0, z1)
     for k in range(NT):
@@ -123,8 +128,8 @@
         tpos[pl.ds(off, TQ), :] = join(ain[dx], dz, TH).T
         toff.append(toff[k] + ceil16(cnts[k, 0]))
     tend = pl.multiple_of(toff[NT], GRAN)
-    psic[pl.ds(tend, TC), :] = jnp.zeros((TC, R), BF16)
-    tpos[pl.ds(tend, TC), :] = jnp.zeros((TC, 8), F32)
+    psic[pl.ds(tend, 2 * TC), :] = jnp.zeros((2 * TC, R), BF16)
+    tpos[pl.ds(tend, 2 * TC), :] = jnp.zeros((2 * TC, 8), F32)
     soff = [jnp.int32(0)]
     for k in range(NS):
         ref, d = sin[k // YN], k % YN
@@ -147,37 +152,55 @@
 
     lax.fori_loop(0, ns, prepare, 0)
 
-    def over_targets(ti, carry):
+    def columns(ti, carry):
         ta = pl.multiple_of(ti * TC, TC)
         tp = tpos[pl.ds(ta, TC), :]
-        bcx[...] = jnp.broadcast_to(tp[:, 0:1], (TC, 128))
-        bcy[...] = jnp.broadcast_to(tp[:, 1:2], (TC, 128))
-        bcz[...] = jnp.broadcast_to(tp[:, 2:3], (TC, 128))
+        bcx[ti] = jnp.broadcast_to(tp[:, 0:1], (TC, 128))
+        bcy[ti] = jnp.broadcast_to(tp[:, 1:2], (TC, 128))
+        bcz[ti] = jnp.broadcast_to(tp[:, 2:3], (TC, 128))
         yc[pl.ds(ta, TC), :] = jnp.zeros((TC, R), F32)
-
-        def over_sources(si, inner):
-            sa = pl.multiple_of(si * SC, SC)
-            pieces = []
-            for j in range(SC // 128):
-                lanes = slice(j * 128, (j + 1) * 128)
-                dx = bcx[...] - srow[si, 0:1, lanes]
-                dy = bcy[...] - srow[si, 1:2, lanes]
-                dz = bcz[...] - srow[si, 2:3, lanes]
-                pieces.append(lax.rsqrt(dx * dx + dy * dy + dz * dz).astype(BF16))
-            tile = jnp.concatenate(pieces, axis=1)
-            yc[pl.ds(ta, TC), :] += jnp.dot(
-                tile, omc[pl.ds(sa, SC), :], preferred_element_type=F32
-            )
-            zc[pl.ds(sa, SC), :] += lax.dot_general(
-                tile, psic[pl.ds(ta, TC), :], (((0,), (0,)), ((), ())),
-                preferred_element_type=F32,
-            )
-            return inner
-
-        lax.fori_loop(0, ns, over_sources, 0)
         return carry
 
-    lax.fori_loop(0, nt, over_targets, 0)
+    lax.fori_loop(0, nt + 1, columns, 0)
+
+    def make(at, tile):
+        ti, si = at
+        for j in range(SC // 128):
+            lanes = slice(j * 128, (j + 1) * 128)
+            dx = bcx[ti] - srow[si, 0:1, lanes]
+            dy = bcy[ti] - srow[si, 1:2, lanes]
+            dz = bcz[ti] - srow[si, 2:3, lanes]
+            tile[:, lanes] = lax.rsqrt(dx * dx + dy * dy + dz * dz).astype(BF16)
+
+    def use(at, tile):
+        ta = pl.multiple_of(at[0] * TC, TC)
+        sa = pl.multiple_of(at[1] * SC, SC)
+        block = tile[...]
+        yc[pl.ds(ta, TC), :] += jnp.dot(
+            block, omc[pl.ds(sa, SC), :], preferred_element_type=F32
+        )
+        zc[pl.ds(sa, SC), :] += lax.dot_general(
+            block, psic[pl.ds(ta, TC), :], (((0,), (0,)), ((), ())),
+            preferred_element_type=F32,
+        )
+
+    def after(at):
+        wrap = at[1] + 1 == ns
+        return jnp.where(wrap, at[0] + 1, at[0]), jnp.where(wrap, 0, at[1] + 1)
+
+    start = (jnp.int32(0), jnp.int32(0))
+    make(start, tile0)
+
+    def two_steps(p, first):
+        second = after(first)
+        use(first, tile0)
+        make(second, tile1)
+        third = after(second)
+        use(second, tile1)
+        make(third, tile0)
+        return third
+
+    lax.fori_loop(0, (nt * ns + 1) // 2, two_steps, start)
     for k in range(NT):
         dx, dz = k // ZN, k % ZN
         off = pl.multiple_of(toff[k], GRAN)
@@ -206,16 +229,19 @@
             pltpu.VMEM((srows, R), BF16),
             pltpu.VMEM((srows, 8), F32),
             pltpu.VMEM((srows // SC, 8, SC), F32),
-            pltpu.VMEM((TC, 128), F32),
-            pltpu.VMEM((TC, 128), F32),
-            pltpu.VMEM((TC, 128), F32),
+            pltpu.VMEM((trows // TC, TC, 128), F32),
+            pltpu.VMEM((trows // TC, TC, 128), F32),
+            pltpu.VMEM((trows // TC, TC, 128), F32),
             pltpu.VMEM((trows, R), F32),
             pltpu.VMEM((srows, R), F32),
+            pltpu.VMEM((TC, SC), BF16),
+            pltpu.VMEM((TC, SC), BF16),
             pltpu.VMEM((NT + NS, 128), jnp.int32),
             pltpu.SMEM((NT + NS, 128), jnp.int32),
             pltpu.SemaphoreType.DMA(()),
         ],
-    )(*ain, *bin_, *sin)
+        compiler_params=pltpu.CompilerParams(vmem_limit_bytes=34 << 20),
+    )(*inside(*ain, *bin_, *sin))
 
 
 def finish_kernel(where_ref, a0, a1, a2, a3, b0, b1, b2, b3, z0, z1, z2, z3, pa, pb,
@@ -266,7 +292,8 @@
         ),
         in_specs=[pl.BlockSpec(memory_space=pltpu.SMEM)] + [vm] * 14,
         out_specs=(vm,) * 4,
-    )(where, *a, *b, *z, pa, pb)
+        compiler_params=pltpu.CompilerParams(vmem_limit_bytes=14 << 20),
+    )(where, *inside(*a, *b, *z, pa, pb))
 
 
 def place_kernel(where_ref, *refs):
@@ -298,7 +325,8 @@
         ),
         in_specs=[pl.BlockSpec(memory_space=pltpu.SMEM)] + [vm] * (YN + ZN + 1),
         out_specs=(vm,) * 4,
-    )(where, *ys, *own, other)
+        compiler_params=pltpu.CompilerParams(vmem_limit_bytes=10 << 20),
+    )(where, *inside(*ys, *own, other))
 
 
 def fetch(v, axis, d):

time: 229 us -> 213 us (0.930)
  Pallas kernels: 29.6 us -> 18.9 us
  other arithmetic: 6.74 us -> 1.09 us
  waiting for transfers between devices: 119 us -> 122 us
    pallas_call x1, Pallas kernels: 20.5 us -> 14.1 us  [sketch(): pl.pallas_call(sketch_kernel, out_shape=(*[jax.ShapeDtypeStruct((ZN, TH,...]
    ppermute x19, waiting for transfers between devices: 49.3 us -> 52.1 us  [give(): return lax.ppermute(v, axis, [(i, (i + d) % n) for i in range(n)])]
    add x1, other arithmetic: 2.77 us -> 0.43 us  [steps(): zmine = [z0[d] + zfar[d] for d in range(YN)]]
  transfers between devices with their start and end apart: 49 -> 49, of which waited for: 27 -> 27; matrix products, arithmetic and copies ran while one was open for 2% -> 0% of each run, Pallas kernels for 0% -> 0%
where the time goes in v1:
time: 213 us
  waiting for transfers between devices  122 us (57%)
  starting transfers between devices  65.4 us (31%)
  Pallas kernels  18.9 us (9%)
  local copies, waits for them, and re-layouts  3.52 us (2%)
    ppermute x30, waiting for transfers between devices, fetch(): return lax.ppermute(v, axis, [((i + d) % n, i) for i in range(n)])  69.8 us
    ppermute x19, waiting for transfers between devices, give(): return lax.ppermute(v, axis, [(i, (i + d) % n) for i in range(n)])  52.1 us
    ppermute x30, starting transfers between devices, fetch(): return lax.ppermute(v, axis, [((i + d) % n, i) for i in range(n)])  45.1 us
    ppermute x19, starting transfers between devices, give(): return lax.ppermute(v, axis, [(i, (i + d) % n) for i in range(n)])  20.4 us
    pallas_call x1, Pallas kernels, sketch(): pl.pallas_call(sketch_kernel, out_shape=(*[jax.ShapeDtypeStruct((ZN, TH,...  14.1 us
  transfers between devices with their start and end apart: 49, of which 27 were waited for; matrix products, arithmetic and copies ran while one was open for 0% of the time, Pallas kernels for 0%

profile of v1, /device:TPU:1, one launch (start us, length us, event | category | flops | bytes accessed | tf_op | source)
XLA Modules:
  0.0 212.9 jit_solution(3960434146467113284)
XLA Ops:
  6.3 3.6 %collective-permute-start.12 = (bf16[576,256]{1,0:T(8,128)(2,1)S(1)}, bf16[576,256]{1,0:T(8,128)(2,1)S(1)}, u32[]{:S(2)}, u32[]{:S(2)}) collective-permute-start(bf16[576,256]{1,0:T(8,128)(2,1)S(1)} %get-tuple-element.28), channel_id=1, source_target_pairs={{1,0},{2,1},{3,2},{0,3},{5,4},{6,5},{7,6},{4,7},{9,8},{10,9},{11,1... | collective-permute-start | bytes 884744 | tf_op jit(solution)/shard_map/ppermute | solution.py:334
  10.9 10.8 %collective-permute-done.12 = bf16[576,256]{1,0:T(8,128)(2,1)S(1)} collective-permute-done((bf16[576,256]{1,0:T(8,128)(2,1)S(1)}, bf16[576,256]{1,0:T(8,128)(2,1)S(1)}, u32[]{:S(2)}, u32[]{:S(2)}) %collective-permute-start.12) | collective-permute-done | bytes 294944 | tf_op jit(solution)/shard_map/ppermute | solution.py:334
  21.8 4.9 %collective-permute-done.14 = bf16[576,256]{1,0:T(8,128)(2,1)S(1)} collective-permute-done((bf16[576,256]{1,0:T(8,128)(2,1)S(1)}, bf16[576,256]{1,0:T(8,128)(2,1)S(1)}, u32[]{:S(2)}, u32[]{:S(2)}) %collective-permute-start.14) | collective-permute-done | bytes 294944 | tf_op jit(solution)/shard_map/ppermute | solution.py:334
  31.6 3.8 %collective-permute-start = (bf16[160,256]{1,0:T(8,128)(2,1)S(1)}, bf16[160,256]{1,0:T(8,128)(2,1)S(1)}, u32[]{:S(2)}, u32[]{:S(2)}) collective-permute-start(bf16[160,256]{1,0:T(8,128)(2,1)S(1)} %get-tuple-element.26.refs_13_), channel_id=1, source_target_pairs={{32,0},{64,32},{96,64},{0,96},{33,1},{65,33},{97,65},{1,97},{34,2}... | collective-permute-start | bytes 245768 | tf_op jit(solution)/shard_map/ppermute | solution.py:334
  35.4 3.0 %collective-permute-start.10 = (bf16[4,128,256]{2,1,0:T(8,128)(2,1)S(1)}, bf16[4,128,256]{2,1,0:T(8,128)(2,1)S(1)}, u32[]{:S(2)}, u32[]{:S(2)}) collective-permute-start(bf16[4,128,256]{2,1,0:T(8,128)(2,1)S(1)} %pad_maximum_fusion.3.b0), channel_id=1, source_target_pairs={{64,0},{96,32},{0,64},{32,96},{65,1},{97,33},{1,65},{33,97},{66,2}... | collective-permute-start | bytes 786440 | tf_op jit(solution)/shard_map/ppermute | solution.py:334
  41.0 4.1 %collective-permute-done.1 = bf16[160,256]{1,0:T(8,128)(2,1)S(1)} collective-permute-done((bf16[160,256]{1,0:T(8,128)(2,1)S(1)}, bf16[160,256]{1,0:T(8,128)(2,1)S(1)}, u32[]{:S(2)}, u32[]{:S(2)}) %collective-permute-start.1) | collective-permute-done | bytes 81952 | tf_op jit(solution)/shard_map/ppermute | solution.py:334
  45.2 3.2 %collective-permute-done.2 = bf16[160,256]{1,0:T(8,128)(2,1)S(1)} collective-permute-done((bf16[160,256]{1,0:T(8,128)(2,1)S(1)}, bf16[160,256]{1,0:T(8,128)(2,1)S(1)}, u32[]{:S(2)}, u32[]{:S(2)}) %collective-permute-start.2) | collective-permute-done | bytes 81952 | tf_op jit(solution)/shard_map/ppermute | solution.py:334
  50.9 3.4 %collective-permute-done.11.b3 = bf16[4,128,256]{2,1,0:T(8,128)(2,1)S(1)} collective-permute-done((bf16[4,128,256]{2,1,0:T(8,128)(2,1)S(1)}, bf16[4,128,256]{2,1,0:T(8,128)(2,1)S(1)}, u32[]{:S(2)}, u32[]{:S(2)}) %collective-permute-start.11) | collective-permute-done | bytes 262176 | tf_op jit(solution)/shard_map/ppermute | solution.py:334
  54.3 7.4 %collective-permute-done.9.b1 = bf16[4,128,256]{2,1,0:T(8,128)(2,1)S(1)} collective-permute-done((bf16[4,128,256]{2,1,0:T(8,128)(2,1)S(1)}, bf16[4,128,256]{2,1,0:T(8,128)(2,1)S(1)}, u32[]{:S(2)}, u32[]{:S(2)}) %collective-permute-start.9) | collective-permute-done | bytes 262176 | tf_op jit(solution)/shard_map/ppermute | solution.py:334
  61.7 6.0 %collective-permute-done.5.a3 = bf16[4,160,256]{2,1,0:T(8,128)(2,1)S(1)} collective-permute-done((bf16[4,160,256]{2,1,0:T(8,128)(2,1)S(1)}, bf16[4,160,256]{2,1,0:T(8,128)(2,1)S(1)}, u32[]{:S(2)}, u32[]{:S(2)}) %collective-permute-start.5) | collective-permute-done | bytes 327712 | tf_op jit(solution)/shard_map/ppermute | solution.py:334
  67.7 14.1 %shard_map.102 = (f32[4,128,256]{2,1,0:T(8,128)S(1)}, f32[4,128,256]{2,1,0:T(8,128)S(1)}, f32[4,128,256]{2,1,0:T(8,128)S(1)}, f32[4,128,256]{2,1,0:T(8,128)S(1)}...) custom-call(bf16[4,160,256]{2,1,0:T(8,128)(2,1)S(1)} %pad_maximum_fu, ...), custom_call_target="tpu_custom_call" | custom-call | tf_op jit(solution)/shard_map/pallas_call | solution.py:218
  85.1 23.1 %collective-permute-done.22 = f32[4,128,256]{2,1,0:T(8,128)S(1)} collective-permute-done((f32[4,128,256]{2,1,0:T(8,128)S(1)}, f32[4,128,256]{2,1,0:T(8,128)S(1)}, u32[]{:S(2)}, u32[]{:S(2)}) %collective-permute-start.22) | collective-permute-done | bytes 524320 | tf_op jit(solution)/shard_map/ppermute | solution.py:339
  108.2 2.3 %collective-permute-start.18 = (f32[4,128,256]{2,1,0:T(8,128)S(1)}, f32[4,128,256]{2,1,0:T(8,128)S(1)}, u32[]{:S(2)}, u32[]{:S(2)}) collective-permute-start(f32[4,128,256]{2,1,0:T(8,128)S(1)} %get-tuple-element.32), channel_id=1, source_target_pairs={{0,24},{8,0},{16,8},{24,16},{1,25},{9,1},{17,9},{25,17},{2,26},{10... | collective-permute-start | bytes 1572872 | tf_op jit(solution)/shard_map/ppermute | solution.py:339
  111.7 2.1 collective-permute-start.31
  113.9 8.3 %collective-permute-done.17 = f32[4,128,256]{2,1,0:T(8,128)S(1)} collective-permute-done((f32[4,128,256]{2,1,0:T(8,128)S(1)}, f32[4,128,256]{2,1,0:T(8,128)S(1)}, u32[]{:S(2)}, u32[]{:S(2)}) %collective-permute-start.17) | collective-permute-done | bytes 524320 | tf_op jit(solution)/shard_map/ppermute | solution.py:339
  122.3 8.5 %collective-permute-done.18 = f32[4,128,256]{2,1,0:T(8,128)S(1)} collective-permute-done((f32[4,128,256]{2,1,0:T(8,128)S(1)}, f32[4,128,256]{2,1,0:T(8,128)S(1)}, u32[]{:S(2)}, u32[]{:S(2)}) %collective-permute-start.18) | collective-permute-done | bytes 524320 | tf_op jit(solution)/shard_map/ppermute | solution.py:339
  130.8 3.3 %collective-permute-start.26 = (f32[128,256]{1,0:T(8,128)S(1)}, f32[128,256]{1,0:T(8,128)S(1)}, u32[]{:S(2)}, u32[]{:S(2)}) collective-permute-start(f32[128,256]{1,0:T(8,128)S(1)} %get-tuple-element.52), channel_id=1, source_target_pairs={{0,16},{8,24},{16,0},{24,8},{1,17},{9,25},{17,1},{25,9},{2,18},{10... | collective-permute-start | bytes 393224 | tf_op jit(solution)/shard_map/ppermute | solution.py:339
  134.3 2.6 %collective-permute-start.27 = (f32[128,256]{1,0:T(8,128)S(1)}, f32[128,256]{1,0:T(8,128)S(1)}, u32[]{:S(2)}, u32[]{:S(2)}) collective-permute-start(f32[128,256]{1,0:T(8,128)S(1)} %get-tuple-element.51), channel_id=1, source_target_pairs={{0,24},{8,0},{16,8},{24,16},{1,25},{9,1},{17,9},{25,17},{2,26},{10... | collective-permute-start | bytes 393224 | tf_op jit(solution)/shard_map/ppermute | solution.py:339
  136.9 3.7 %collective-permute-done.27.refs_8_ = f32[128,256]{1,0:T(8,128)S(1)} collective-permute-done((f32[128,256]{1,0:T(8,128)S(1)}, f32[128,256]{1,0:T(8,128)S(1)}, u32[]{:S(2)}, u32[]{:S(2)}) %collective-permute-start.27) | collective-permute-done | bytes 131104 | tf_op jit(solution)/shard_map/ppermute | solution.py:339
  140.6 2.6 %collective-permute-start.20 = (f32[128,256]{1,0:T(8,128)S(1)}, f32[128,256]{1,0:T(8,128)S(1)}, u32[]{:S(2)}, u32[]{:S(2)}) collective-permute-start(f32[128,256]{1,0:T(8,128)S(1)} %get-tuple-element.56), channel_id=1, source_target_pairs={{0,64},{32,96},{64,0},{96,32},{1,65},{33,97},{65,1},{97,33},{2,66}... | collective-permute-start | bytes 393224 | tf_op jit(solution)/shard_map/ppermute | solution.py:339
  143.3 2.7 %collective-permute-done.20.refs_3_ = f32[128,256]{1,0:T(8,128)S(1)} collective-permute-done((f32[128,256]{1,0:T(8,128)S(1)}, f32[128,256]{1,0:T(8,128)S(1)}, u32[]{:S(2)}, u32[]{:S(2)}) %collective-permute-start.20) | collective-permute-done | bytes 131104 | tf_op jit(solution)/shard_map/ppermute | solution.py:339
  149.4 2.9 %collective-permute-start.35 = (f32[3,128,256]{2,1,0:T(8,128)S(1)}, f32[3,128,256]{2,1,0:T(8,128)S(1)}, u32[]{:S(2)}, u32[]{:S(2)}) collective-permute-start(f32[3,128,256]{2,1,0:T(8,128)S(1)} %get-tuple-element.41), channel_id=1, source_target_pairs={{4,0},{0,4},{5,1},{1,5},{6,2},{2,6},{7,3},{3,7},{12,8},{8,12},{13,... | collective-permute-start | bytes 1179656 | tf_op jit(solution)/shard_map/ppermute | solution.py:334
  157.1 2.3 %collective-permute-done.36 = f32[3,32,256]{2,1,0:T(8,128)S(1)} collective-permute-done((f32[3,32,256]{2,1,0:T(8,128)S(1)}, f32[3,32,256]{2,1,0:T(8,128)S(1)}, u32[]{:S(2)}, u32[]{:S(2)}) %collective-permute-start.36) | collective-permute-done | bytes 98336 | tf_op jit(solution)/shard_map/ppermute | solution.py:339
  161.5 4.8 %collective-permute-start.39 = (f32[3,32,256]{2,1,0:T(8,128)S(1)}, f32[3,32,256]{2,1,0:T(8,128)S(1)}, u32[]{:S(2)}, u32[]{:S(2)}) collective-permute-start(f32[3,32,256]{2,1,0:T(8,128)S(1)} %fusion.20), channel_id=1, source_target_pairs={{16,0},{24,8},{0,16},{8,24},{17,1},{25,9},{1,17},{9,25},{18,2},{26... | collective-permute-start | bytes 294920 | tf_op jit(solution)/shard_map/ppermute | solution.py:334
  166.3 3.5 %collective-permute-start.40 = (f32[3,32,256]{2,1,0:T(8,128)S(1)}, f32[3,32,256]{2,1,0:T(8,128)S(1)}, u32[]{:S(2)}, u32[]{:S(2)}) collective-permute-start(f32[3,32,256]{2,1,0:T(8,128)S(1)} %fusion.20), channel_id=1, source_target_pairs={{8,0},{16,8},{24,16},{0,24},{9,1},{17,9},{25,17},{1,25},{10,2},{18... | collective-permute-start | bytes 294920 | tf_op jit(solution)/shard_map/ppermute | solution.py:334
  169.7 2.6 %collective-permute-done.40 = f32[3,32,256]{2,1,0:T(8,128)S(1)} collective-permute-done((f32[3,32,256]{2,1,0:T(8,128)S(1)}, f32[3,32,256]{2,1,0:T(8,128)S(1)}, u32[]{:S(2)}, u32[]{:S(2)}) %collective-permute-start.40) | collective-permute-done | bytes 98336 | tf_op jit(solution)/shard_map/ppermute | solution.py:334
  176.3 3.2 %collective-permute-done.42 = f32[3,32,256]{2,1,0:T(8,128)S(1)} collective-permute-done((f32[3,32,256]{2,1,0:T(8,128)S(1)}, f32[3,32,256]{2,1,0:T(8,128)S(1)}, u32[]{:S(2)}, u32[]{:S(2)}) %collective-permute-start.42) | collective-permute-done | bytes 98336 | tf_op jit(solution)/shard_map/ppermute | solution.py:334
  180.6 2.8 %collective-permute-start.45 = (f32[3,32,256]{2,1,0:T(8,128)S(1)}, f32[3,32,256]{2,1,0:T(8,128)S(1)}, u32[]{:S(2)}, u32[]{:S(2)}) collective-permute-start(f32[3,32,256]{2,1,0:T(8,128)S(1)} %add_add_fusion.refs_4_), channel_id=1, source_target_pairs={{32,0},{64,32},{96,64},{0,96},{33,1},{65,33},{97,65},{1,97},{34,2}... | collective-permute-start | bytes 294920 | tf_op jit(solution)/shard_map/ppermute | solution.py:334
  186.0 2.5 %collective-permute-done.46.refs_6_ = f32[3,32,256]{2,1,0:T(8,128)S(1)} collective-permute-done((f32[3,32,256]{2,1,0:T(8,128)S(1)}, f32[3,32,256]{2,1,0:T(8,128)S(1)}, u32[]{:S(2)}, u32[]{:S(2)}) %collective-permute-start.46) | collective-permute-done | bytes 98336 | tf_op jit(solution)/shard_map/ppermute | solution.py:334
  189.1 5.7 %collective-permute-start.48 = (f32[4,3,32,256]{3,2,1,0:T(8,128)S(1)}, f32[4,3,32,256]{3,2,1,0:T(8,128)S(1)}, u32[]{:S(2)}, u32[]{:S(2)}) collective-permute-start(f32[4,3,32,256]{3,2,1,0:T(8,128)S(1)} %pad_maximum_fusion.1), channel_id=1, source_target_pairs={{4,0},{0,4},{5,1},{1,5},{6,2},{2,6},{7,3},{3,7},{12,8},{8,12},{13,... | collective-permute-start | bytes 1179656 | tf_op jit(solution)/shard_map/ppermute | solution.py:334
  196.3 6.3 %collective-permute-done.32.refs_1_ = f32[256,256]{1,0:T(8,128)S(1)} collective-permute-done((f32[256,256]{1,0:T(8,128)S(1)}, f32[256,256]{1,0:T(8,128)S(1)}, u32[]{:S(2)}, u32[]{:S(2)}) %collective-permute-start.32) | collective-permute-done | bytes 262176 | tf_op jit(solution)/shard_map/ppermute | solution.py:334
  204.7 6.3 %collective-permute-done.34.refs_3_ = f32[256,256]{1,0:T(8,128)S(1)} collective-permute-done((f32[256,256]{1,0:T(8,128)S(1)}, f32[256,256]{1,0:T(8,128)S(1)}, u32[]{:S(2)}, u32[]{:S(2)}) %collective-permute-start.34) | collective-permute-done | bytes 262176 | tf_op jit(solution)/shard_map/ppermute | solution.py:334
  (91 shorter events, 44.3 us)
Async XLA Ops:
  6.3 15.5 %collective-permute-start.12 = (bf16[576,256]{1,0:T(8,128)(2,1)S(1)}, bf16[576,256]{1,0:T(8,128)(2,1)S(1)}, u32[]{:S(2)}, u32[]{:S(2)}) collective-permute-start(bf16[576,256]{1,0:T(8,128)(2,1)S(1)} %get-tuple-element.28), channel_id=1, source_target_pairs={{1,0},{2,1},{3,2},{0,3},{5,4},{6,5},{7,6},{4,7},{9,8},{10,9},{11,1... | collective-permute-start | bytes 884744 | tf_op jit(solution)/shard_map/ppermute | solution.py:334
  9.9 11.9 %collective-permute-start.13 = (bf16[576,256]{1,0:T(8,128)(2,1)S(1)}, bf16[576,256]{1,0:T(8,128)(2,1)S(1)}, u32[]{:S(2)}, u32[]{:S(2)}) collective-permute-start(bf16[576,256]{1,0:T(8,128)(2,1)S(1)} %get-tuple-element.28), channel_id=1, source_target_pairs={{2,0},{3,1},{0,2},{1,3},{6,4},{7,5},{4,6},{5,7},{10,8},{11,9},{8,1... | collective-permute-start | bytes 884744 | tf_op jit(solution)/shard_map/ppermute | solution.py:334
  10.2 16.4 %collective-permute-start.14 = (bf16[576,256]{1,0:T(8,128)(2,1)S(1)}, bf16[576,256]{1,0:T(8,128)(2,1)S(1)}, u32[]{:S(2)}, u32[]{:S(2)}) collective-permute-start(bf16[576,256]{1,0:T(8,128)(2,1)S(1)} %get-tuple-element.28), channel_id=1, source_target_pairs={{3,0},{0,1},{1,2},{2,3},{7,4},{4,5},{5,6},{6,7},{11,8},{8,9},{9,10... | collective-permute-start | bytes 884744 | tf_op jit(solution)/shard_map/ppermute | solution.py:334
  26.8 40.9 %collective-permute-start.15 = (bf16[4,576,256]{2,1,0:T(8,128)(2,1)S(1)}, bf16[4,576,256]{2,1,0:T(8,128)(2,1)S(1)}, u32[]{:S(2)}, u32[]{:S(2)}) collective-permute-start(bf16[4,576,256]{2,1,0:T(8,128)(2,1)S(1)} %pad_maximum_fusion.s0), channel_id=1, source_target_pairs={{4,0},{0,4},{5,1},{1,5},{6,2},{2,6},{7,3},{3,7},{12,8},{8,12},{13,... | collective-permute-start | bytes 3538952 | tf_op jit(solution)/shard_map/ppermute | solution.py:334
  27.4 8.0 %collective-permute-start.8 = (bf16[128,256]{1,0:T(8,128)(2,1)S(1)}, bf16[128,256]{1,0:T(8,128)(2,1)S(1)}, u32[]{:S(2)}, u32[]{:S(2)}) collective-permute-start(bf16[128,256]{1,0:T(8,128)(2,1)S(1)} %get-tuple-element.27.refs_14_), channel_id=1, source_target_pairs={{24,0},{0,8},{8,16},{16,24},{25,1},{1,9},{9,17},{17,25},{26,2},{2,... | collective-permute-start | bytes 196616 | tf_op jit(solution)/shard_map/ppermute | solution.py:334
  28.6 6.8 %collective-permute-start.6 = (bf16[128,256]{1,0:T(8,128)(2,1)S(1)}, bf16[128,256]{1,0:T(8,128)(2,1)S(1)}, u32[]{:S(2)}, u32[]{:S(2)}) collective-permute-start(bf16[128,256]{1,0:T(8,128)(2,1)S(1)} %get-tuple-element.27.refs_14_), channel_id=1, source_target_pairs={{8,0},{16,8},{24,16},{0,24},{9,1},{17,9},{25,17},{1,25},{10,2},{18... | collective-permute-start | bytes 196616 | tf_op jit(solution)/shard_map/ppermute | solution.py:334
  31.6 7.8 %collective-permute-start = (bf16[160,256]{1,0:T(8,128)(2,1)S(1)}, bf16[160,256]{1,0:T(8,128)(2,1)S(1)}, u32[]{:S(2)}, u32[]{:S(2)}) collective-permute-start(bf16[160,256]{1,0:T(8,128)(2,1)S(1)} %get-tuple-element.26.refs_13_), channel_id=1, source_target_pairs={{32,0},{64,32},{96,64},{0,96},{33,1},{65,33},{97,65},{1,97},{34,2}... | collective-permute-start | bytes 245768 | tf_op jit(solution)/shard_map/ppermute | solution.py:334
  35.4 15.6 %collective-permute-start.10 = (bf16[4,128,256]{2,1,0:T(8,128)(2,1)S(1)}, bf16[4,128,256]{2,1,0:T(8,128)(2,1)S(1)}, u32[]{:S(2)}, u32[]{:S(2)}) collective-permute-start(bf16[4,128,256]{2,1,0:T(8,128)(2,1)S(1)} %pad_maximum_fusion.3.b0), channel_id=1, source_target_pairs={{64,0},{96,32},{0,64},{32,96},{65,1},{97,33},{1,65},{33,97},{66,2}... | collective-permute-start | bytes 786440 | tf_op jit(solution)/shard_map/ppermute | solution.py:334
  38.4 6.8 %collective-permute-start.1 = (bf16[160,256]{1,0:T(8,128)(2,1)S(1)}, bf16[160,256]{1,0:T(8,128)(2,1)S(1)}, u32[]{:S(2)}, u32[]{:S(2)}) collective-permute-start(bf16[160,256]{1,0:T(8,128)(2,1)S(1)} %get-tuple-element.26.refs_13_), channel_id=1, source_target_pairs={{64,0},{96,32},{0,64},{32,96},{65,1},{97,33},{1,65},{33,97},{66,2}... | collective-permute-start | bytes 245768 | tf_op jit(solution)/shard_map/ppermute | solution.py:334
  38.5 9.9 %collective-permute-start.2 = (bf16[160,256]{1,0:T(8,128)(2,1)S(1)}, bf16[160,256]{1,0:T(8,128)(2,1)S(1)}, u32[]{:S(2)}, u32[]{:S(2)}) collective-permute-start(bf16[160,256]{1,0:T(8,128)(2,1)S(1)} %get-tuple-element.26.refs_13_), channel_id=1, source_target_pairs={{96,0},{0,32},{32,64},{64,96},{97,1},{1,33},{33,65},{65,97},{98,2}... | collective-permute-start | bytes 245768 | tf_op jit(solution)/shard_map/ppermute | solution.py:334
  39.4 14.9 %collective-permute-start.11 = (bf16[4,128,256]{2,1,0:T(8,128)(2,1)S(1)}, bf16[4,128,256]{2,1,0:T(8,128)(2,1)S(1)}, u32[]{:S(2)}, u32[]{:S(2)}) collective-permute-start(bf16[4,128,256]{2,1,0:T(8,128)(2,1)S(1)} %pad_maximum_fusion.3.b0), channel_id=1, source_target_pairs={{96,0},{0,32},{32,64},{64,96},{97,1},{1,33},{33,65},{65,97},{98,2}... | collective-permute-start | bytes 786440 | tf_op jit(solution)/shard_map/ppermute | solution.py:334
  48.5 13.3 %collective-permute-start.3 = (bf16[4,160,256]{2,1,0:T(8,128)(2,1)S(1)}, bf16[4,160,256]{2,1,0:T(8,128)(2,1)S(1)}, u32[]{:S(2)}, u32[]{:S(2)}) collective-permute-start(bf16[4,160,256]{2,1,0:T(8,128)(2,1)S(1)} %pad_maximum_fusion.2.a0), channel_id=1, source_target_pairs={{8,0},{16,8},{24,16},{0,24},{9,1},{17,9},{25,17},{1,25},{10,2},{18... | collective-permute-start | bytes 983048 | tf_op jit(solution)/shard_map/ppermute | solution.py:334
  49.6 12.1 %collective-permute-start.4 = (bf16[4,160,256]{2,1,0:T(8,128)(2,1)S(1)}, bf16[4,160,256]{2,1,0:T(8,128)(2,1)S(1)}, u32[]{:S(2)}, u32[]{:S(2)}) collective-permute-start(bf16[4,160,256]{2,1,0:T(8,128)(2,1)S(1)} %pad_maximum_fusion.2.a0), channel_id=1, source_target_pairs={{16,0},{24,8},{0,16},{8,24},{17,1},{25,9},{1,17},{9,25},{18,2},{26... | collective-permute-start | bytes 983048 | tf_op jit(solution)/shard_map/ppermute | solution.py:334
  50.9 16.8 %collective-permute-start.5 = (bf16[4,160,256]{2,1,0:T(8,128)(2,1)S(1)}, bf16[4,160,256]{2,1,0:T(8,128)(2,1)S(1)}, u32[]{:S(2)}, u32[]{:S(2)}) collective-permute-start(bf16[4,160,256]{2,1,0:T(8,128)(2,1)S(1)} %pad_maximum_fusion.2.a0), channel_id=1, source_target_pairs={{24,0},{0,8},{8,16},{16,24},{25,1},{1,9},{9,17},{17,25},{26,2},{2,... | collective-permute-start | bytes 983048 | tf_op jit(solution)/shard_map/ppermute | solution.py:334
  54.3 7.4 %collective-permute-start.9 = (bf16[4,128,256]{2,1,0:T(8,128)(2,1)S(1)}, bf16[4,128,256]{2,1,0:T(8,128)(2,1)S(1)}, u32[]{:S(2)}, u32[]{:S(2)}) collective-permute-start(bf16[4,128,256]{2,1,0:T(8,128)(2,1)S(1)} %pad_maximum_fusion.3.b0), channel_id=1, source_target_pairs={{32,0},{64,32},{96,64},{0,96},{33,1},{65,33},{97,65},{1,97},{34,2}... | collective-permute-start | bytes 786440 | tf_op jit(solution)/shard_map/ppermute | solution.py:334
  81.8 26.4 %collective-permute-start.28 = (f32[4,512,256]{2,1,0:T(8,128)S(1)}, f32[4,512,256]{2,1,0:T(8,128)S(1)}, u32[]{:S(2)}, u32[]{:S(2)}) collective-permute-start(f32[4,512,256]{2,1,0:T(8,128)S(1)} %get-tuple-element.38), channel_id=1, source_target_pairs={{0,4},{4,0},{1,5},{5,1},{2,6},{6,2},{3,7},{7,3},{8,12},{12,8},{9,1... | collective-permute-start | bytes 6291464 | tf_op jit(solution)/shard_map/ppermute | solution.py:339
  82.4 25.8 %collective-permute-start.22 = (f32[4,128,256]{2,1,0:T(8,128)S(1)}, f32[4,128,256]{2,1,0:T(8,128)S(1)}, u32[]{:S(2)}, u32[]{:S(2)}) collective-permute-start(f32[4,128,256]{2,1,0:T(8,128)S(1)} %get-tuple-element.34), channel_id=1, source_target_pairs={{0,32},{32,64},{64,96},{96,0},{1,33},{33,65},{65,97},{97,1},{2,34}... | collective-permute-start | bytes 1572872 | tf_op jit(solution)/shard_map/ppermute | solution.py:339
  82.4 28.6 %collective-permute-start.23 = (f32[4,128,256]{2,1,0:T(8,128)S(1)}, f32[4,128,256]{2,1,0:T(8,128)S(1)}, u32[]{:S(2)}, u32[]{:S(2)}) collective-permute-start(f32[4,128,256]{2,1,0:T(8,128)S(1)} %get-tuple-element.35), channel_id=1, source_target_pairs={{0,64},{32,96},{64,0},{96,32},{1,65},{33,97},{65,1},{97,33},{2,66}... | collective-permute-start | bytes 1572872 | tf_op jit(solution)/shard_map/ppermute | solution.py:339
  83.2 27.8 %collective-permute-start.24 = (f32[4,128,256]{2,1,0:T(8,128)S(1)}, f32[4,128,256]{2,1,0:T(8,128)S(1)}, u32[]{:S(2)}, u32[]{:S(2)}) collective-permute-start(f32[4,128,256]{2,1,0:T(8,128)S(1)} %get-tuple-element.36), channel_id=1, source_target_pairs={{0,96},{32,0},{64,32},{96,64},{1,97},{33,1},{65,33},{97,65},{2,98}... | collective-permute-start | bytes 1572872 | tf_op jit(solution)/shard_map/ppermute | solution.py:339
  85.1 26.5 %collective-permute-start.16 = (f32[4,128,256]{2,1,0:T(8,128)S(1)}, f32[4,128,256]{2,1,0:T(8,128)S(1)}, u32[]{:S(2)}, u32[]{:S(2)}) collective-permute-start(f32[4,128,256]{2,1,0:T(8,128)S(1)} %get-tuple-element.30), channel_id=1, source_target_pairs={{0,8},{8,16},{16,24},{24,0},{1,9},{9,17},{17,25},{25,1},{2,10},{10... | collective-permute-start | bytes 1572872 | tf_op jit(solution)/shard_map/ppermute | solution.py:339
  108.2 14.0 %collective-permute-start.17 = (f32[4,128,256]{2,1,0:T(8,128)S(1)}, f32[4,128,256]{2,1,0:T(8,128)S(1)}, u32[]{:S(2)}, u32[]{:S(2)}) collective-permute-start(f32[4,128,256]{2,1,0:T(8,128)S(1)} %get-tuple-element.31), channel_id=1, source_target_pairs={{0,16},{8,24},{16,0},{24,8},{1,17},{9,25},{17,1},{25,9},{2,18},{10... | collective-permute-start | bytes 1572872 | tf_op jit(solution)/shard_map/ppermute | solution.py:339
  108.2 22.5 %collective-permute-start.18 = (f32[4,128,256]{2,1,0:T(8,128)S(1)}, f32[4,128,256]{2,1,0:T(8,128)S(1)}, u32[]{:S(2)}, u32[]{:S(2)}) collective-permute-start(f32[4,128,256]{2,1,0:T(8,128)S(1)} %get-tuple-element.32), channel_id=1, source_target_pairs={{0,24},{8,0},{16,8},{24,16},{1,25},{9,1},{17,9},{25,17},{2,26},{10... | collective-permute-start | bytes 1572872 | tf_op jit(solution)/shard_map/ppermute | solution.py:339
  111.0 36.4 %collective-permute-start.29 = (f32[512,256]{1,0:T(8,128)S(1)}, f32[512,256]{1,0:T(8,128)S(1)}, u32[]{:S(2)}, u32[]{:S(2)}) collective-permute-start(f32[512,256]{1,0:T(8,128)S(1)} %get-tuple-element.49), channel_id=1, source_target_pairs={{0,1},{1,2},{2,3},{3,0},{4,5},{5,6},{6,7},{7,4},{8,9},{9,10},{10,1... | collective-permute-start | bytes 1572872 | tf_op jit(solution)/shard_map/ppermute | solution.py:339
  111.1 36.3 %collective-permute-start.30 = (f32[512,256]{1,0:T(8,128)S(1)}, f32[512,256]{1,0:T(8,128)S(1)}, u32[]{:S(2)}, u32[]{:S(2)}) collective-permute-start(f32[512,256]{1,0:T(8,128)S(1)} %get-tuple-element.48), channel_id=1, source_target_pairs={{0,2},{1,3},{2,0},{3,1},{4,6},{5,7},{6,4},{7,5},{8,10},{9,11},{10,... | collective-permute-start | bytes 1572872 | tf_op jit(solution)/shard_map/ppermute | solution.py:339
  111.7 35.7 %collective-permute-start.31 = (f32[512,256]{1,0:T(8,128)S(1)}, f32[512,256]{1,0:T(8,128)S(1)}, u32[]{:S(2)}, u32[]{:S(2)}) collective-permute-start(f32[512,256]{1,0:T(8,128)S(1)} %get-tuple-element.47), channel_id=1, source_target_pairs={{0,3},{1,0},{2,1},{3,2},{4,7},{5,4},{6,5},{7,6},{8,11},{9,8},{10,9... | collective-permute-start | bytes 1572872 | tf_op jit(solution)/shard_map/ppermute | solution.py:339
  122.3 12.0 %collective-permute-start.25 = (f32[128,256]{1,0:T(8,128)S(1)}, f32[128,256]{1,0:T(8,128)S(1)}, u32[]{:S(2)}, u32[]{:S(2)}) collective-permute-start(f32[128,256]{1,0:T(8,128)S(1)} %get-tuple-element.53), channel_id=1, source_target_pairs={{0,8},{8,16},{16,24},{24,0},{1,9},{9,17},{17,25},{25,1},{2,10},{10... | collective-permute-start | bytes 393224 | tf_op jit(solution)/shard_map/ppermute | solution.py:339
  154.1 6.6 %collective-permute-start.37 = (f32[3,32,256]{2,1,0:T(8,128)S(1)}, f32[3,32,256]{2,1,0:T(8,128)S(1)}, u32[]{:S(2)}, u32[]{:S(2)}) collective-permute-start(f32[3,32,256]{2,1,0:T(8,128)S(1)} %get-tuple-element.60), channel_id=1, source_target_pairs={{0,64},{32,96},{64,0},{96,32},{1,65},{33,97},{65,1},{97,33},{2,66}... | collective-permute-start | bytes 294920 | tf_op jit(solution)/shard_map/ppermute | solution.py:339
  161.5 8.3 %collective-permute-start.39 = (f32[3,32,256]{2,1,0:T(8,128)S(1)}, f32[3,32,256]{2,1,0:T(8,128)S(1)}, u32[]{:S(2)}, u32[]{:S(2)}) collective-permute-start(f32[3,32,256]{2,1,0:T(8,128)S(1)} %fusion.20), channel_id=1, source_target_pairs={{16,0},{24,8},{0,16},{8,24},{17,1},{25,9},{1,17},{9,25},{18,2},{26... | collective-permute-start | bytes 294920 | tf_op jit(solution)/shard_map/ppermute | solution.py:334
  189.1 21.8 %collective-permute-start.48 = (f32[4,3,32,256]{3,2,1,0:T(8,128)S(1)}, f32[4,3,32,256]{3,2,1,0:T(8,128)S(1)}, u32[]{:S(2)}, u32[]{:S(2)}) collective-permute-start(f32[4,3,32,256]{3,2,1,0:T(8,128)S(1)} %pad_maximum_fusion.1), channel_id=1, source_target_pairs={{4,0},{0,4},{5,1},{1,5},{6,2},{2,6},{7,3},{3,7},{12,8},{8,12},{13,... | collective-permute-start | bytes 1179656 | tf_op jit(solution)/shard_map/ppermute | solution.py:334
  194.9 7.8 %collective-permute-start.32 = (f32[256,256]{1,0:T(8,128)S(1)}, f32[256,256]{1,0:T(8,128)S(1)}, u32[]{:S(2)}, u32[]{:S(2)}) collective-permute-start(f32[256,256]{1,0:T(8,128)S(1)} %get-tuple-element.39.refs_0_), channel_id=1, source_target_pairs={{1,0},{2,1},{3,2},{0,3},{5,4},{6,5},{7,6},{4,7},{9,8},{10,9},{11,1... | collective-permute-start | bytes 786440 | tf_op jit(solution)/shard_map/ppermute | solution.py:334
  195.6 9.1 %collective-permute-start.33 = (f32[256,256]{1,0:T(8,128)S(1)}, f32[256,256]{1,0:T(8,128)S(1)}, u32[]{:S(2)}, u32[]{:S(2)}) collective-permute-start(f32[256,256]{1,0:T(8,128)S(1)} %get-tuple-element.39.refs_0_), channel_id=1, source_target_pairs={{2,0},{3,1},{0,2},{1,3},{6,4},{7,5},{4,6},{5,7},{10,8},{11,9},{8,1... | collective-permute-start | bytes 786440 | tf_op jit(solution)/shard_map/ppermute | solution.py:334
  196.0 15.0 %collective-permute-start.34 = (f32[256,256]{1,0:T(8,128)S(1)}, f32[256,256]{1,0:T(8,128)S(1)}, u32[]{:S(2)}, u32[]{:S(2)}) collective-permute-start(f32[256,256]{1,0:T(8,128)S(1)} %get-tuple-element.39.refs_0_), channel_id=1, source_target_pairs={{3,0},{0,1},{1,2},{2,3},{7,4},{4,5},{5,6},{6,7},{11,8},{8,9},{9,10... | collective-permute-start | bytes 786440 | tf_op jit(solution)/shard_map/ppermute | solution.py:334
  (21 other events, 93.7 us)

commit v2 on v1

--- a/solution.py
+++ b/solution.py
@@ -20,8 +20,7 @@
 NS = CN * YN
 TC = 256
 SC = 512
-TH = TQ // 2
-TPAY = TH + 32
+TPAY = TQ + 32
 SPAY = SCAP + 64
 FAR = 4.0
 F32 = jnp.float32
@@ -40,7 +39,7 @@
     return hi, mid, low
 
 
-def pack_kernel(where_ref, txyz_ref, sxyz_ref, psi_ref, omega_ref, apay_ref, bpay_ref, spay_ref, cols, quarter):
+def pack_kernel(where_ref, txyz_ref, sxyz_ref, psi_ref, omega_ref, tpay_ref, spay_ref, cols, quarter):
     yq = where_ref[0]
     tcount = where_ref[1]
     scount = where_ref[2]
@@ -51,9 +50,7 @@
     for a in range(TQ // GRAN):
         start = pl.multiple_of((a * YN + yq) * GRAN, GRAN)
         block = psi_ref[pl.ds(start, GRAN), :]
-        half = (apay_ref, bpay_ref)[a * GRAN // TH]
-        at = a * GRAN % TH
-        half[at:at + GRAN, :] = jnp.where(
+        tpay_ref[a * GRAN:(a + 1) * GRAN, :] = jnp.where(
             rows16 + start < tcount, block, jnp.zeros_like(block)
         )
         quarter[a * GRAN:(a + 1) * GRAN, :] = cols[pl.ds(start, GRAN), :]
@@ -64,7 +61,7 @@
     tpos = jnp.where((sub == 1) | (sub == 2), tpos * SPREAD, tpos)
     tpos = jnp.where(sub == 3, tlive.astype(F32), tpos)
     tail = jnp.zeros((8, R), BF16)
-    apay_ref[TH:TPAY, :] = jnp.concatenate([*three_pieces(tpos), tail], axis=0)
+    tpay_ref[TQ:TPAY, :] = jnp.concatenate([*three_pieces(tpos), tail], axis=0)
     srow = lax.broadcasted_iota(jnp.int32, (SCAP, R), 0)
     om = omega_ref[...]
     spay_ref[0:SCAP, :] = jnp.where(srow < scount, om, jnp.zeros_like(om))
@@ -85,13 +82,11 @@
         pack_kernel,
         out_shape=(
             jax.ShapeDtypeStruct((TPAY, R), BF16),
-            jax.ShapeDtypeStruct((TH, R), BF16),
             jax.ShapeDtypeStruct((SPAY, R), BF16),
         ),
         in_specs=[pl.BlockSpec(memory_space=pltpu.SMEM), vm, vm, vm, vm],
-        out_specs=(vm, vm, vm),
+        out_specs=(vm, vm),
         scratch_shapes=[pltpu.VMEM((TCAP, 8), F32), pltpu.VMEM((TQ, 8), F32)],
-        compiler_params=pltpu.CompilerParams(vmem_limit_bytes=8 << 20),
     )(where, txyz, sxyz, psi, omega)
 
 
@@ -106,13 +101,12 @@
     return ((n + GRAN - 1) // GRAN) * GRAN
 
 
-def sketch_kernel(a0, a1, a2, a3, b0, b1, b2, b3, s0, s1, ya0, ya1, ya2, ya3,
-                  yb0, yb1, yb2, yb3, z0, z1, psic, tpos, omc, spos, srow,
+def sketch_kernel(t0, t1, t2, t3, s0, s1, y0, y1, y2, y3, z0, z1, psic, tpos, omc, spos, srow,
                   bcx, bcy, bcz, yc, zc, tile0, tile1, cntv, cnts, sem):
-    ain, bin_, sin = (a0, a1, a2, a3), (b0, b1, b2, b3), (s0, s1)
-    yas, ybs, zouts = (ya0, ya1, ya2, ya3), (yb0, yb1, yb2, yb3), (z0, z1)
+    tin, sin = (t0, t1, t2, t3), (s0, s1)
+    youts, zouts = (y0, y1, y2, y3), (z0, z1)
     for k in range(NT):
-        cntv[k:k + 1, :] = join(ain[k // ZN], k % ZN, TH)[3:4, 0:128].astype(jnp.int32)
+        cntv[k:k + 1, :] = join(tin[k // ZN], k % ZN, TQ)[3:4, 0:128].astype(jnp.int32)
     for k in range(NS):
         both = [join(sin[k // YN], k % YN, SCAP + 32 * h)[3:4, 0:128] for h in range(SCAP // R)]
         cntv[NT + k:NT + k + 1, :] = sum(both).astype(jnp.int32)
@@ -121,11 +115,10 @@
     fetch_counts.wait()
     toff = [jnp.int32(0)]
     for k in range(NT):
-        dx, dz = k // ZN, k % ZN
+        ref, d = tin[k // ZN], k % ZN
         off = pl.multiple_of(toff[k], GRAN)
-        psic[pl.ds(off, TH), :] = ain[dx][dz, 0:TH, :]
-        psic[pl.ds(off + TH, TH), :] = bin_[dz][dx]
-        tpos[pl.ds(off, TQ), :] = join(ain[dx], dz, TH).T
+        psic[pl.ds(off, TQ), :] = ref[d, 0:TQ, :]
+        tpos[pl.ds(off, TQ), :] = join(ref, d, TQ).T
         toff.append(toff[k] + ceil16(cnts[k, 0]))
     tend = pl.multiple_of(toff[NT], GRAN)
     psic[pl.ds(tend, 2 * TC), :] = jnp.zeros((2 * TC, R), BF16)
@@ -202,27 +195,25 @@
 
     lax.fori_loop(0, (nt * ns + 1) // 2, two_steps, start)
     for k in range(NT):
-        dx, dz = k // ZN, k % ZN
         off = pl.multiple_of(toff[k], GRAN)
-        yas[dx][dz] = yc[pl.ds(off, TH), :]
-        ybs[dz][dx] = yc[pl.ds(off + TH, TH), :]
+        youts[k // ZN][k % ZN] = yc[pl.ds(off, TQ), :]
     for k in range(NS):
         off = pl.multiple_of(soff[k], GRAN)
         zouts[k // YN][k % YN] = zc[pl.ds(off, SCAP), :]
 
 
-def sketch(ain, bin_, sin):
+def sketch(tin, sin):
     vm = pl.BlockSpec(memory_space=pltpu.VMEM)
     trows = NT * TQ + 2 * TC
     srows = NS * SCAP + 2 * SC
     return pl.pallas_call(
         sketch_kernel,
         out_shape=(
-            *[jax.ShapeDtypeStruct((ZN, TH, R), F32)] * (2 * XN),
+            *[jax.ShapeDtypeStruct((ZN, TQ, R), F32)] * XN,
             *[jax.ShapeDtypeStruct((YN, SCAP, R), F32)] * CN,
         ),
-        in_specs=[vm] * 10,
-        out_specs=(vm,) * 10,
+        in_specs=[vm] * 6,
+        out_specs=(vm,) * 6,
         scratch_shapes=[
             pltpu.VMEM((trows, R), BF16),
             pltpu.VMEM((trows, 8), F32),
@@ -241,22 +232,20 @@
             pltpu.SemaphoreType.DMA(()),
         ],
         compiler_params=pltpu.CompilerParams(vmem_limit_bytes=34 << 20),
-    )(*inside(*ain, *bin_, *sin))
-
-
-def finish_kernel(where_ref, a0, a1, a2, a3, b0, b1, b2, b3, z0, z1, z2, z3, pa, pb,
+    )(*inside(*tin, *sin))
+
+
+def finish_kernel(where_ref, y0, y1, y2, y3, z0, z1, z2, z3, tpay,
                   yfin_ref, zfin_ref, keep_ref, send_ref, *, yscale, zscale, tn, sn):
     yq, tcount, scount, core = where_ref[0], where_ref[1], where_ref[2], where_ref[3]
-    row = lax.broadcasted_iota(jnp.int32, (TH, R), 0)
-    for h, part in enumerate(((a0, a1, a2, a3), (b0, b1, b2, b3))):
-        total = (part[0][...] + part[1][...]) + (part[2][...] + part[3][...])
-        q = row + h * TH
-        slot = (q // GRAN) * (GRAN * YN) + yq * GRAN + q % GRAN
-        yfin_ref[h * TH:(h + 1) * TH, :] = jnp.where(slot < tcount, total * yscale, 0.0)
+    q = lax.broadcasted_iota(jnp.int32, (TQ, R), 0)
+    slot = (q // GRAN) * (GRAN * YN) + yq * GRAN + q % GRAN
+    total = (y0[...] + y1[...]) + (y2[...] + y3[...])
+    yfin_ref[...] = jnp.where(slot < tcount, total * yscale, 0.0)
     srow = lax.broadcasted_iota(jnp.int32, (SCAP, R), 0)
     total = (z0[...] + z1[...]) + (z2[...] + z3[...])
     zfin_ref[...] = jnp.where(srow < scount, total * zscale, 0.0)
-    psi = jnp.concatenate([pa[0:TH, :], pb[...]], axis=0).astype(F32)
+    psi = tpay[0:TQ, :].astype(F32)
     y, z = yfin_ref[...], zfin_ref[...]
     hi = lax.Precision.HIGHEST
     dims = (((0,), (0,)), ((), ()))
@@ -272,7 +261,7 @@
         send_ref[k] = jnp.where(first, low, top)
 
 
-def finish(where, a, b, z, pa, pb):
+def finish(where, y, z, tpay):
     tn, sn = TCAP * NT * CN, SCAP * NT * NS
     vm = pl.BlockSpec(memory_space=pltpu.VMEM)
     half = jax.ShapeDtypeStruct((3, R // 2, R), F32)
@@ -290,16 +279,16 @@
             half,
             half,
         ),
-        in_specs=[pl.BlockSpec(memory_space=pltpu.SMEM)] + [vm] * 14,
+        in_specs=[pl.BlockSpec(memory_space=pltpu.SMEM)] + [vm] * 9,
         out_specs=(vm,) * 4,
         compiler_params=pltpu.CompilerParams(vmem_limit_bytes=14 << 20),
-    )(where, *inside(*a, *b, *z, pa, pb))
+    )(where, *inside(*y, *z, tpay))
 
 
 def place_kernel(where_ref, *refs):
     ys, own, other = refs[0:YN], refs[YN:YN + ZN], refs[YN + ZN]
     yout, outs = refs[YN + ZN + 1], refs[YN + ZN + 2:]
-    yq, core, z = where_ref[0], where_ref[3], where_ref[4]
+    yq, core = where_ref[0], where_ref[3]
     for d in range(YN):
         q = lax.rem(yq + d, YN)
         for a in range(TQ // GRAN):
@@ -307,8 +296,9 @@
             yout[pl.ds(at, GRAN), :] = ys[d][a * GRAN:(a + 1) * GRAN, :]
     share = R // CN // ZN
     for d in range(ZN):
-        q = lax.rem(z + d, ZN)
+        q = lax.rem(where_ref[4] + d, ZN)
         at = pl.multiple_of((core * ZN + q) * share, share)
+        q = lax.rem(where_ref[5] + d, ZN)
         far = pl.multiple_of(((1 - core) * ZN + q) * share, share)
         for k in range(3):
             outs[k][pl.ds(at, share), :] = own[d][k]
@@ -329,64 +319,80 @@
     )(where, *inside(*ys, *own, other))
 
 
-def fetch(v, axis, d):
-    n = lax.axis_size(axis)
-    return lax.ppermute(v, axis, [((i + d) % n, i) for i in range(n)])
-
-
-def give(v, axis, d):
-    n = lax.axis_size(axis)
-    return lax.ppermute(v, axis, [(i, (i + d) % n) for i in range(n)])
-
-
-def ring(v, axis):
-    return [v] + [fetch(v, axis, d) for d in range(1, lax.axis_size(axis))]
-
-
-def gathered_sum(v, axis):
-    p = ring(v, axis)
+FIRST = ("x", "z")
+LAST = ("z", "x")
+SAME = {name: (name, name) for name in ALL}
+
+
+def shifted(axes, d):
+    pairs = []
+    size = dict(z=ZN, x=XN, c=CN, y=YN)
+    for z in range(ZN):
+        for x in range(XN):
+            for c in range(CN):
+                for y in range(YN):
+                    at = dict(z=z, x=x, c=c, y=y)
+                    to = dict(at)
+                    to[axes[c]] = (at[axes[c]] + d) % size[axes[c]]
+                    flat = [((p["z"] * XN + p["x"]) * CN + p["c"]) * YN + p["y"] for p in (at, to)]
+                    pairs.append(tuple(flat))
+    return pairs
+
+
+def fetch(v, axes, d):
+    return lax.ppermute(v, ALL, [(b, a) for a, b in shifted(axes, d)])
+
+
+def give(v, axes, d):
+    return lax.ppermute(v, ALL, shifted(axes, d))
+
+
+def ring(v, axes):
+    return [v] + [fetch(v, axes, d) for d in range(1, 4)]
+
+
+def gathered_sum(v, axes):
+    p = ring(v, axes)
     return (p[0] + p[2]) + (p[1] + p[3])
 
 
-def returned(vs, axis):
-    return [vs[0]] + [give(vs[d], axis, d) for d in range(1, len(vs))]
+def returned(vs, axes):
+    return [vs[0]] + [give(vs[d], axes, d) for d in range(1, len(vs))]
 
 
 def steps(target_xyz, source_xyz, target_count, source_count, psi, omega):
-    yq, core, z = (lax.axis_index(n) for n in ("y", "c", "z"))
-    where = jnp.stack([yq, target_count[0], source_count[0], core, z]).astype(jnp.int32)
-    apay, bpay, spay = pack(where, target_xyz, source_xyz, psi, omega)
-    arow = ring(apay, "z")
-    brow = ring(bpay, "x")
-    srow = ring(spay, "y")
-    ain = ring(jnp.stack(arow), "x")
-    bin_ = ring(jnp.stack(brow), "z")
+    z, x, core, yq = (lax.axis_index(n) for n in ALL)
+    along = jnp.where(core == 0, x, z)
+    across = jnp.where(core == 0, z, x)
+    where = jnp.stack([yq, target_count[0], source_count[0], core, along, across])
+    where = where.astype(jnp.int32)
+    tpay, spay = pack(where, target_xyz, source_xyz, psi, omega)
+    trow = ring(tpay, FIRST)
+    srow = ring(spay, SAME["y"])
+    tin = ring(jnp.stack(trow), LAST)
     srep = jnp.stack(srow)
-    sfar = fetch(srep, "c", 1)
-    parts = sketch(ain, bin_, [srep, sfar])
-    ya, yb, (z0, z1) = parts[0:4], parts[4:8], parts[8:10]
-    zfar = give(z1, "c", 1)
-    ax = returned(ya, "x")
-    bz = returned(yb, "z")
+    sfar = fetch(srep, SAME["c"], 1)
+    parts = sketch(tin, [srep, sfar])
+    ys, (z0, z1) = parts[0:4], parts[4:6]
+    zfar = give(z1, SAME["c"], 1)
+    ys = returned(ys, LAST)
     zmine = [z0[d] + zfar[d] for d in range(YN)]
-    zs = returned(zmine, "y")
-    ax = [(ax[0][d] + ax[1][d]) + (ax[2][d] + ax[3][d]) for d in range(ZN)]
-    bz = [(bz[0][d] + bz[1][d]) + (bz[2][d] + bz[3][d]) for d in range(XN)]
-    a = returned(ax, "z")
-    b = returned(bz, "x")
-    yfin, zfin, keep, send = finish(where, a, b, zs, apay, bpay)
-    ys = ring(yfin, "y")
-    half = keep + fetch(send, "c", 1)
+    zs = returned(zmine, SAME["y"])
+    ys = [(ys[0][d] + ys[1][d]) + (ys[2][d] + ys[3][d]) for d in range(ZN)]
+    ys = returned(ys, FIRST)
+    yfin, zfin, keep, send = finish(where, ys, zs, tpay)
+    ys = ring(yfin, SAME["y"])
+    half = keep + fetch(send, SAME["c"], 1)
     half = half.reshape(3, ZN, R // CN // ZN, R)
     chunks = [
-        lax.dynamic_index_in_dim(half, lax.rem(z + d, ZN), 1, keepdims=False)
+        lax.dynamic_index_in_dim(half, lax.rem(along + d, ZN), 1, keepdims=False)
         for d in range(ZN)
     ]
-    p = returned(chunks, "z")
+    p = returned(chunks, FIRST)
     mine = (p[0] + p[1]) + (p[2] + p[3])
-    mine = gathered_sum(gathered_sum(mine, "x"), "y")
-    own = ring(mine, "z")
-    other = fetch(jnp.stack(own), "c", 1)
+    mine = gathered_sum(gathered_sum(mine, LAST), SAME["y"])
+    own = ring(mine, FIRST)
+    other = fetch(jnp.stack(own), SAME["c"], 1)
     y, g0, g1, g2 = place(where, ys, own, other)
     return (y, zfin, g0, g1, g2)
 

time: 213 us -> 185 us (0.87)
  starting transfers between devices: 65.4 us -> 47.9 us
  waiting for transfers between devices: 122 us -> 112 us
  local copies, waits for them, and re-layouts: 3.52 us -> 0.64 us
    ppermute x49 -> x37, starting transfers between devices: 65.4 us -> 47.9 us  [the longest x24 32.6 us: fetch(): return lax.ppermute(v, ALL, [(b, a) for a, b in shifted(axes, d)])]
    ppermute x49 -> x37, waiting for transfers between devices: 122 us -> 112 us  [the longest x24 63.8 us: fetch(): return lax.ppermute(v, ALL, [(b, a) for a, b in shifted(axes, d)])]
    unnamed x8 -> x4, local copies, waits for them, and re-layouts: 3.4 us -> 0.01 us
  transfers between devices with their start and end apart: 49 -> 37, of which waited for: 27 -> 31; matrix products, arithmetic and copies ran while one was open for 0% -> 0% of each run, Pallas kernels for 0% -> 0%
where the time goes in v2:
time: 185 us
  waiting for transfers between devices  112 us (61%)
  starting transfers between devices  47.9 us (26%)
  Pallas kernels  20.2 us (11%)
  other arithmetic  2.12 us (1%)
  between operations  2.05 us (1%)
    ppermute x24, waiting for transfers between devices, fetch(): return lax.ppermute(v, ALL, [(b, a) for a, b in shifted(axes, d)])  63.8 us
    ppermute x13, waiting for transfers between devices, give(): return lax.ppermute(v, ALL, shifted(axes, d))  48 us
    ppermute x24, starting transfers between devices, fetch(): return lax.ppermute(v, ALL, [(b, a) for a, b in shifted(axes, d)])  32.6 us
    ppermute x13, starting transfers between devices, give(): return lax.ppermute(v, ALL, shifted(axes, d))  15.4 us
    pallas_call x1, Pallas kernels, sketch(): pl.pallas_call(sketch_kernel, out_shape=(*[jax.ShapeDtypeStruct((ZN, TQ,...  14.1 us
  transfers between devices with their start and end apart: 37, of which 31 were waited for; matrix products, arithmetic and copies ran while one was open for 0% of the time, Pallas kernels for 0%

profile of v2, /device:TPU:1, one launch (start us, length us, event | category | flops | bytes accessed | tf_op | source)
XLA Modules:
  0.0 184.8 jit_solution(15820623204084570318)
XLA Ops:
  2.5 2.2 %shard_map.101 = (bf16[288,256]{1,0:T(8,128)(2,1)}, bf16[576,256]{1,0:T(8,128)(2,1)}) custom-call(s32[6]{0:T(128)} %stack.64.where_ref.refs_0_, f32[3,1024]{1,0:T(4,128)} %txyz_ref.1, f32[3,512]{1,0:T(4,128)} %sxyz_ref.1, bf16[1024,256]{1,0:T(8,128)(2,1)} %psi_ref.1, bf16[512,256]{1,0:T(8,128)(2,1)} %omega_ref.1), custom_call_target="tpu_custom_call" | custom-call | tf_op jit(solution)/shard_map/pallas_call | solution.py:81
  4.7 3.7 %collective-permute-start.7 = (bf16[576,256]{1,0:T(8,128)(2,1)}, bf16[576,256]{1,0:T(8,128)(2,1)S(1)}, u32[]{:S(2)}, u32[]{:S(2)}) collective-permute-start(bf16[576,256]{1,0:T(8,128)(2,1)} %get-tuple-element.22), channel_id=1, source_target_pairs={{2,0},{3,1},{0,2},{1,3},{6,4},{7,5},{4,6},{5,7},{10,8},{11,9},{8,1... | collective-permute-start | bytes 884744 | tf_op jit(solution)/shard_map/ppermute | solution.py:343
  8.9 2.3 %collective-permute-start.6 = (bf16[576,256]{1,0:T(8,128)(2,1)}, bf16[576,256]{1,0:T(8,128)(2,1)S(1)}, u32[]{:S(2)}, u32[]{:S(2)}) collective-permute-start(bf16[576,256]{1,0:T(8,128)(2,1)} %get-tuple-element.22), channel_id=1, source_target_pairs={{1,0},{2,1},{3,2},{0,3},{5,4},{6,5},{7,6},{4,7},{9,8},{10,9},{11,1... | collective-permute-start | bytes 884744 | tf_op jit(solution)/shard_map/ppermute | solution.py:343
  11.1 4.1 %collective-permute-done.7 = bf16[576,256]{1,0:T(8,128)(2,1)S(1)} collective-permute-done((bf16[576,256]{1,0:T(8,128)(2,1)}, bf16[576,256]{1,0:T(8,128)(2,1)S(1)}, u32[]{:S(2)}, u32[]{:S(2)}) %collective-permute-start.7) | collective-permute-done | bytes 294944 | tf_op jit(solution)/shard_map/ppermute | solution.py:343
  15.2 7.3 %collective-permute-done.8 = bf16[576,256]{1,0:T(8,128)(2,1)S(1)} collective-permute-done((bf16[576,256]{1,0:T(8,128)(2,1)}, bf16[576,256]{1,0:T(8,128)(2,1)S(1)}, u32[]{:S(2)}, u32[]{:S(2)}) %collective-permute-start.8) | collective-permute-done | bytes 294944 | tf_op jit(solution)/shard_map/ppermute | solution.py:343
  24.6 3.8 %collective-permute-start = (bf16[288,256]{1,0:T(8,128)(2,1)S(1)}, bf16[288,256]{1,0:T(8,128)(2,1)S(1)}, u32[]{:S(2)}, u32[]{:S(2)}) collective-permute-start(bf16[288,256]{1,0:T(8,128)(2,1)S(1)} %copy-done), channel_id=1, source_target_pairs={{8,0},{9,1},{10,2},{11,3},{36,4},{37,5},{38,6},{39,7},{16,8},{17,9... | collective-permute-start | bytes 442376 | tf_op jit(solution)/shard_map/ppermute | solution.py:343
  29.1 3.0 %collective-permute-done = bf16[288,256]{1,0:T(8,128)(2,1)S(1)} collective-permute-done((bf16[288,256]{1,0:T(8,128)(2,1)S(1)}, bf16[288,256]{1,0:T(8,128)(2,1)S(1)}, u32[]{:S(2)}, u32[]{:S(2)}) %collective-permute-start) | collective-permute-done | bytes 147488 | tf_op jit(solution)/shard_map/ppermute | solution.py:343
  32.0 1.9 %collective-permute-done.1 = bf16[288,256]{1,0:T(8,128)(2,1)S(1)} collective-permute-done((bf16[288,256]{1,0:T(8,128)(2,1)S(1)}, bf16[288,256]{1,0:T(8,128)(2,1)S(1)}, u32[]{:S(2)}, u32[]{:S(2)}) %collective-permute-start.1) | collective-permute-done | bytes 147488 | tf_op jit(solution)/shard_map/ppermute | solution.py:343
  35.4 2.4 %collective-permute-start.3 = (bf16[4,288,256]{2,1,0:T(8,128)(2,1)S(1)}, bf16[4,288,256]{2,1,0:T(8,128)(2,1)S(1)}, u32[]{:S(2)}, u32[]{:S(2)}) collective-permute-start(bf16[4,288,256]{2,1,0:T(8,128)(2,1)S(1)} %pad_maximum_fusion.1.t0), channel_id=1, source_target_pairs={{32,0},{33,1},{34,2},{35,3},{12,4},{13,5},{14,6},{15,7},{40,8},{41... | collective-permute-start | bytes 1769480 | tf_op jit(solution)/shard_map/ppermute | solution.py:343
  38.9 12.0 %collective-permute-done.3.t1 = bf16[4,288,256]{2,1,0:T(8,128)(2,1)S(1)} collective-permute-done((bf16[4,288,256]{2,1,0:T(8,128)(2,1)S(1)}, bf16[4,288,256]{2,1,0:T(8,128)(2,1)S(1)}, u32[]{:S(2)}, u32[]{:S(2)}) %collective-permute-start.3) | collective-permute-done | bytes 589856 | tf_op jit(solution)/shard_map/ppermute | solution.py:343
  50.9 3.7 %collective-permute-done.5.t3 = bf16[4,288,256]{2,1,0:T(8,128)(2,1)S(1)} collective-permute-done((bf16[4,288,256]{2,1,0:T(8,128)(2,1)S(1)}, bf16[4,288,256]{2,1,0:T(8,128)(2,1)S(1)}, u32[]{:S(2)}, u32[]{:S(2)}) %collective-permute-start.5) | collective-permute-done | bytes 589856 | tf_op jit(solution)/shard_map/ppermute | solution.py:343
  54.6 14.1 %shard_map.102 = (f32[4,256,256]{2,1,0:T(8,128)S(1)}, f32[4,256,256]{2,1,0:T(8,128)S(1)}, f32[4,256,256]{2,1,0:T(8,128)S(1)}, f32[4,256,256]{2,1,0:T(8,128)S(1)}...) custom-call(bf16[4,288,256]{2,1,0:T(8,128)(2,1)S(1)} %pad_maximum_fusion.1.t0, ...), custom_call_target="tpu_custom_call" | custom-call | tf_op jit(solution)/shard_map/pallas_call | solution.py:209
  68.7 2.7 %collective-permute-start.16 = (f32[4,512,256]{2,1,0:T(8,128)S(1)}, f32[4,512,256]{2,1,0:T(8,128)S(1)}, u32[]{:S(2)}, u32[]{:S(2)}) collective-permute-start(f32[4,512,256]{2,1,0:T(8,128)S(1)} %get-tuple-element.28), channel_id=1, source_target_pairs={{0,4},{1,5},{2,6},{3,7},{4,0},{5,1},{6,2},{7,3},{8,12},{9,13},{10,... | collective-permute-start | bytes 6291464 | tf_op jit(solution)/shard_map/ppermute | solution.py:347
  72.0 2.2 %collective-permute-start.12 = (f32[4,256,256]{2,1,0:T(8,128)S(1)}, f32[4,256,256]{2,1,0:T(8,128)S(1)}, u32[]{:S(2)}, u32[]{:S(2)}) collective-permute-start(f32[4,256,256]{2,1,0:T(8,128)S(1)} %get-tuple-element.26), channel_id=1, source_target_pairs={{0,96},{1,97},{2,98},{3,99},{4,28},{5,29},{6,30},{7,31},{8,104},{9... | collective-permute-start | bytes 3145736 | tf_op jit(solution)/shard_map/ppermute | solution.py:347
  74.1 23.7 %collective-permute-done.10 = f32[4,256,256]{2,1,0:T(8,128)S(1)} collective-permute-done((f32[4,256,256]{2,1,0:T(8,128)S(1)}, f32[4,256,256]{2,1,0:T(8,128)S(1)}, u32[]{:S(2)}, u32[]{:S(2)}) %collective-permute-start.10) | collective-permute-done | bytes 1048608 | tf_op jit(solution)/shard_map/ppermute | solution.py:347
  101.4 1.8 collective-permute-start.19
  103.2 1.8 collective-permute-start.14
  105.9 4.4 %collective-permute-done.14.refs_3_ = f32[256,256]{1,0:T(8,128)S(1)} collective-permute-done((f32[256,256]{1,0:T(8,128)S(1)}, f32[256,256]{1,0:T(8,128)S(1)}, u32[]{:S(2)}, u32[]{:S(2)}) %collective-permute-start.14) | collective-permute-done | bytes 262176 | tf_op jit(solution)/shard_map/ppermute | solution.py:347
  110.3 3.1 %collective-permute-done.15.refs_4_ = f32[256,256]{1,0:T(8,128)S(1)} collective-permute-done((f32[256,256]{1,0:T(8,128)S(1)}, f32[256,256]{1,0:T(8,128)S(1)}, u32[]{:S(2)}, u32[]{:S(2)}) %collective-permute-start.15) | collective-permute-done | bytes 262176 | tf_op jit(solution)/shard_map/ppermute | solution.py:347
  113.5 10.0 %collective-permute-done.18.refs_7_ = f32[512,256]{1,0:T(8,128)S(1)} collective-permute-done((f32[512,256]{1,0:T(8,128)S(1)}, f32[512,256]{1,0:T(8,128)S(1)}, u32[]{:S(2)}, u32[]{:S(2)}) %collective-permute-start.18) | collective-permute-done | bytes 524320 | tf_op jit(solution)/shard_map/ppermute | solution.py:347
  123.5 1.8 collective-permute-done.19.refs_8_
  125.2 2.1 %shard_map.103 = (f32[256,256]{1,0:T(8,128)S(1)}, f32[512,256]{1,0:T(8,128)}, f32[3,128,256]{2,1,0:T(8,128)S(1)}, f32[3,128,256]{2,1,0:T(8,128)S(1)}) custom-call(s32[6]{0:T(128)S(1)} %copy-done.1, f32[256,256]{1,0:T(8,128)S(1)} %get-tuple-element.44.refs_1_, f32[256,256]{1,0:T(8,128)S(1)} %collective-permute-done.13.refs_2_, ...), custom_call_target="tpu_custom_call" | custom-call | tf_op jit(solution)/shard_map/pallas_call | solution.py:274
  130.4 3.8 %collective-permute-start.25 = (f32[3,32,256]{2,1,0:T(8,128)S(1)}, f32[3,32,256]{2,1,0:T(8,128)S(1)}, u32[]{:S(2)}, u32[]{:S(2)}) collective-permute-start(f32[3,32,256]{2,1,0:T(8,128)S(1)} %get-tuple-element.46), channel_id=1, source_target_pairs={{0,16},{1,17},{2,18},{3,19},{4,68},{5,69},{6,70},{7,71},{8,24},{9,... | collective-permute-start | bytes 294920 | tf_op jit(solution)/shard_map/ppermute | solution.py:347
  135.3 2.2 %collective-permute-done.25 = f32[3,32,256]{2,1,0:T(8,128)S(1)} collective-permute-done((f32[3,32,256]{2,1,0:T(8,128)S(1)}, f32[3,32,256]{2,1,0:T(8,128)S(1)}, u32[]{:S(2)}, u32[]{:S(2)}) %collective-permute-start.25) | collective-permute-done | bytes 98336 | tf_op jit(solution)/shard_map/ppermute | solution.py:347
  140.4 2.6 %collective-permute-done.27 = f32[3,32,256]{2,1,0:T(8,128)S(1)} collective-permute-done((f32[3,32,256]{2,1,0:T(8,128)S(1)}, f32[3,32,256]{2,1,0:T(8,128)S(1)}, u32[]{:S(2)}, u32[]{:S(2)}) %collective-permute-start.27) | collective-permute-done | bytes 98336 | tf_op jit(solution)/shard_map/ppermute | solution.py:343
  145.0 1.9 %collective-permute-start.30 = (f32[3,32,256]{2,1,0:T(8,128)S(1)}, f32[3,32,256]{2,1,0:T(8,128)S(1)}, u32[]{:S(2)}, u32[]{:S(2)}) collective-permute-start(f32[3,32,256]{2,1,0:T(8,128)S(1)} %add_add_fusion.1), channel_id=1, source_target_pairs={{2,0},{3,1},{0,2},{1,3},{6,4},{7,5},{4,6},{5,7},{10,8},{11,9},{8,1... | collective-permute-start | bytes 294920 | tf_op jit(solution)/shard_map/ppermute | solution.py:343
  151.1 3.3 %collective-permute-done.32 = f32[3,32,256]{2,1,0:T(8,128)S(1)} collective-permute-done((f32[3,32,256]{2,1,0:T(8,128)S(1)}, f32[3,32,256]{2,1,0:T(8,128)S(1)}, u32[]{:S(2)}, u32[]{:S(2)}) %collective-permute-start.32) | collective-permute-done | bytes 98336 | tf_op jit(solution)/shard_map/ppermute | solution.py:343
  157.9 2.8 %collective-permute-done.34.refs_6_ = f32[3,32,256]{2,1,0:T(8,128)S(1)} collective-permute-done((f32[3,32,256]{2,1,0:T(8,128)S(1)}, f32[3,32,256]{2,1,0:T(8,128)S(1)}, u32[]{:S(2)}, u32[]{:S(2)}) %collective-permute-start.34) | collective-permute-done | bytes 98336 | tf_op jit(solution)/shard_map/ppermute | solution.py:343
  161.6 5.8 %collective-permute-start.36 = (f32[4,3,32,256]{3,2,1,0:T(8,128)S(1)}, f32[4,3,32,256]{3,2,1,0:T(8,128)S(1)}, u32[]{:S(2)}, u32[]{:S(2)}) collective-permute-start(f32[4,3,32,256]{3,2,1,0:T(8,128)S(1)} %pad_maximum_fusion.2), channel_id=1, source_target_pairs={{4,0},{5,1},{6,2},{7,3},{0,4},{1,5},{2,6},{3,7},{12,8},{13,9},{14,... | collective-permute-start | bytes 1179656 | tf_op jit(solution)/shard_map/ppermute | solution.py:343
  169.0 6.3 %collective-permute-done.20.refs_1_ = f32[256,256]{1,0:T(8,128)S(1)} collective-permute-done((f32[256,256]{1,0:T(8,128)S(1)}, f32[256,256]{1,0:T(8,128)S(1)}, u32[]{:S(2)}, u32[]{:S(2)}) %collective-permute-start.20) | collective-permute-done | bytes 262176 | tf_op jit(solution)/shard_map/ppermute | solution.py:343
  176.7 6.1 %collective-permute-done.22.refs_3_ = f32[256,256]{1,0:T(8,128)S(1)} collective-permute-done((f32[256,256]{1,0:T(8,128)S(1)}, f32[256,256]{1,0:T(8,128)S(1)}, u32[]{:S(2)}, u32[]{:S(2)}) %collective-permute-start.22) | collective-permute-done | bytes 262176 | tf_op jit(solution)/shard_map/ppermute | solution.py:343
  182.9 1.9 %shard_map.104 = (f32[1024,256]{1,0:T(8,128)}, f32[256,256]{1,0:T(8,128)}, f32[256,256]{1,0:T(8,128)}, f32[256,256]{1,0:T(8,128)}) custom-call(s32[6]{0:T(128)S(1)} %copy-done.1, f32[256,256]{1,0:T(8,128)S(1)} %get-tuple-element.29.refs_0_, f32[256,256]{1,0:T(8,128)S(1)} %collective-permute-done.20.refs_1_, f32[256,256]{1,0:T(8,128)S(1)} %collective-permute-done.21.refs_2_, ...), custom_call_target="tpu_custom_call" | custom-call | tf_op jit(solution)/shard_map/pallas_call | solution.py:310
  (61 shorter events, 32.2 us)
Async XLA Ops:
  4.7 10.5 %collective-permute-start.7 = (bf16[576,256]{1,0:T(8,128)(2,1)}, bf16[576,256]{1,0:T(8,128)(2,1)S(1)}, u32[]{:S(2)}, u32[]{:S(2)}) collective-permute-start(bf16[576,256]{1,0:T(8,128)(2,1)} %get-tuple-element.22), channel_id=1, source_target_pairs={{2,0},{3,1},{0,2},{1,3},{6,4},{7,5},{4,6},{5,7},{10,8},{11,9},{8,1... | collective-permute-start | bytes 884744 | tf_op jit(solution)/shard_map/ppermute | solution.py:343
  8.5 14.0 %collective-permute-start.8 = (bf16[576,256]{1,0:T(8,128)(2,1)}, bf16[576,256]{1,0:T(8,128)(2,1)S(1)}, u32[]{:S(2)}, u32[]{:S(2)}) collective-permute-start(bf16[576,256]{1,0:T(8,128)(2,1)} %get-tuple-element.22), channel_id=1, source_target_pairs={{3,0},{0,1},{1,2},{2,3},{7,4},{4,5},{5,6},{6,7},{11,8},{8,9},{9,10... | collective-permute-start | bytes 884744 | tf_op jit(solution)/shard_map/ppermute | solution.py:343
  8.9 13.6 %collective-permute-start.6 = (bf16[576,256]{1,0:T(8,128)(2,1)}, bf16[576,256]{1,0:T(8,128)(2,1)S(1)}, u32[]{:S(2)}, u32[]{:S(2)}) collective-permute-start(bf16[576,256]{1,0:T(8,128)(2,1)} %get-tuple-element.22), channel_id=1, source_target_pairs={{1,0},{2,1},{3,2},{0,3},{5,4},{6,5},{7,6},{4,7},{9,8},{10,9},{11,1... | collective-permute-start | bytes 884744 | tf_op jit(solution)/shard_map/ppermute | solution.py:343
  23.6 31.0 %collective-permute-start.9 = (bf16[4,576,256]{2,1,0:T(8,128)(2,1)S(1)}, bf16[4,576,256]{2,1,0:T(8,128)(2,1)S(1)}, u32[]{:S(2)}, u32[]{:S(2)}) collective-permute-start(bf16[4,576,256]{2,1,0:T(8,128)(2,1)S(1)} %pad_maximum_fusion.s0), channel_id=1, source_target_pairs={{4,0},{5,1},{6,2},{7,3},{0,4},{1,5},{2,6},{3,7},{12,8},{13,9},{14,... | collective-permute-start | bytes 3538952 | tf_op jit(solution)/shard_map/ppermute | solution.py:343
  24.6 7.4 %collective-permute-start = (bf16[288,256]{1,0:T(8,128)(2,1)S(1)}, bf16[288,256]{1,0:T(8,128)(2,1)S(1)}, u32[]{:S(2)}, u32[]{:S(2)}) collective-permute-start(bf16[288,256]{1,0:T(8,128)(2,1)S(1)} %copy-done), channel_id=1, source_target_pairs={{8,0},{9,1},{10,2},{11,3},{36,4},{37,5},{38,6},{39,7},{16,8},{17,9... | collective-permute-start | bytes 442376 | tf_op jit(solution)/shard_map/ppermute | solution.py:343
  28.4 5.6 %collective-permute-start.1 = (bf16[288,256]{1,0:T(8,128)(2,1)S(1)}, bf16[288,256]{1,0:T(8,128)(2,1)S(1)}, u32[]{:S(2)}, u32[]{:S(2)}) collective-permute-start(bf16[288,256]{1,0:T(8,128)(2,1)S(1)} %copy-done), channel_id=1, source_target_pairs={{16,0},{17,1},{18,2},{19,3},{68,4},{69,5},{70,6},{71,7},{24,8},{25... | collective-permute-start | bytes 442376 | tf_op jit(solution)/shard_map/ppermute | solution.py:343
  28.4 6.9 %collective-permute-start.2 = (bf16[288,256]{1,0:T(8,128)(2,1)S(1)}, bf16[288,256]{1,0:T(8,128)(2,1)S(1)}, u32[]{:S(2)}, u32[]{:S(2)}) collective-permute-start(bf16[288,256]{1,0:T(8,128)(2,1)S(1)} %copy-done), channel_id=1, source_target_pairs={{24,0},{25,1},{26,2},{27,3},{100,4},{101,5},{102,6},{103,7},{0,8},... | collective-permute-start | bytes 442376 | tf_op jit(solution)/shard_map/ppermute | solution.py:343
  35.4 15.6 %collective-permute-start.3 = (bf16[4,288,256]{2,1,0:T(8,128)(2,1)S(1)}, bf16[4,288,256]{2,1,0:T(8,128)(2,1)S(1)}, u32[]{:S(2)}, u32[]{:S(2)}) collective-permute-start(bf16[4,288,256]{2,1,0:T(8,128)(2,1)S(1)} %pad_maximum_fusion.1.t0), channel_id=1, source_target_pairs={{32,0},{33,1},{34,2},{35,3},{12,4},{13,5},{14,6},{15,7},{40,8},{41... | collective-permute-start | bytes 1769480 | tf_op jit(solution)/shard_map/ppermute | solution.py:343
  37.8 13.2 %collective-permute-start.4 = (bf16[4,288,256]{2,1,0:T(8,128)(2,1)S(1)}, bf16[4,288,256]{2,1,0:T(8,128)(2,1)S(1)}, u32[]{:S(2)}, u32[]{:S(2)}) collective-permute-start(bf16[4,288,256]{2,1,0:T(8,128)(2,1)S(1)} %pad_maximum_fusion.1.t0), channel_id=1, source_target_pairs={{64,0},{65,1},{66,2},{67,3},{20,4},{21,5},{22,6},{23,7},{72,8},{73... | collective-permute-start | bytes 1769480 | tf_op jit(solution)/shard_map/ppermute | solution.py:343
  38.3 16.3 %collective-permute-start.5 = (bf16[4,288,256]{2,1,0:T(8,128)(2,1)S(1)}, bf16[4,288,256]{2,1,0:T(8,128)(2,1)S(1)}, u32[]{:S(2)}, u32[]{:S(2)}) collective-permute-start(bf16[4,288,256]{2,1,0:T(8,128)(2,1)S(1)} %pad_maximum_fusion.1.t0), channel_id=1, source_target_pairs={{96,0},{97,1},{98,2},{99,3},{28,4},{29,5},{30,6},{31,7},{104,8},{1... | collective-permute-start | bytes 1769480 | tf_op jit(solution)/shard_map/ppermute | solution.py:343
  68.7 30.2 %collective-permute-start.16 = (f32[4,512,256]{2,1,0:T(8,128)S(1)}, f32[4,512,256]{2,1,0:T(8,128)S(1)}, u32[]{:S(2)}, u32[]{:S(2)}) collective-permute-start(f32[4,512,256]{2,1,0:T(8,128)S(1)} %get-tuple-element.28), channel_id=1, source_target_pairs={{0,4},{1,5},{2,6},{3,7},{4,0},{5,1},{6,2},{7,3},{8,12},{9,13},{10,... | collective-permute-start | bytes 6291464 | tf_op jit(solution)/shard_map/ppermute | solution.py:347
  71.5 26.4 %collective-permute-start.10 = (f32[4,256,256]{2,1,0:T(8,128)S(1)}, f32[4,256,256]{2,1,0:T(8,128)S(1)}, u32[]{:S(2)}, u32[]{:S(2)}) collective-permute-start(f32[4,256,256]{2,1,0:T(8,128)S(1)} %get-tuple-element.24), channel_id=1, source_target_pairs={{0,32},{1,33},{2,34},{3,35},{4,12},{5,13},{6,14},{7,15},{8,40},{9,... | collective-permute-start | bytes 3145736 | tf_op jit(solution)/shard_map/ppermute | solution.py:347
  71.5 26.4 %collective-permute-start.11 = (f32[4,256,256]{2,1,0:T(8,128)S(1)}, f32[4,256,256]{2,1,0:T(8,128)S(1)}, u32[]{:S(2)}, u32[]{:S(2)}) collective-permute-start(f32[4,256,256]{2,1,0:T(8,128)S(1)} %get-tuple-element.25), channel_id=1, source_target_pairs={{0,64},{1,65},{2,66},{3,67},{4,20},{5,21},{6,22},{7,23},{8,72},{9,... | collective-permute-start | bytes 3145736 | tf_op jit(solution)/shard_map/ppermute | solution.py:347
  72.0 26.5 %collective-permute-start.12 = (f32[4,256,256]{2,1,0:T(8,128)S(1)}, f32[4,256,256]{2,1,0:T(8,128)S(1)}, u32[]{:S(2)}, u32[]{:S(2)}) collective-permute-start(f32[4,256,256]{2,1,0:T(8,128)S(1)} %get-tuple-element.26), channel_id=1, source_target_pairs={{0,96},{1,97},{2,98},{3,99},{4,28},{5,29},{6,30},{7,31},{8,104},{9... | collective-permute-start | bytes 3145736 | tf_op jit(solution)/shard_map/ppermute | solution.py:347
  98.8 6.8 %collective-permute-start.13 = (f32[256,256]{1,0:T(8,128)S(1)}, f32[256,256]{1,0:T(8,128)S(1)}, u32[]{:S(2)}, u32[]{:S(2)}) collective-permute-start(f32[256,256]{1,0:T(8,128)S(1)} %get-tuple-element.43), channel_id=1, source_target_pairs={{0,8},{1,9},{2,10},{3,11},{4,36},{5,37},{6,38},{7,39},{8,16},{9,17... | collective-permute-start | bytes 786440 | tf_op jit(solution)/shard_map/ppermute | solution.py:347
  99.3 14.2 %collective-permute-start.17 = (f32[512,256]{1,0:T(8,128)S(1)}, f32[512,256]{1,0:T(8,128)S(1)}, u32[]{:S(2)}, u32[]{:S(2)}) collective-permute-start(f32[512,256]{1,0:T(8,128)S(1)} %get-tuple-element.39), channel_id=1, source_target_pairs={{0,1},{1,2},{2,3},{3,0},{4,5},{5,6},{6,7},{7,4},{8,9},{9,10},{10,1... | collective-permute-start | bytes 1572872 | tf_op jit(solution)/shard_map/ppermute | solution.py:347
  100.5 23.0 %collective-permute-start.18 = (f32[512,256]{1,0:T(8,128)S(1)}, f32[512,256]{1,0:T(8,128)S(1)}, u32[]{:S(2)}, u32[]{:S(2)}) collective-permute-start(f32[512,256]{1,0:T(8,128)S(1)} %get-tuple-element.38), channel_id=1, source_target_pairs={{0,2},{1,3},{2,0},{3,1},{4,6},{5,7},{6,4},{7,5},{8,10},{9,11},{10,... | collective-permute-start | bytes 1572872 | tf_op jit(solution)/shard_map/ppermute | solution.py:347
  101.4 23.8 %collective-permute-start.19 = (f32[512,256]{1,0:T(8,128)S(1)}, f32[512,256]{1,0:T(8,128)S(1)}, u32[]{:S(2)}, u32[]{:S(2)}) collective-permute-start(f32[512,256]{1,0:T(8,128)S(1)} %get-tuple-element.37), channel_id=1, source_target_pairs={{0,3},{1,0},{2,1},{3,2},{4,7},{5,4},{6,5},{7,6},{8,11},{9,8},{10,9... | collective-permute-start | bytes 1572872 | tf_op jit(solution)/shard_map/ppermute | solution.py:347
  103.2 7.0 %collective-permute-start.14 = (f32[256,256]{1,0:T(8,128)S(1)}, f32[256,256]{1,0:T(8,128)S(1)}, u32[]{:S(2)}, u32[]{:S(2)}) collective-permute-start(f32[256,256]{1,0:T(8,128)S(1)} %get-tuple-element.42), channel_id=1, source_target_pairs={{0,16},{1,17},{2,18},{3,19},{4,68},{5,69},{6,70},{7,71},{8,24},{9,... | collective-permute-start | bytes 786440 | tf_op jit(solution)/shard_map/ppermute | solution.py:347
  105.6 7.8 %collective-permute-start.15 = (f32[256,256]{1,0:T(8,128)S(1)}, f32[256,256]{1,0:T(8,128)S(1)}, u32[]{:S(2)}, u32[]{:S(2)}) collective-permute-start(f32[256,256]{1,0:T(8,128)S(1)} %get-tuple-element.41), channel_id=1, source_target_pairs={{0,24},{1,25},{2,26},{3,27},{4,100},{5,101},{6,102},{7,103},{8,0},... | collective-permute-start | bytes 786440 | tf_op jit(solution)/shard_map/ppermute | solution.py:347
  130.3 5.0 %collective-permute-start.24 = (f32[3,32,256]{2,1,0:T(8,128)S(1)}, f32[3,32,256]{2,1,0:T(8,128)S(1)}, u32[]{:S(2)}, u32[]{:S(2)}) collective-permute-start(f32[3,32,256]{2,1,0:T(8,128)S(1)} %get-tuple-element.47), channel_id=1, source_target_pairs={{0,8},{1,9},{2,10},{3,11},{4,36},{5,37},{6,38},{7,39},{8,16},{9,17... | collective-permute-start | bytes 294920 | tf_op jit(solution)/shard_map/ppermute | solution.py:347
  130.4 7.1 %collective-permute-start.25 = (f32[3,32,256]{2,1,0:T(8,128)S(1)}, f32[3,32,256]{2,1,0:T(8,128)S(1)}, u32[]{:S(2)}, u32[]{:S(2)}) collective-permute-start(f32[3,32,256]{2,1,0:T(8,128)S(1)} %get-tuple-element.46), channel_id=1, source_target_pairs={{0,16},{1,17},{2,18},{3,19},{4,68},{5,69},{6,70},{7,71},{8,24},{9,... | collective-permute-start | bytes 294920 | tf_op jit(solution)/shard_map/ppermute | solution.py:347
  138.0 5.1 %collective-permute-start.27 = (f32[3,32,256]{2,1,0:T(8,128)S(1)}, f32[3,32,256]{2,1,0:T(8,128)S(1)}, u32[]{:S(2)}, u32[]{:S(2)}) collective-permute-start(f32[3,32,256]{2,1,0:T(8,128)S(1)} %fusion.12), channel_id=1, source_target_pairs={{64,0},{65,1},{66,2},{67,3},{20,4},{21,5},{22,6},{23,7},{72,8},{73... | collective-permute-start | bytes 294920 | tf_op jit(solution)/shard_map/ppermute | solution.py:343
  138.7 5.1 %collective-permute-start.28 = (f32[3,32,256]{2,1,0:T(8,128)S(1)}, f32[3,32,256]{2,1,0:T(8,128)S(1)}, u32[]{:S(2)}, u32[]{:S(2)}) collective-permute-start(f32[3,32,256]{2,1,0:T(8,128)S(1)} %fusion.12), channel_id=1, source_target_pairs={{32,0},{33,1},{34,2},{35,3},{12,4},{13,5},{14,6},{15,7},{40,8},{41... | collective-permute-start | bytes 294920 | tf_op jit(solution)/shard_map/ppermute | solution.py:343
  145.0 5.1 %collective-permute-start.30 = (f32[3,32,256]{2,1,0:T(8,128)S(1)}, f32[3,32,256]{2,1,0:T(8,128)S(1)}, u32[]{:S(2)}, u32[]{:S(2)}) collective-permute-start(f32[3,32,256]{2,1,0:T(8,128)S(1)} %add_add_fusion.1), channel_id=1, source_target_pairs={{2,0},{3,1},{0,2},{1,3},{6,4},{7,5},{4,6},{5,7},{10,8},{11,9},{8,1... | collective-permute-start | bytes 294920 | tf_op jit(solution)/shard_map/ppermute | solution.py:343
  148.6 5.7 %collective-permute-start.32 = (f32[3,32,256]{2,1,0:T(8,128)S(1)}, f32[3,32,256]{2,1,0:T(8,128)S(1)}, u32[]{:S(2)}, u32[]{:S(2)}) collective-permute-start(f32[3,32,256]{2,1,0:T(8,128)S(1)} %add_add_fusion.1), channel_id=1, source_target_pairs={{3,0},{0,1},{1,2},{2,3},{7,4},{4,5},{5,6},{6,7},{11,8},{8,9},{9,10... | collective-permute-start | bytes 294920 | tf_op jit(solution)/shard_map/ppermute | solution.py:343
  155.6 5.1 %collective-permute-start.34 = (f32[3,32,256]{2,1,0:T(8,128)S(1)}, f32[3,32,256]{2,1,0:T(8,128)S(1)}, u32[]{:S(2)}, u32[]{:S(2)}) collective-permute-start(f32[3,32,256]{2,1,0:T(8,128)S(1)} %add_add_fusion.refs_4_), channel_id=1, source_target_pairs={{16,0},{17,1},{18,2},{19,3},{68,4},{69,5},{70,6},{71,7},{24,8},{25... | collective-permute-start | bytes 294920 | tf_op jit(solution)/shard_map/ppermute | solution.py:343
  155.9 5.7 %collective-permute-start.35 = (f32[3,32,256]{2,1,0:T(8,128)S(1)}, f32[3,32,256]{2,1,0:T(8,128)S(1)}, u32[]{:S(2)}, u32[]{:S(2)}) collective-permute-start(f32[3,32,256]{2,1,0:T(8,128)S(1)} %add_add_fusion.refs_4_), channel_id=1, source_target_pairs={{24,0},{25,1},{26,2},{27,3},{100,4},{101,5},{102,6},{103,7},{0,8},... | collective-permute-start | bytes 294920 | tf_op jit(solution)/shard_map/ppermute | solution.py:343
  161.6 21.2 %collective-permute-start.36 = (f32[4,3,32,256]{3,2,1,0:T(8,128)S(1)}, f32[4,3,32,256]{3,2,1,0:T(8,128)S(1)}, u32[]{:S(2)}, u32[]{:S(2)}) collective-permute-start(f32[4,3,32,256]{3,2,1,0:T(8,128)S(1)} %pad_maximum_fusion.2), channel_id=1, source_target_pairs={{4,0},{5,1},{6,2},{7,3},{0,4},{1,5},{2,6},{3,7},{12,8},{13,9},{14,... | collective-permute-start | bytes 1179656 | tf_op jit(solution)/shard_map/ppermute | solution.py:343
  167.5 7.8 %collective-permute-start.20 = (f32[256,256]{1,0:T(8,128)S(1)}, f32[256,256]{1,0:T(8,128)S(1)}, u32[]{:S(2)}, u32[]{:S(2)}) collective-permute-start(f32[256,256]{1,0:T(8,128)S(1)} %get-tuple-element.29.refs_0_), channel_id=1, source_target_pairs={{1,0},{2,1},{3,2},{0,3},{5,4},{6,5},{7,6},{4,7},{9,8},{10,9},{11,1... | collective-permute-start | bytes 786440 | tf_op jit(solution)/shard_map/ppermute | solution.py:343
  167.5 9.2 %collective-permute-start.21 = (f32[256,256]{1,0:T(8,128)S(1)}, f32[256,256]{1,0:T(8,128)S(1)}, u32[]{:S(2)}, u32[]{:S(2)}) collective-permute-start(f32[256,256]{1,0:T(8,128)S(1)} %get-tuple-element.29.refs_0_), channel_id=1, source_target_pairs={{2,0},{3,1},{0,2},{1,3},{6,4},{7,5},{4,6},{5,7},{10,8},{11,9},{8,1... | collective-permute-start | bytes 786440 | tf_op jit(solution)/shard_map/ppermute | solution.py:343
  167.8 15.1 %collective-permute-start.22 = (f32[256,256]{1,0:T(8,128)S(1)}, f32[256,256]{1,0:T(8,128)S(1)}, u32[]{:S(2)}, u32[]{:S(2)}) collective-permute-start(f32[256,256]{1,0:T(8,128)S(1)} %get-tuple-element.29.refs_0_), channel_id=1, source_target_pairs={{3,0},{0,1},{1,2},{2,3},{7,4},{4,5},{5,6},{6,7},{11,8},{8,9},{9,10... | collective-permute-start | bytes 786440 | tf_op jit(solution)/shard_map/ppermute | solution.py:343
  (7 other events, 47.6 us)

commit v3 on v2

--- a/solution.py
+++ b/solution.py
@@ -1,3 +1,4 @@
+import functools
 import math
 
 import jax
@@ -101,49 +102,100 @@
     return ((n + GRAN - 1) // GRAN) * GRAN
 
 
-def sketch_kernel(t0, t1, t2, t3, s0, s1, y0, y1, y2, y3, z0, z1, psic, tpos, omc, spos, srow,
-                  bcx, bcy, bcz, yc, zc, tile0, tile1, cntv, cnts, sem):
-    tin, sin = (t0, t1, t2, t3), (s0, s1)
-    youts, zouts = (y0, y1, y2, y3), (z0, z1)
-    for k in range(NT):
-        cntv[k:k + 1, :] = join(tin[k // ZN], k % ZN, TQ)[3:4, 0:128].astype(jnp.int32)
+TROWS = 2 * TC
+SROWS = NS * SCAP + 2 * SC
+
+
+def spread_counts(cntv, cnts, sem):
+    copy = pltpu.make_async_copy(cntv, cnts, sem)
+    copy.start()
+    copy.wait()
+
+
+def offsets(cnts, first, number):
+    off = [jnp.int32(0)]
+    for k in range(number):
+        off.append(off[k] + ceil16(cnts[first + k, 0]))
+    return [pl.multiple_of(v, GRAN) for v in off]
+
+
+def sources_kernel(s0, s1, omc, srow, scnt, spos, cnts, sem):
+    sin = (s0, s1)
     for k in range(NS):
         both = [join(sin[k // YN], k % YN, SCAP + 32 * h)[3:4, 0:128] for h in range(SCAP // R)]
-        cntv[NT + k:NT + k + 1, :] = sum(both).astype(jnp.int32)
-    fetch_counts = pltpu.make_async_copy(cntv, cnts, sem)
-    fetch_counts.start()
-    fetch_counts.wait()
-    toff = [jnp.int32(0)]
-    for k in range(NT):
-        ref, d = tin[k // ZN], k % ZN
-        off = pl.multiple_of(toff[k], GRAN)
-        psic[pl.ds(off, TQ), :] = ref[d, 0:TQ, :]
-        tpos[pl.ds(off, TQ), :] = join(ref, d, TQ).T
-        toff.append(toff[k] + ceil16(cnts[k, 0]))
-    tend = pl.multiple_of(toff[NT], GRAN)
-    psic[pl.ds(tend, 2 * TC), :] = jnp.zeros((2 * TC, R), BF16)
-    tpos[pl.ds(tend, 2 * TC), :] = jnp.zeros((2 * TC, 8), F32)
-    soff = [jnp.int32(0)]
+        scnt[k:k + 1, :] = sum(both).astype(jnp.int32)
+    spread_counts(scnt, cnts, sem)
+    soff = offsets(cnts, 0, NS)
     for k in range(NS):
         ref, d = sin[k // YN], k % YN
-        off = pl.multiple_of(soff[k], GRAN)
-        omc[pl.ds(off, SCAP), :] = ref[d, 0:SCAP, :]
+        omc[pl.ds(soff[k], SCAP), :] = ref[d, 0:SCAP, :]
         for h in range(SCAP // R):
-            spos[pl.ds(off + h * R, R), :] = join(ref, d, SCAP + 32 * h).T
-        soff.append(soff[k] + ceil16(cnts[NT + k, 0]))
-    send = pl.multiple_of(soff[NS], GRAN)
-    omc[pl.ds(send, SC), :] = jnp.zeros((SC, R), BF16)
-    spos[pl.ds(send, SC), :] = jnp.full((SC, 8), FAR, F32)
-    nt = (toff[NT] + TC - 1) // TC
+            spos[pl.ds(soff[k] + h * R, R), :] = join(ref, d, SCAP + 32 * h).T
+    omc[pl.ds(soff[NS], SC), :] = jnp.zeros((SC, R), BF16)
+    spos[pl.ds(soff[NS], SC), :] = jnp.full((SC, 8), FAR, F32)
+
+    def prepare(si, carry):
+        srow[si] = spos[pl.ds(pl.multiple_of(si * SC, SC), SC), :].T
+        return carry
+
+    lax.fori_loop(0, (soff[NS] + SC - 1) // SC, prepare, 0)
+
+
+def sources(sin):
+    vm = pl.BlockSpec(memory_space=pltpu.VMEM)
+    return pl.pallas_call(
+        sources_kernel,
+        out_shape=(
+            jax.ShapeDtypeStruct((SROWS, R), BF16),
+            jax.ShapeDtypeStruct((SROWS // SC, 8, SC), F32),
+            jax.ShapeDtypeStruct((NS, 128), jnp.int32),
+        ),
+        in_specs=[vm] * 2,
+        out_specs=(vm,) * 3,
+        scratch_shapes=[
+            pltpu.VMEM((SROWS, 8), F32),
+            pltpu.SMEM((NS, 128), jnp.int32),
+            pltpu.SemaphoreType.DMA(()),
+        ],
+        compiler_params=pltpu.CompilerParams(vmem_limit_bytes=5 << 20),
+    )(*inside(*sin))
+
+
+def sketch_kernel(m, last, *refs):
+    groups = m * ZN
+    tin, refs = refs[:m], refs[m:]
+    omc, srow, scnt = refs[:3]
+    refs = refs[3:]
+    if last:
+        earlier, refs = refs[:2], refs[2:]
+    youts, refs = refs[:m], refs[m:]
+    if last:
+        zouts, refs = refs[:2], refs[2:]
+        (psic, tpos, bcx, bcy, bcz, yc, tile0, tile1, cntv, cnts, sem, zc) = refs
+    else:
+        zc = refs[0]
+        (psic, tpos, bcx, bcy, bcz, yc, tile0, tile1, cntv, cnts, sem) = refs[1:]
+    cntv[0:NS, :] = scnt[...]
+    for k in range(groups):
+        count = join(tin[k // ZN], k % ZN, TQ)[3:4, 0:128]
+        cntv[NS + k:NS + k + 1, :] = count.astype(jnp.int32)
+    spread_counts(cntv, cnts, sem)
+    soff = offsets(cnts, 0, NS)
+    toff = offsets(cnts, NS, groups)
+    for k in range(groups):
+        ref, d = tin[k // ZN], k % ZN
+        psic[pl.ds(toff[k], TQ), :] = ref[d, 0:TQ, :]
+        tpos[pl.ds(toff[k], TQ), :] = join(ref, d, TQ).T
+    psic[pl.ds(toff[groups], 2 * TC), :] = jnp.zeros((2 * TC, R), BF16)
+    tpos[pl.ds(toff[groups], 2 * TC), :] = jnp.zeros((2 * TC, 8), F32)
+    nt = (toff[groups] + TC - 1) // TC
     ns = (soff[NS] + SC - 1) // SC
 
-    def prepare(si, carry):
-        at = pl.multiple_of(si * SC, SC)
-        srow[si] = spos[pl.ds(at, SC), :].T
-        zc[pl.ds(at, SC), :] = jnp.zeros((SC, R), F32)
+    def clear(si, carry):
+        zc[pl.ds(pl.multiple_of(si * SC, SC), SC), :] = jnp.zeros((SC, R), F32)
         return carry
 
-    lax.fori_loop(0, ns, prepare, 0)
+    lax.fori_loop(0, ns, clear, 0)
 
     def columns(ti, carry):
         ta = pl.multiple_of(ti * TC, TC)
@@ -194,45 +246,47 @@
         return third
 
     lax.fori_loop(0, (nt * ns + 1) // 2, two_steps, start)
-    for k in range(NT):
-        off = pl.multiple_of(toff[k], GRAN)
-        youts[k // ZN][k % ZN] = yc[pl.ds(off, TQ), :]
-    for k in range(NS):
-        off = pl.multiple_of(soff[k], GRAN)
-        zouts[k // YN][k % YN] = zc[pl.ds(off, SCAP), :]
-
-
-def sketch(tin, sin):
+    for k in range(groups):
+        youts[k // ZN][k % ZN] = yc[pl.ds(toff[k], TQ), :]
+    if last:
+        for k in range(NS):
+            rows = pl.ds(soff[k], SCAP)
+            total = zc[rows, :] + (earlier[0][rows, :] + earlier[1][rows, :])
+            zouts[k // YN][k % YN] = total
+
+
+def sketch(tin, src, earlier=None):
+    m = len(tin)
+    last = earlier is not None
     vm = pl.BlockSpec(memory_space=pltpu.VMEM)
-    trows = NT * TQ + 2 * TC
-    srows = NS * SCAP + 2 * SC
+    trows = m * ZN * TQ + TROWS
+    ypart = jax.ShapeDtypeStruct((ZN, TQ, R), F32)
+    zhalf = jax.ShapeDtypeStruct((YN, SCAP, R), F32)
+    zall = (SROWS, R)
+    outs = [ypart] * m + ([zhalf] * CN if last else [jax.ShapeDtypeStruct(zall, F32)])
+    operands = [*tin, *src, *(earlier or ())]
+    column = pltpu.VMEM((trows // TC, TC, 128), F32)
+    scratch = [
+        pltpu.VMEM((trows, R), BF16),
+        pltpu.VMEM((trows, 8), F32),
+        column,
+        column,
+        column,
+        pltpu.VMEM((trows, R), F32),
+        pltpu.VMEM((TC, SC), BF16),
+        pltpu.VMEM((TC, SC), BF16),
+        pltpu.VMEM((NS + m * ZN + 8 - m * ZN % 8, 128), jnp.int32),
+        pltpu.SMEM((NS + m * ZN + 8 - m * ZN % 8, 128), jnp.int32),
+        pltpu.SemaphoreType.DMA(()),
+    ]
     return pl.pallas_call(
-        sketch_kernel,
-        out_shape=(
-            *[jax.ShapeDtypeStruct((ZN, TQ, R), F32)] * XN,
-            *[jax.ShapeDtypeStruct((YN, SCAP, R), F32)] * CN,
-        ),
-        in_specs=[vm] * 6,
-        out_specs=(vm,) * 6,
-        scratch_shapes=[
-            pltpu.VMEM((trows, R), BF16),
-            pltpu.VMEM((trows, 8), F32),
-            pltpu.VMEM((srows, R), BF16),
-            pltpu.VMEM((srows, 8), F32),
-            pltpu.VMEM((srows // SC, 8, SC), F32),
-            pltpu.VMEM((trows // TC, TC, 128), F32),
-            pltpu.VMEM((trows // TC, TC, 128), F32),
-            pltpu.VMEM((trows // TC, TC, 128), F32),
-            pltpu.VMEM((trows, R), F32),
-            pltpu.VMEM((srows, R), F32),
-            pltpu.VMEM((TC, SC), BF16),
-            pltpu.VMEM((TC, SC), BF16),
-            pltpu.VMEM((NT + NS, 128), jnp.int32),
-            pltpu.SMEM((NT + NS, 128), jnp.int32),
-            pltpu.SemaphoreType.DMA(()),
-        ],
-        compiler_params=pltpu.CompilerParams(vmem_limit_bytes=34 << 20),
-    )(*inside(*tin, *sin))
+        functools.partial(sketch_kernel, m, last),
+        out_shape=tuple(outs),
+        in_specs=[vm] * len(operands),
+        out_specs=(vm,) * len(outs),
+        scratch_shapes=scratch + ([pltpu.VMEM(zall, F32)] if last else []),
+        compiler_params=pltpu.CompilerParams(vmem_limit_bytes=(8 + 5 * m + 6 * last) << 20),
+    )(*inside(*operands))
 
 
 def finish_kernel(where_ref, y0, y1, y2, y3, z0, z1, z2, z3, tpay,
@@ -369,13 +423,20 @@
     tpay, spay = pack(where, target_xyz, source_xyz, psi, omega)
     trow = ring(tpay, FIRST)
     srow = ring(spay, SAME["y"])
-    tin = ring(jnp.stack(trow), LAST)
+    column = jnp.stack(trow)
+    tin = [column]
+    for d in (1, 2, 3):
+        tin.append(fetch(column, LAST, d))
     srep = jnp.stack(srow)
     sfar = fetch(srep, SAME["c"], 1)
-    parts = sketch(tin, [srep, sfar])
-    ys, (z0, z1) = parts[0:4], parts[4:6]
+    src = sources([srep, sfar])
+    y0, za = sketch(tin[0:1], src)
+    y1, y2, zb = sketch(tin[1:3], src)
+    y3, z0, z1 = sketch(tin[3:4], src, (za, zb))
+    ys = [y0, y1, y2, y3]
     zfar = give(z1, SAME["c"], 1)
-    ys = returned(ys, LAST)
+    ys[1:3] = [give(ys[d], LAST, d) for d in (1, 2)]
+    ys[3] = give(ys[3], LAST, 3)
     zmine = [z0[d] + zfar[d] for d in range(YN)]
     zs = returned(zmine, SAME["y"])
     ys = [(ys[0][d] + ys[1][d]) + (ys[2][d] + ys[3][d]) for d in range(ZN)]

time: 185 us -> 182 us (0.984)
  waiting for transfers between devices: 112 us -> 96.1 us
  starting transfers between devices: 47.9 us -> 55 us
  Pallas kernels: 20.2 us -> 26 us
    ppermute x24, waiting for transfers between devices: 63.8 us -> 52.8 us  [fetch(): return lax.ppermute(v, ALL, [(b, a) for a, b in shifted(axes, d)])]
    pallas_call x1 -> x4, Pallas kernels: 14.1 us -> 19.8 us  [the longest x3 18.1 us: sketch(): pl.pallas_call(functools.partial(sketch_kernel, m, last), out_shape=tuple...]
    ppermute x13, starting transfers between devices: 15.4 us -> 20.5 us  [give(): return lax.ppermute(v, ALL, shifted(axes, d))]
    ppermute x13, waiting for transfers between devices: 48 us -> 43.3 us  [give(): return lax.ppermute(v, ALL, shifted(axes, d))]
    ppermute x24, starting transfers between devices: 32.6 us -> 34.5 us  [fetch(): return lax.ppermute(v, ALL, [(b, a) for a, b in shifted(axes, d)])]
  transfers between devices with their start and end apart: 37 -> 37, of which waited for: 31 -> 27; matrix products, arithmetic and copies ran while one was open for 0% -> 0% of each run, Pallas kernels for 0% -> 8%
where the time goes in v3:
time: 182 us
  waiting for transfers between devices  96.1 us (53%)
  starting transfers between devices  55 us (30%)
  Pallas kernels  26 us (14%)
  between operations  2.05 us (1%)
  other arithmetic  1.93 us (1%)
    ppermute x24, waiting for transfers between devices, fetch(): return lax.ppermute(v, ALL, [(b, a) for a, b in shifted(axes, d)])  52.8 us
    ppermute x13, waiting for transfers between devices, give(): return lax.ppermute(v, ALL, shifted(axes, d))  43.3 us
    ppermute x24, starting transfers between devices, fetch(): return lax.ppermute(v, ALL, [(b, a) for a, b in shifted(axes, d)])  34.5 us
    ppermute x13, starting transfers between devices, give(): return lax.ppermute(v, ALL, shifted(axes, d))  20.5 us
    pallas_call x3, Pallas kernels, sketch(): pl.pallas_call(functools.partial(sketch_kernel, m, last), out_shape=tuple...  18.1 us
  transfers between devices with their start and end apart: 37, of which 27 were waited for; matrix products, arithmetic and copies ran while one was open for 0% of the time, Pallas kernels for 8%

profile of v3, /device:TPU:1, one launch (start us, length us, event | category | flops | bytes accessed | tf_op | source)
XLA Modules:
  0.0 181.7 jit_solution(12940091368823328509)
XLA Ops:
  2.5 2.2 %shard_map.101 = (bf16[288,256]{1,0:T(8,128)(2,1)}, bf16[576,256]{1,0:T(8,128)(2,1)}) custom-call(s32[6]{0:T(128)} %stack.64.where_ref.refs_0_, f32[3,1024]{1,0:T(4,128)} %txyz_ref.1, f32[3,512]{1,0:T(4,128)} %sxyz_ref.1, bf16[1024,256]{1,0:T(8,128)(2,1)} %psi_ref.1, bf16[512,256]{1,0:T(8,128)(2,1)} %omega_ref.1), custom_call_target="tpu_custom_call" | custom-call | tf_op jit(solution)/shard_map/pallas_call | solution.py:82
  4.7 3.7 %collective-permute-start.4 = (bf16[576,256]{1,0:T(8,128)(2,1)}, bf16[576,256]{1,0:T(8,128)(2,1)S(1)}, u32[]{:S(2)}, u32[]{:S(2)}) collective-permute-start(bf16[576,256]{1,0:T(8,128)(2,1)} %get-tuple-element.27), channel_id=1, source_target_pairs={{2,0},{3,1},{0,2},{1,3},{6,4},{7,5},{4,6},{5,7},{10,8},{11,9},{8,1... | collective-permute-start | bytes 884744 | tf_op jit(solution)/shard_map/ppermute | solution.py:397
  8.9 2.3 %collective-permute-start.3 = (bf16[576,256]{1,0:T(8,128)(2,1)}, bf16[576,256]{1,0:T(8,128)(2,1)S(1)}, u32[]{:S(2)}, u32[]{:S(2)}) collective-permute-start(bf16[576,256]{1,0:T(8,128)(2,1)} %get-tuple-element.27), channel_id=1, source_target_pairs={{1,0},{2,1},{3,2},{0,3},{5,4},{6,5},{7,6},{4,7},{9,8},{10,9},{11,1... | collective-permute-start | bytes 884744 | tf_op jit(solution)/shard_map/ppermute | solution.py:397
  11.1 4.1 %collective-permute-done.4 = bf16[576,256]{1,0:T(8,128)(2,1)S(1)} collective-permute-done((bf16[576,256]{1,0:T(8,128)(2,1)}, bf16[576,256]{1,0:T(8,128)(2,1)S(1)}, u32[]{:S(2)}, u32[]{:S(2)}) %collective-permute-start.4) | collective-permute-done | bytes 294944 | tf_op jit(solution)/shard_map/ppermute | solution.py:397
  15.2 7.3 %collective-permute-done.5 = bf16[576,256]{1,0:T(8,128)(2,1)S(1)} collective-permute-done((bf16[576,256]{1,0:T(8,128)(2,1)}, bf16[576,256]{1,0:T(8,128)(2,1)S(1)}, u32[]{:S(2)}, u32[]{:S(2)}) %collective-permute-start.5) | collective-permute-done | bytes 294944 | tf_op jit(solution)/shard_map/ppermute | solution.py:397
  24.6 3.8 %collective-permute-start = (bf16[288,256]{1,0:T(8,128)(2,1)S(1)}, bf16[288,256]{1,0:T(8,128)(2,1)S(1)}, u32[]{:S(2)}, u32[]{:S(2)}) collective-permute-start(bf16[288,256]{1,0:T(8,128)(2,1)S(1)} %copy-done), channel_id=1, source_target_pairs={{8,0},{9,1},{10,2},{11,3},{36,4},{37,5},{38,6},{39,7},{16,8},{17,9... | collective-permute-start | bytes 442376 | tf_op jit(solution)/shard_map/ppermute | solution.py:397
  29.1 3.0 %collective-permute-done = bf16[288,256]{1,0:T(8,128)(2,1)S(1)} collective-permute-done((bf16[288,256]{1,0:T(8,128)(2,1)S(1)}, bf16[288,256]{1,0:T(8,128)(2,1)S(1)}, u32[]{:S(2)}, u32[]{:S(2)}) %collective-permute-start) | collective-permute-done | bytes 147488 | tf_op jit(solution)/shard_map/ppermute | solution.py:397
  32.0 1.9 %collective-permute-done.1 = bf16[288,256]{1,0:T(8,128)(2,1)S(1)} collective-permute-done((bf16[288,256]{1,0:T(8,128)(2,1)S(1)}, bf16[288,256]{1,0:T(8,128)(2,1)S(1)}, u32[]{:S(2)}, u32[]{:S(2)}) %collective-permute-start.1) | collective-permute-done | bytes 147488 | tf_op jit(solution)/shard_map/ppermute | solution.py:397
  35.4 2.4 %collective-permute-start.7 = (bf16[4,288,256]{2,1,0:T(8,128)(2,1)S(1)}, bf16[4,288,256]{2,1,0:T(8,128)(2,1)S(1)}, u32[]{:S(2)}, u32[]{:S(2)}) collective-permute-start(bf16[4,288,256]{2,1,0:T(8,128)(2,1)S(1)} %pad_maximum_fusion.1.refs_0_), channel_id=1, source_target_pairs={{32,0},{33,1},{34,2},{35,3},{12,4},{13,5},{14,6},{15,7},{40,8},{41... | collective-permute-start | bytes 1769480 | tf_op jit(solution)/shard_map/ppermute | solution.py:397
  40.7 4.6 %shard_map.103 = (f32[4,256,256]{2,1,0:T(8,128)S(1)}, f32[5120,256]{1,0:T(8,128)S(1)}) custom-call(bf16[4,288,256]{2,1,0:T(8,128)(2,1)S(1)} %pad_maximum_fusion.1.refs_0_, bf16[5120,256]{1,0:T(8,128)(2,1)S(1)} %get-tuple-element.28.refs_1_.refs_2_, f32[10,8,512]{2,1,0:T(8,128)S(1)} %get-tuple-element.29.refs_2_.refs_3_, ...), custom_call_target="tpu_custom_call" | custom-call | tf_op jit(solution)/shard_map/pallas_call | solution.py:282
  45.3 5.7 %collective-permute-done.7.refs_0_ = bf16[4,288,256]{2,1,0:T(8,128)(2,1)S(1)} collective-permute-done((bf16[4,288,256]{2,1,0:T(8,128)(2,1)S(1)}, bf16[4,288,256]{2,1,0:T(8,128)(2,1)S(1)}, u32[]{:S(2)}, u32[]{:S(2)}) %collective-permute-start.7) | collective-permute-done | bytes 589856 | tf_op jit(solution)/shard_map/ppermute | solution.py:397
  50.9 8.0 %shard_map.104 = (f32[4,256,256]{2,1,0:T(8,128)S(1)}, f32[4,256,256]{2,1,0:T(8,128)S(1)}, f32[5120,256]{1,0:T(8,128)S(1)}) custom-call(bf16[4,288,256]{2,1,0:T(8,128)(2,1)S(1)} %collective-permute-done.7.refs_0_, bf16[4,288,256]{2,1,0:T(8,128)(2,1)S(1)} %collective-permute-done.8.refs_1_, bf16[5120,256]{1,0:T(8,128)(2,1)S(1)} %get-tuple-element.28.refs_1_.refs_2_, ...), custom_call_target="tpu_custom_call" | custom-call | tf_op jit(solution)/shard_map/pallas_call | solution.py:282
  59.0 5.4 %shard_map.105 = (f32[4,256,256]{2,1,0:T(8,128)S(1)}, f32[4,512,256]{2,1,0:T(8,128)S(1)}, f32[4,512,256]{2,1,0:T(8,128)S(1)}) custom-call(bf16[4,288,256]{2,1,0:T(8,128)(2,1)S(1)} %collective-permute-done.11.refs_0_, bf16[5120,256]{1,0:T(8,128)(2,1)S(1)} %get-tuple-element.28.refs_1_.refs_2_, f32[10,8,512]{2,1,0:T(8,128)S(1)} %get-tuple-element.29.refs_2_.refs_3_, ...), custom_call_target="tpu_custom_call" | custom-call | tf_op jit(solution)/shard_map/pallas_call | solution.py:282
  65.9 2.4 %collective-permute-start.10 = (f32[4,256,256]{2,1,0:T(8,128)S(1)}, f32[4,256,256]{2,1,0:T(8,128)S(1)}, u32[]{:S(2)}, u32[]{:S(2)}) collective-permute-start(f32[4,256,256]{2,1,0:T(8,128)S(1)} %get-tuple-element.33), channel_id=1, source_target_pairs={{0,64},{1,65},{2,66},{3,67},{4,20},{5,21},{6,22},{7,23},{8,72},{9,... | collective-permute-start | bytes 3145736 | tf_op jit(solution)/shard_map/ppermute | solution.py:401
  68.3 11.3 %collective-permute-done.12 = f32[4,256,256]{2,1,0:T(8,128)S(1)} collective-permute-done((f32[4,256,256]{2,1,0:T(8,128)S(1)}, f32[4,256,256]{2,1,0:T(8,128)S(1)}, u32[]{:S(2)}, u32[]{:S(2)}) %collective-permute-start.12) | collective-permute-done | bytes 1048608 | tf_op jit(solution)/shard_map/ppermute | solution.py:401
  81.4 11.2 %collective-permute-done.9 = f32[4,256,256]{2,1,0:T(8,128)S(1)} collective-permute-done((f32[4,256,256]{2,1,0:T(8,128)S(1)}, f32[4,256,256]{2,1,0:T(8,128)S(1)}, u32[]{:S(2)}, u32[]{:S(2)}) %collective-permute-start.9) | collective-permute-done | bytes 1048608 | tf_op jit(solution)/shard_map/ppermute | solution.py:401
  95.6 2.5 %collective-permute-start.18 = (f32[512,256]{1,0:T(8,128)S(1)}, f32[512,256]{1,0:T(8,128)S(1)}, u32[]{:S(2)}, u32[]{:S(2)}) collective-permute-start(f32[512,256]{1,0:T(8,128)S(1)} %get-tuple-element.48), channel_id=1, source_target_pairs={{0,2},{1,3},{2,0},{3,1},{4,6},{5,7},{6,4},{7,5},{8,10},{9,11},{10,... | collective-permute-start | bytes 1572872 | tf_op jit(solution)/shard_map/ppermute | solution.py:401
  98.4 4.6 %collective-permute-start.14 = (f32[256,256]{1,0:T(8,128)S(1)}, f32[256,256]{1,0:T(8,128)S(1)}, u32[]{:S(2)}, u32[]{:S(2)}) collective-permute-start(f32[256,256]{1,0:T(8,128)S(1)} %get-tuple-element.52), channel_id=1, source_target_pairs={{0,16},{1,17},{2,18},{3,19},{4,68},{5,69},{6,70},{7,71},{8,24},{9,... | collective-permute-start | bytes 786440 | tf_op jit(solution)/shard_map/ppermute | solution.py:401
  103.0 3.8 %collective-permute-done.14.refs_3_ = f32[256,256]{1,0:T(8,128)S(1)} collective-permute-done((f32[256,256]{1,0:T(8,128)S(1)}, f32[256,256]{1,0:T(8,128)S(1)}, u32[]{:S(2)}, u32[]{:S(2)}) %collective-permute-start.14) | collective-permute-done | bytes 262176 | tf_op jit(solution)/shard_map/ppermute | solution.py:401
  106.8 2.6 %collective-permute-done.15.refs_4_ = f32[256,256]{1,0:T(8,128)S(1)} collective-permute-done((f32[256,256]{1,0:T(8,128)S(1)}, f32[256,256]{1,0:T(8,128)S(1)}, u32[]{:S(2)}, u32[]{:S(2)}) %collective-permute-start.15) | collective-permute-done | bytes 262176 | tf_op jit(solution)/shard_map/ppermute | solution.py:401
  109.4 7.6 %collective-permute-done.18.refs_7_ = f32[512,256]{1,0:T(8,128)S(1)} collective-permute-done((f32[512,256]{1,0:T(8,128)S(1)}, f32[512,256]{1,0:T(8,128)S(1)}, u32[]{:S(2)}, u32[]{:S(2)}) %collective-permute-start.18) | collective-permute-done | bytes 524320 | tf_op jit(solution)/shard_map/ppermute | solution.py:401
  117.0 3.5 %collective-permute-done.19.refs_8_ = f32[512,256]{1,0:T(8,128)S(1)} collective-permute-done((f32[512,256]{1,0:T(8,128)S(1)}, f32[512,256]{1,0:T(8,128)S(1)}, u32[]{:S(2)}, u32[]{:S(2)}) %collective-permute-start.19) | collective-permute-done | bytes 524320 | tf_op jit(solution)/shard_map/ppermute | solution.py:401
  120.4 2.0 %shard_map.106 = (f32[256,256]{1,0:T(8,128)S(1)}, f32[512,256]{1,0:T(8,128)}, f32[3,128,256]{2,1,0:T(8,128)S(1)}, f32[3,128,256]{2,1,0:T(8,128)S(1)}) custom-call(s32[6]{0:T(128)S(1)} %copy-done.1, f32[256,256]{1,0:T(8,128)S(1)} %get-tuple-element.54.refs_1_, f32[256,256]{1,0:T(8,128)S(1)} %collective-permute-done.13.refs_2_, ...), custom_call_target="tpu_custom_call" | custom-call | tf_op jit(solution)/shard_map/pallas_call | solution.py:328
  126.0 4.5 %collective-permute-start.25 = (f32[3,32,256]{2,1,0:T(8,128)S(1)}, f32[3,32,256]{2,1,0:T(8,128)S(1)}, u32[]{:S(2)}, u32[]{:S(2)}) collective-permute-start(f32[3,32,256]{2,1,0:T(8,128)S(1)} %get-tuple-element.56), channel_id=1, source_target_pairs={{0,16},{1,17},{2,18},{3,19},{4,68},{5,69},{6,70},{7,71},{8,24},{9,... | collective-permute-start | bytes 294920 | tf_op jit(solution)/shard_map/ppermute | solution.py:401
  130.5 2.0 %collective-permute-start.26 = (f32[3,32,256]{2,1,0:T(8,128)S(1)}, f32[3,32,256]{2,1,0:T(8,128)S(1)}, u32[]{:S(2)}, u32[]{:S(2)}) collective-permute-start(f32[3,32,256]{2,1,0:T(8,128)S(1)} %get-tuple-element.55), channel_id=1, source_target_pairs={{0,24},{1,25},{2,26},{3,27},{4,100},{5,101},{6,102},{7,103},{8,0},... | collective-permute-start | bytes 294920 | tf_op jit(solution)/shard_map/ppermute | solution.py:401
  136.1 3.1 %collective-permute-done.27 = f32[3,32,256]{2,1,0:T(8,128)S(1)} collective-permute-done((f32[3,32,256]{2,1,0:T(8,128)S(1)}, f32[3,32,256]{2,1,0:T(8,128)S(1)}, u32[]{:S(2)}, u32[]{:S(2)}) %collective-permute-start.27) | collective-permute-done | bytes 98336 | tf_op jit(solution)/shard_map/ppermute | solution.py:397
  146.9 2.2 %collective-permute-done.32 = f32[3,32,256]{2,1,0:T(8,128)S(1)} collective-permute-done((f32[3,32,256]{2,1,0:T(8,128)S(1)}, f32[3,32,256]{2,1,0:T(8,128)S(1)}, u32[]{:S(2)}, u32[]{:S(2)}) %collective-permute-start.32) | collective-permute-done | bytes 98336 | tf_op jit(solution)/shard_map/ppermute | solution.py:397
  149.1 3.0 %collective-permute-start.33 = (f32[3,32,256]{2,1,0:T(8,128)S(1)}, f32[3,32,256]{2,1,0:T(8,128)S(1)}, u32[]{:S(2)}, u32[]{:S(2)}) collective-permute-start(f32[3,32,256]{2,1,0:T(8,128)S(1)} %add_add_fusion.refs_4_), channel_id=1, source_target_pairs={{8,0},{9,1},{10,2},{11,3},{36,4},{37,5},{38,6},{39,7},{16,8},{17,9... | collective-permute-start | bytes 294920 | tf_op jit(solution)/shard_map/ppermute | solution.py:397
  153.8 3.4 %collective-permute-done.34.refs_6_ = f32[3,32,256]{2,1,0:T(8,128)S(1)} collective-permute-done((f32[3,32,256]{2,1,0:T(8,128)S(1)}, f32[3,32,256]{2,1,0:T(8,128)S(1)}, u32[]{:S(2)}, u32[]{:S(2)}) %collective-permute-start.34) | collective-permute-done | bytes 98336 | tf_op jit(solution)/shard_map/ppermute | solution.py:397
  158.2 6.3 %collective-permute-start.36 = (f32[4,3,32,256]{3,2,1,0:T(8,128)S(1)}, f32[4,3,32,256]{3,2,1,0:T(8,128)S(1)}, u32[]{:S(2)}, u32[]{:S(2)}) collective-permute-start(f32[4,3,32,256]{3,2,1,0:T(8,128)S(1)} %pad_maximum_fusion.2), channel_id=1, source_target_pairs={{4,0},{5,1},{6,2},{7,3},{0,4},{1,5},{2,6},{3,7},{12,8},{13,9},{14,... | collective-permute-start | bytes 1179656 | tf_op jit(solution)/shard_map/ppermute | solution.py:397
  165.9 6.3 %collective-permute-done.20.refs_1_ = f32[256,256]{1,0:T(8,128)S(1)} collective-permute-done((f32[256,256]{1,0:T(8,128)S(1)}, f32[256,256]{1,0:T(8,128)S(1)}, u32[]{:S(2)}, u32[]{:S(2)}) %collective-permute-start.20) | collective-permute-done | bytes 262176 | tf_op jit(solution)/shard_map/ppermute | solution.py:397
  173.7 6.1 %collective-permute-done.22.refs_3_ = f32[256,256]{1,0:T(8,128)S(1)} collective-permute-done((f32[256,256]{1,0:T(8,128)S(1)}, f32[256,256]{1,0:T(8,128)S(1)}, u32[]{:S(2)}, u32[]{:S(2)}) %collective-permute-start.22) | collective-permute-done | bytes 262176 | tf_op jit(solution)/shard_map/ppermute | solution.py:397
  (64 shorter events, 37.2 us)
Async XLA Ops:
  4.7 10.5 %collective-permute-start.4 = (bf16[576,256]{1,0:T(8,128)(2,1)}, bf16[576,256]{1,0:T(8,128)(2,1)S(1)}, u32[]{:S(2)}, u32[]{:S(2)}) collective-permute-start(bf16[576,256]{1,0:T(8,128)(2,1)} %get-tuple-element.27), channel_id=1, source_target_pairs={{2,0},{3,1},{0,2},{1,3},{6,4},{7,5},{4,6},{5,7},{10,8},{11,9},{8,1... | collective-permute-start | bytes 884744 | tf_op jit(solution)/shard_map/ppermute | solution.py:397
  8.5 14.0 %collective-permute-start.5 = (bf16[576,256]{1,0:T(8,128)(2,1)}, bf16[576,256]{1,0:T(8,128)(2,1)S(1)}, u32[]{:S(2)}, u32[]{:S(2)}) collective-permute-start(bf16[576,256]{1,0:T(8,128)(2,1)} %get-tuple-element.27), channel_id=1, source_target_pairs={{3,0},{0,1},{1,2},{2,3},{7,4},{4,5},{5,6},{6,7},{11,8},{8,9},{9,10... | collective-permute-start | bytes 884744 | tf_op jit(solution)/shard_map/ppermute | solution.py:397
  8.9 13.6 %collective-permute-start.3 = (bf16[576,256]{1,0:T(8,128)(2,1)}, bf16[576,256]{1,0:T(8,128)(2,1)S(1)}, u32[]{:S(2)}, u32[]{:S(2)}) collective-permute-start(bf16[576,256]{1,0:T(8,128)(2,1)} %get-tuple-element.27), channel_id=1, source_target_pairs={{1,0},{2,1},{3,2},{0,3},{5,4},{6,5},{7,6},{4,7},{9,8},{10,9},{11,1... | collective-permute-start | bytes 884744 | tf_op jit(solution)/shard_map/ppermute | solution.py:397
  23.6 15.3 %collective-permute-start.6 = (bf16[4,576,256]{2,1,0:T(8,128)(2,1)S(1)}, bf16[4,576,256]{2,1,0:T(8,128)(2,1)S(1)}, u32[]{:S(2)}, u32[]{:S(2)}) collective-permute-start(bf16[4,576,256]{2,1,0:T(8,128)(2,1)S(1)} %pad_maximum_fusion.s0), channel_id=1, source_target_pairs={{4,0},{5,1},{6,2},{7,3},{0,4},{1,5},{2,6},{3,7},{12,8},{13,9},{14,... | collective-permute-start | bytes 3538952 | tf_op jit(solution)/shard_map/ppermute | solution.py:397
  24.6 7.4 %collective-permute-start = (bf16[288,256]{1,0:T(8,128)(2,1)S(1)}, bf16[288,256]{1,0:T(8,128)(2,1)S(1)}, u32[]{:S(2)}, u32[]{:S(2)}) collective-permute-start(bf16[288,256]{1,0:T(8,128)(2,1)S(1)} %copy-done), channel_id=1, source_target_pairs={{8,0},{9,1},{10,2},{11,3},{36,4},{37,5},{38,6},{39,7},{16,8},{17,9... | collective-permute-start | bytes 442376 | tf_op jit(solution)/shard_map/ppermute | solution.py:397
  28.4 5.6 %collective-permute-start.1 = (bf16[288,256]{1,0:T(8,128)(2,1)S(1)}, bf16[288,256]{1,0:T(8,128)(2,1)S(1)}, u32[]{:S(2)}, u32[]{:S(2)}) collective-permute-start(bf16[288,256]{1,0:T(8,128)(2,1)S(1)} %copy-done), channel_id=1, source_target_pairs={{16,0},{17,1},{18,2},{19,3},{68,4},{69,5},{70,6},{71,7},{24,8},{25... | collective-permute-start | bytes 442376 | tf_op jit(solution)/shard_map/ppermute | solution.py:397
  28.4 6.9 %collective-permute-start.2 = (bf16[288,256]{1,0:T(8,128)(2,1)S(1)}, bf16[288,256]{1,0:T(8,128)(2,1)S(1)}, u32[]{:S(2)}, u32[]{:S(2)}) collective-permute-start(bf16[288,256]{1,0:T(8,128)(2,1)S(1)} %copy-done), channel_id=1, source_target_pairs={{24,0},{25,1},{26,2},{27,3},{100,4},{101,5},{102,6},{103,7},{0,8},... | collective-permute-start | bytes 442376 | tf_op jit(solution)/shard_map/ppermute | solution.py:397
  35.4 15.6 %collective-permute-start.7 = (bf16[4,288,256]{2,1,0:T(8,128)(2,1)S(1)}, bf16[4,288,256]{2,1,0:T(8,128)(2,1)S(1)}, u32[]{:S(2)}, u32[]{:S(2)}) collective-permute-start(bf16[4,288,256]{2,1,0:T(8,128)(2,1)S(1)} %pad_maximum_fusion.1.refs_0_), channel_id=1, source_target_pairs={{32,0},{33,1},{34,2},{35,3},{12,4},{13,5},{14,6},{15,7},{40,8},{41... | collective-permute-start | bytes 1769480 | tf_op jit(solution)/shard_map/ppermute | solution.py:397
  37.8 13.2 %collective-permute-start.8 = (bf16[4,288,256]{2,1,0:T(8,128)(2,1)S(1)}, bf16[4,288,256]{2,1,0:T(8,128)(2,1)S(1)}, u32[]{:S(2)}, u32[]{:S(2)}) collective-permute-start(bf16[4,288,256]{2,1,0:T(8,128)(2,1)S(1)} %pad_maximum_fusion.1.refs_0_), channel_id=1, source_target_pairs={{64,0},{65,1},{66,2},{67,3},{20,4},{21,5},{22,6},{23,7},{72,8},{73... | collective-permute-start | bytes 1769480 | tf_op jit(solution)/shard_map/ppermute | solution.py:397
  38.3 20.7 %collective-permute-start.11 = (bf16[4,288,256]{2,1,0:T(8,128)(2,1)S(1)}, bf16[4,288,256]{2,1,0:T(8,128)(2,1)S(1)}, u32[]{:S(2)}, u32[]{:S(2)}) collective-permute-start(bf16[4,288,256]{2,1,0:T(8,128)(2,1)S(1)} %pad_maximum_fusion.1.refs_0_), channel_id=1, source_target_pairs={{96,0},{97,1},{98,2},{99,3},{28,4},{29,5},{30,6},{31,7},{104,8},{1... | collective-permute-start | bytes 1769480 | tf_op jit(solution)/shard_map/ppermute | solution.py:397
  64.4 29.8 %collective-permute-start.16 = (f32[4,512,256]{2,1,0:T(8,128)S(1)}, f32[4,512,256]{2,1,0:T(8,128)S(1)}, u32[]{:S(2)}, u32[]{:S(2)}) collective-permute-start(f32[4,512,256]{2,1,0:T(8,128)S(1)} %get-tuple-element.38), channel_id=1, source_target_pairs={{0,4},{1,5},{2,6},{3,7},{4,0},{5,1},{6,2},{7,3},{8,12},{9,13},{10,... | collective-permute-start | bytes 6291464 | tf_op jit(solution)/shard_map/ppermute | solution.py:401
  65.6 13.9 %collective-permute-start.12 = (f32[4,256,256]{2,1,0:T(8,128)S(1)}, f32[4,256,256]{2,1,0:T(8,128)S(1)}, u32[]{:S(2)}, u32[]{:S(2)}) collective-permute-start(f32[4,256,256]{2,1,0:T(8,128)S(1)} %get-tuple-element.36), channel_id=1, source_target_pairs={{0,96},{1,97},{2,98},{3,99},{4,28},{5,29},{6,30},{7,31},{8,104},{9... | collective-permute-start | bytes 3145736 | tf_op jit(solution)/shard_map/ppermute | solution.py:401
  65.9 15.5 %collective-permute-start.10 = (f32[4,256,256]{2,1,0:T(8,128)S(1)}, f32[4,256,256]{2,1,0:T(8,128)S(1)}, u32[]{:S(2)}, u32[]{:S(2)}) collective-permute-start(f32[4,256,256]{2,1,0:T(8,128)S(1)} %get-tuple-element.33), channel_id=1, source_target_pairs={{0,64},{1,65},{2,66},{3,67},{4,20},{5,21},{6,22},{7,23},{8,72},{9,... | collective-permute-start | bytes 3145736 | tf_op jit(solution)/shard_map/ppermute | solution.py:401
  68.3 24.3 %collective-permute-start.9 = (f32[4,256,256]{2,1,0:T(8,128)S(1)}, f32[4,256,256]{2,1,0:T(8,128)S(1)}, u32[]{:S(2)}, u32[]{:S(2)}) collective-permute-start(f32[4,256,256]{2,1,0:T(8,128)S(1)} %get-tuple-element.32), channel_id=1, source_target_pairs={{0,32},{1,33},{2,34},{3,35},{4,12},{5,13},{6,14},{7,15},{8,40},{9,... | collective-permute-start | bytes 3145736 | tf_op jit(solution)/shard_map/ppermute | solution.py:401
  92.8 10.2 %collective-permute-start.13 = (f32[256,256]{1,0:T(8,128)S(1)}, f32[256,256]{1,0:T(8,128)S(1)}, u32[]{:S(2)}, u32[]{:S(2)}) collective-permute-start(f32[256,256]{1,0:T(8,128)S(1)} %get-tuple-element.53), channel_id=1, source_target_pairs={{0,8},{1,9},{2,10},{3,11},{4,36},{5,37},{6,38},{7,39},{8,16},{9,17... | collective-permute-start | bytes 786440 | tf_op jit(solution)/shard_map/ppermute | solution.py:401
  94.5 14.9 %collective-permute-start.17 = (f32[512,256]{1,0:T(8,128)S(1)}, f32[512,256]{1,0:T(8,128)S(1)}, u32[]{:S(2)}, u32[]{:S(2)}) collective-permute-start(f32[512,256]{1,0:T(8,128)S(1)} %get-tuple-element.49), channel_id=1, source_target_pairs={{0,1},{1,2},{2,3},{3,0},{4,5},{5,6},{6,7},{7,4},{8,9},{9,10},{10,1... | collective-permute-start | bytes 1572872 | tf_op jit(solution)/shard_map/ppermute | solution.py:401
  95.6 21.3 %collective-permute-start.18 = (f32[512,256]{1,0:T(8,128)S(1)}, f32[512,256]{1,0:T(8,128)S(1)}, u32[]{:S(2)}, u32[]{:S(2)}) collective-permute-start(f32[512,256]{1,0:T(8,128)S(1)} %get-tuple-element.48), channel_id=1, source_target_pairs={{0,2},{1,3},{2,0},{3,1},{4,6},{5,7},{6,4},{7,5},{8,10},{9,11},{10,... | collective-permute-start | bytes 1572872 | tf_op jit(solution)/shard_map/ppermute | solution.py:401
  98.1 22.3 %collective-permute-start.19 = (f32[512,256]{1,0:T(8,128)S(1)}, f32[512,256]{1,0:T(8,128)S(1)}, u32[]{:S(2)}, u32[]{:S(2)}) collective-permute-start(f32[512,256]{1,0:T(8,128)S(1)} %get-tuple-element.47), channel_id=1, source_target_pairs={{0,3},{1,0},{2,1},{3,2},{4,7},{5,4},{6,5},{7,6},{8,11},{9,8},{10,9... | collective-permute-start | bytes 1572872 | tf_op jit(solution)/shard_map/ppermute | solution.py:401
  98.4 8.4 %collective-permute-start.14 = (f32[256,256]{1,0:T(8,128)S(1)}, f32[256,256]{1,0:T(8,128)S(1)}, u32[]{:S(2)}, u32[]{:S(2)}) collective-permute-start(f32[256,256]{1,0:T(8,128)S(1)} %get-tuple-element.52), channel_id=1, source_target_pairs={{0,16},{1,17},{2,18},{3,19},{4,68},{5,69},{6,70},{7,71},{8,24},{9,... | collective-permute-start | bytes 786440 | tf_op jit(solution)/shard_map/ppermute | solution.py:401
  103.0 6.3 %collective-permute-start.15 = (f32[256,256]{1,0:T(8,128)S(1)}, f32[256,256]{1,0:T(8,128)S(1)}, u32[]{:S(2)}, u32[]{:S(2)}) collective-permute-start(f32[256,256]{1,0:T(8,128)S(1)} %get-tuple-element.51), channel_id=1, source_target_pairs={{0,24},{1,25},{2,26},{3,27},{4,100},{5,101},{6,102},{7,103},{8,0},... | collective-permute-start | bytes 786440 | tf_op jit(solution)/shard_map/ppermute | solution.py:401
  125.7 6.7 %collective-permute-start.24 = (f32[3,32,256]{2,1,0:T(8,128)S(1)}, f32[3,32,256]{2,1,0:T(8,128)S(1)}, u32[]{:S(2)}, u32[]{:S(2)}) collective-permute-start(f32[3,32,256]{2,1,0:T(8,128)S(1)} %get-tuple-element.57), channel_id=1, source_target_pairs={{0,8},{1,9},{2,10},{3,11},{4,36},{5,37},{6,38},{7,39},{8,16},{9,17... | collective-permute-start | bytes 294920 | tf_op jit(solution)/shard_map/ppermute | solution.py:401
  126.0 7.5 %collective-permute-start.25 = (f32[3,32,256]{2,1,0:T(8,128)S(1)}, f32[3,32,256]{2,1,0:T(8,128)S(1)}, u32[]{:S(2)}, u32[]{:S(2)}) collective-permute-start(f32[3,32,256]{2,1,0:T(8,128)S(1)} %get-tuple-element.56), channel_id=1, source_target_pairs={{0,16},{1,17},{2,18},{3,19},{4,68},{5,69},{6,70},{7,71},{8,24},{9,... | collective-permute-start | bytes 294920 | tf_op jit(solution)/shard_map/ppermute | solution.py:401
  134.1 5.1 %collective-permute-start.27 = (f32[3,32,256]{2,1,0:T(8,128)S(1)}, f32[3,32,256]{2,1,0:T(8,128)S(1)}, u32[]{:S(2)}, u32[]{:S(2)}) collective-permute-start(f32[3,32,256]{2,1,0:T(8,128)S(1)} %fusion.12), channel_id=1, source_target_pairs={{64,0},{65,1},{66,2},{67,3},{20,4},{21,5},{22,6},{23,7},{72,8},{73... | collective-permute-start | bytes 294920 | tf_op jit(solution)/shard_map/ppermute | solution.py:397
  136.1 5.0 %collective-permute-start.29 = (f32[3,32,256]{2,1,0:T(8,128)S(1)}, f32[3,32,256]{2,1,0:T(8,128)S(1)}, u32[]{:S(2)}, u32[]{:S(2)}) collective-permute-start(f32[3,32,256]{2,1,0:T(8,128)S(1)} %fusion.12), channel_id=1, source_target_pairs={{96,0},{97,1},{98,2},{99,3},{28,4},{29,5},{30,6},{31,7},{104,8},{1... | collective-permute-start | bytes 294920 | tf_op jit(solution)/shard_map/ppermute | solution.py:397
  141.1 5.1 %collective-permute-start.30 = (f32[3,32,256]{2,1,0:T(8,128)S(1)}, f32[3,32,256]{2,1,0:T(8,128)S(1)}, u32[]{:S(2)}, u32[]{:S(2)}) collective-permute-start(f32[3,32,256]{2,1,0:T(8,128)S(1)} %add_add_fusion.1), channel_id=1, source_target_pairs={{2,0},{3,1},{0,2},{1,3},{6,4},{7,5},{4,6},{5,7},{10,8},{11,9},{8,1... | collective-permute-start | bytes 294920 | tf_op jit(solution)/shard_map/ppermute | solution.py:397
  144.4 4.7 %collective-permute-start.32 = (f32[3,32,256]{2,1,0:T(8,128)S(1)}, f32[3,32,256]{2,1,0:T(8,128)S(1)}, u32[]{:S(2)}, u32[]{:S(2)}) collective-permute-start(f32[3,32,256]{2,1,0:T(8,128)S(1)} %add_add_fusion.1), channel_id=1, source_target_pairs={{3,0},{0,1},{1,2},{2,3},{7,4},{4,5},{5,6},{6,7},{11,8},{8,9},{9,10... | collective-permute-start | bytes 294920 | tf_op jit(solution)/shard_map/ppermute | solution.py:397
  152.1 5.1 %collective-permute-start.34 = (f32[3,32,256]{2,1,0:T(8,128)S(1)}, f32[3,32,256]{2,1,0:T(8,128)S(1)}, u32[]{:S(2)}, u32[]{:S(2)}) collective-permute-start(f32[3,32,256]{2,1,0:T(8,128)S(1)} %add_add_fusion.refs_4_), channel_id=1, source_target_pairs={{16,0},{17,1},{18,2},{19,3},{68,4},{69,5},{70,6},{71,7},{24,8},{25... | collective-permute-start | bytes 294920 | tf_op jit(solution)/shard_map/ppermute | solution.py:397
  152.6 5.5 %collective-permute-start.35 = (f32[3,32,256]{2,1,0:T(8,128)S(1)}, f32[3,32,256]{2,1,0:T(8,128)S(1)}, u32[]{:S(2)}, u32[]{:S(2)}) collective-permute-start(f32[3,32,256]{2,1,0:T(8,128)S(1)} %add_add_fusion.refs_4_), channel_id=1, source_target_pairs={{24,0},{25,1},{26,2},{27,3},{100,4},{101,5},{102,6},{103,7},{0,8},... | collective-permute-start | bytes 294920 | tf_op jit(solution)/shard_map/ppermute | solution.py:397
  158.2 21.6 %collective-permute-start.36 = (f32[4,3,32,256]{3,2,1,0:T(8,128)S(1)}, f32[4,3,32,256]{3,2,1,0:T(8,128)S(1)}, u32[]{:S(2)}, u32[]{:S(2)}) collective-permute-start(f32[4,3,32,256]{3,2,1,0:T(8,128)S(1)} %pad_maximum_fusion.2), channel_id=1, source_target_pairs={{4,0},{5,1},{6,2},{7,3},{0,4},{1,5},{2,6},{3,7},{12,8},{13,9},{14,... | collective-permute-start | bytes 1179656 | tf_op jit(solution)/shard_map/ppermute | solution.py:397
  164.4 7.8 %collective-permute-start.20 = (f32[256,256]{1,0:T(8,128)S(1)}, f32[256,256]{1,0:T(8,128)S(1)}, u32[]{:S(2)}, u32[]{:S(2)}) collective-permute-start(f32[256,256]{1,0:T(8,128)S(1)} %get-tuple-element.39.refs_0_), channel_id=1, source_target_pairs={{1,0},{2,1},{3,2},{0,3},{5,4},{6,5},{7,6},{4,7},{9,8},{10,9},{11,1... | collective-permute-start | bytes 786440 | tf_op jit(solution)/shard_map/ppermute | solution.py:397
  164.4 9.2 %collective-permute-start.21 = (f32[256,256]{1,0:T(8,128)S(1)}, f32[256,256]{1,0:T(8,128)S(1)}, u32[]{:S(2)}, u32[]{:S(2)}) collective-permute-start(f32[256,256]{1,0:T(8,128)S(1)} %get-tuple-element.39.refs_0_), channel_id=1, source_target_pairs={{2,0},{3,1},{0,2},{1,3},{6,4},{7,5},{4,6},{5,7},{10,8},{11,9},{8,1... | collective-permute-start | bytes 786440 | tf_op jit(solution)/shard_map/ppermute | solution.py:397
  164.7 15.1 %collective-permute-start.22 = (f32[256,256]{1,0:T(8,128)S(1)}, f32[256,256]{1,0:T(8,128)S(1)}, u32[]{:S(2)}, u32[]{:S(2)}) collective-permute-start(f32[256,256]{1,0:T(8,128)S(1)} %get-tuple-element.39.refs_0_), channel_id=1, source_target_pairs={{3,0},{0,1},{1,2},{2,3},{7,4},{4,5},{5,6},{6,7},{11,8},{8,9},{9,10... | collective-permute-start | bytes 786440 | tf_op jit(solution)/shard_map/ppermute | solution.py:397
  (7 other events, 48.4 us)

commit v4 on v3

--- a/solution.py
+++ b/solution.py
@@ -106,26 +106,27 @@
 SROWS = NS * SCAP + 2 * SC
 
 
-def spread_counts(cntv, cnts, sem):
-    copy = pltpu.make_async_copy(cntv, cnts, sem)
-    copy.start()
-    copy.wait()
-
-
-def offsets(cnts, first, number):
+def first_lane(row):
+    return jnp.max(row).astype(jnp.int32)
+
+
+def offsets(counts):
     off = [jnp.int32(0)]
-    for k in range(number):
-        off.append(off[k] + ceil16(cnts[first + k, 0]))
+    for n in counts:
+        off.append(off[-1] + ceil16(n))
     return [pl.multiple_of(v, GRAN) for v in off]
 
 
-def sources_kernel(s0, s1, omc, srow, scnt, spos, cnts, sem):
+def sources_kernel(s0, s1, omc, srow, scnt, spos):
     sin = (s0, s1)
+    counts = []
     for k in range(NS):
         both = [join(sin[k // YN], k % YN, SCAP + 32 * h)[3:4, 0:128] for h in range(SCAP // R)]
-        scnt[k:k + 1, :] = sum(both).astype(jnp.int32)
-    spread_counts(scnt, cnts, sem)
-    soff = offsets(cnts, 0, NS)
+        scnt[k:k + 1, :] = sum(both)
+        counts.append(first_lane(sum(both)))
+    soff = offsets(counts)
+    chunks = (soff[NS] + SC - 1) // SC
+    scnt[NS:NS + 1, :] = jnp.full((1, 128), chunks.astype(F32))
     for k in range(NS):
         ref, d = sin[k // YN], k % YN
         omc[pl.ds(soff[k], SCAP), :] = ref[d, 0:SCAP, :]
@@ -138,7 +139,7 @@
         srow[si] = spos[pl.ds(pl.multiple_of(si * SC, SC), SC), :].T
         return carry
 
-    lax.fori_loop(0, (soff[NS] + SC - 1) // SC, prepare, 0)
+    lax.fori_loop(0, chunks, prepare, 0)
 
 
 def sources(sin):
@@ -148,14 +149,12 @@
         out_shape=(
             jax.ShapeDtypeStruct((SROWS, R), BF16),
             jax.ShapeDtypeStruct((SROWS // SC, 8, SC), F32),
-            jax.ShapeDtypeStruct((NS, 128), jnp.int32),
+            jax.ShapeDtypeStruct((2 * NS, 128), F32),
         ),
         in_specs=[vm] * 2,
         out_specs=(vm,) * 3,
         scratch_shapes=[
             pltpu.VMEM((SROWS, 8), F32),
-            pltpu.SMEM((NS, 128), jnp.int32),
-            pltpu.SemaphoreType.DMA(()),
         ],
         compiler_params=pltpu.CompilerParams(vmem_limit_bytes=5 << 20),
     )(*inside(*sin))
@@ -167,21 +166,17 @@
     omc, srow, scnt = refs[:3]
     refs = refs[3:]
     if last:
-        earlier, refs = refs[:2], refs[2:]
+        earlier, refs = refs[:3], refs[3:]
     youts, refs = refs[:m], refs[m:]
     if last:
         zouts, refs = refs[:2], refs[2:]
-        (psic, tpos, bcx, bcy, bcz, yc, tile0, tile1, cntv, cnts, sem, zc) = refs
+        psic, tpos, bcx, bcy, bcz, yc, tile0, tile1, zc = refs
     else:
-        zc = refs[0]
-        (psic, tpos, bcx, bcy, bcz, yc, tile0, tile1, cntv, cnts, sem) = refs[1:]
-    cntv[0:NS, :] = scnt[...]
-    for k in range(groups):
-        count = join(tin[k // ZN], k % ZN, TQ)[3:4, 0:128]
-        cntv[NS + k:NS + k + 1, :] = count.astype(jnp.int32)
-    spread_counts(cntv, cnts, sem)
-    soff = offsets(cnts, 0, NS)
-    toff = offsets(cnts, NS, groups)
+        zc, psic, tpos, bcx, bcy, bcz, yc, tile0, tile1 = refs
+    ns = first_lane(scnt[NS:NS + 1, :])
+    toff = offsets(
+        [first_lane(join(tin[k // ZN], k % ZN, TQ)[3:4, 0:128]) for k in range(groups)]
+    )
     for k in range(groups):
         ref, d = tin[k // ZN], k % ZN
         psic[pl.ds(toff[k], TQ), :] = ref[d, 0:TQ, :]
@@ -189,7 +184,6 @@
     psic[pl.ds(toff[groups], 2 * TC), :] = jnp.zeros((2 * TC, R), BF16)
     tpos[pl.ds(toff[groups], 2 * TC), :] = jnp.zeros((2 * TC, 8), F32)
     nt = (toff[groups] + TC - 1) // TC
-    ns = (soff[NS] + SC - 1) // SC
 
     def clear(si, carry):
         zc[pl.ds(pl.multiple_of(si * SC, SC), SC), :] = jnp.zeros((SC, R), F32)
@@ -249,9 +243,11 @@
     for k in range(groups):
         youts[k // ZN][k % ZN] = yc[pl.ds(toff[k], TQ), :]
     if last:
+        soff = offsets([first_lane(scnt[k:k + 1, :]) for k in range(NS)])
         for k in range(NS):
             rows = pl.ds(soff[k], SCAP)
-            total = zc[rows, :] + (earlier[0][rows, :] + earlier[1][rows, :])
+            total = zc[rows, :] + earlier[2][rows, :]
+            total = total + (earlier[0][rows, :] + earlier[1][rows, :])
             zouts[k // YN][k % YN] = total
 
 
@@ -275,9 +271,6 @@
         pltpu.VMEM((trows, R), F32),
         pltpu.VMEM((TC, SC), BF16),
         pltpu.VMEM((TC, SC), BF16),
-        pltpu.VMEM((NS + m * ZN + 8 - m * ZN % 8, 128), jnp.int32),
-        pltpu.SMEM((NS + m * ZN + 8 - m * ZN % 8, 128), jnp.int32),
-        pltpu.SemaphoreType.DMA(()),
     ]
     return pl.pallas_call(
         functools.partial(sketch_kernel, m, last),
@@ -431,12 +424,14 @@
     sfar = fetch(srep, SAME["c"], 1)
     src = sources([srep, sfar])
     y0, za = sketch(tin[0:1], src)
-    y1, y2, zb = sketch(tin[1:3], src)
-    y3, z0, z1 = sketch(tin[3:4], src, (za, zb))
+    y1, zb = sketch(tin[1:2], src)
+    y3, zd = sketch(tin[3:4], src)
+    y2, z0, z1 = sketch(tin[2:3], src, (za, zb, zd))
     ys = [y0, y1, y2, y3]
     zfar = give(z1, SAME["c"], 1)
-    ys[1:3] = [give(ys[d], LAST, d) for d in (1, 2)]
+    ys[1] = give(ys[1], LAST, 1)
     ys[3] = give(ys[3], LAST, 3)
+    ys[2] = give(ys[2], LAST, 2)
     zmine = [z0[d] + zfar[d] for d in range(YN)]
     zs = returned(zmine, SAME["y"])
     ys = [(ys[0][d] + ys[1][d]) + (ys[2][d] + ys[3][d]) for d in range(ZN)]

time: 182 us -> 181 us (level)
  starting transfers between devices: 55 us -> 62.1 us
  waiting for transfers between devices: 96.1 us -> 89.6 us
    ppermute x24, waiting for transfers between devices: 52.8 us -> 45.6 us  [fetch(): return lax.ppermute(v, ALL, [(b, a) for a, b in shifted(axes, d)])]
    ppermute x13, starting transfers between devices: 20.5 us -> 24.9 us  [give(): return lax.ppermute(v, ALL, shifted(axes, d))]
    ppermute x24, starting transfers between devices: 34.5 us -> 37.1 us  [fetch(): return lax.ppermute(v, ALL, [(b, a) for a, b in shifted(axes, d)])]
    pallas_call x3 -> x4, Pallas kernels: 18.1 us -> 17.1 us  [sketch(): pl.pallas_call(functools.partial(sketch_kernel, m, last), out_shape=tuple...]
  transfers between devices with their start and end apart: 37 -> 37, of which waited for: 27 -> 26; matrix products, arithmetic and copies ran while one was open for 0% -> 0% of each run, Pallas kernels for 8% -> 7%
where the time goes in v4:
time: 181 us
  waiting for transfers between devices  89.6 us (50%)
  starting transfers between devices  62.1 us (34%)
  Pallas kernels  24.4 us (13%)
  between operations  2.06 us (1%)
  other arithmetic  1.89 us (1%)
    ppermute x24, waiting for transfers between devices, fetch(): return lax.ppermute(v, ALL, [(b, a) for a, b in shifted(axes, d)])  45.6 us
    ppermute x13, waiting for transfers between devices, give(): return lax.ppermute(v, ALL, shifted(axes, d))  44 us
    ppermute x24, starting transfers between devices, fetch(): return lax.ppermute(v, ALL, [(b, a) for a, b in shifted(axes, d)])  37.1 us
    ppermute x13, starting transfers between devices, give(): return lax.ppermute(v, ALL, shifted(axes, d))  24.9 us
    pallas_call x4, Pallas kernels, sketch(): pl.pallas_call(functools.partial(sketch_kernel, m, last), out_shape=tuple...  17.1 us
  transfers between devices with their start and end apart: 37, of which 26 were waited for; matrix products, arithmetic and copies ran while one was open for 0% of the time, Pallas kernels for 7%

profile of v4, /device:TPU:1, one launch (start us, length us, event | category | flops | bytes accessed | tf_op | source)
XLA Modules:
  0.0 180.7 jit_solution(7973777265836369069)
XLA Ops:
  2.5 2.2 %shard_map.101 = (bf16[288,256]{1,0:T(8,128)(2,1)}, bf16[576,256]{1,0:T(8,128)(2,1)}) custom-call(s32[6]{0:T(128)} %stack.64.where_ref.refs_0_, f32[3,1024]{1,0:T(4,128)} %txyz_ref.1, f32[3,512]{1,0:T(4,128)} %sxyz_ref.1, bf16[1024,256]{1,0:T(8,128)(2,1)} %psi_ref.1, bf16[512,256]{1,0:T(8,128)(2,1)} %omega_ref.1), custom_call_target="tpu_custom_call" | custom-call | tf_op jit(solution)/shard_map/pallas_call | solution.py:82
  4.7 2.1 %collective-permute-start.5 = (bf16[576,256]{1,0:T(8,128)(2,1)}, bf16[576,256]{1,0:T(8,128)(2,1)S(1)}, u32[]{:S(2)}, u32[]{:S(2)}) collective-permute-start(bf16[576,256]{1,0:T(8,128)(2,1)} %get-tuple-element.28), channel_id=1, source_target_pairs={{3,0},{0,1},{1,2},{2,3},{7,4},{4,5},{5,6},{6,7},{11,8},{8,9},{9,10... | collective-permute-start | bytes 884744 | tf_op jit(solution)/shard_map/ppermute | solution.py:390
  6.8 2.6 %collective-permute-start.4 = (bf16[576,256]{1,0:T(8,128)(2,1)}, bf16[576,256]{1,0:T(8,128)(2,1)S(1)}, u32[]{:S(2)}, u32[]{:S(2)}) collective-permute-start(bf16[576,256]{1,0:T(8,128)(2,1)} %get-tuple-element.28), channel_id=1, source_target_pairs={{2,0},{3,1},{0,2},{1,3},{6,4},{7,5},{4,6},{5,7},{10,8},{11,9},{8,1... | collective-permute-start | bytes 884744 | tf_op jit(solution)/shard_map/ppermute | solution.py:390
  10.5 4.6 %collective-permute-done.5 = bf16[576,256]{1,0:T(8,128)(2,1)S(1)} collective-permute-done((bf16[576,256]{1,0:T(8,128)(2,1)}, bf16[576,256]{1,0:T(8,128)(2,1)S(1)}, u32[]{:S(2)}, u32[]{:S(2)}) %collective-permute-start.5) | collective-permute-done | bytes 294944 | tf_op jit(solution)/shard_map/ppermute | solution.py:390
  15.1 7.3 %collective-permute-done.4 = bf16[576,256]{1,0:T(8,128)(2,1)S(1)} collective-permute-done((bf16[576,256]{1,0:T(8,128)(2,1)}, bf16[576,256]{1,0:T(8,128)(2,1)S(1)}, u32[]{:S(2)}, u32[]{:S(2)}) %collective-permute-start.4) | collective-permute-done | bytes 294944 | tf_op jit(solution)/shard_map/ppermute | solution.py:390
  26.8 3.3 %collective-permute-start.1 = (bf16[288,256]{1,0:T(8,128)(2,1)S(1)}, bf16[288,256]{1,0:T(8,128)(2,1)S(1)}, u32[]{:S(2)}, u32[]{:S(2)}) collective-permute-start(bf16[288,256]{1,0:T(8,128)(2,1)S(1)} %copy-done), channel_id=1, source_target_pairs={{16,0},{17,1},{18,2},{19,3},{68,4},{69,5},{70,6},{71,7},{24,8},{25... | collective-permute-start | bytes 442376 | tf_op jit(solution)/shard_map/ppermute | solution.py:390
  31.4 2.8 %collective-permute-done.1 = bf16[288,256]{1,0:T(8,128)(2,1)S(1)} collective-permute-done((bf16[288,256]{1,0:T(8,128)(2,1)S(1)}, bf16[288,256]{1,0:T(8,128)(2,1)S(1)}, u32[]{:S(2)}, u32[]{:S(2)}) %collective-permute-start.1) | collective-permute-done | bytes 147488 | tf_op jit(solution)/shard_map/ppermute | solution.py:390
  39.7 4.0 %shard_map.103 = (f32[4,256,256]{2,1,0:T(8,128)S(1)}, f32[5120,256]{1,0:T(8,128)S(1)}) custom-call(bf16[4,288,256]{2,1,0:T(8,128)(2,1)S(1)} %pad_maximum_fusion.1.refs_0_, bf16[5120,256]{1,0:T(8,128)(2,1)S(1)} %get-tuple-element.29.refs_1_, f32[10,8,512]{2,1,0:T(8,128)S(1)} %get-tuple-element.30.refs_2_, f32[16,128]{1,0:T(8,128)S(1)} %get-tuple-element.31.refs_3_), custom_call_target="tpu_custom_call" | custom-call | tf_op jit(solution)/shard_map/pallas_call | solution.py:275
  44.6 4.0 %shard_map.105 = (f32[4,256,256]{2,1,0:T(8,128)S(1)}, f32[5120,256]{1,0:T(8,128)S(1)}) custom-call(bf16[4,288,256]{2,1,0:T(8,128)(2,1)S(1)} %collective-permute-done.10.refs_0_, bf16[5120,256]{1,0:T(8,128)(2,1)S(1)} %get-tuple-element.29.refs_1_, f32[10,8,512]{2,1,0:T(8,128)S(1)} %get-tuple-element.30.refs_2_, f32[16,128]{1,0:T(8,128)S(1)} %get-tuple-element.31.refs_3_), custom_call_target="tpu_custom_call" | custom-call | tf_op jit(solution)/shard_map/pallas_call | solution.py:275
  48.6 4.0 %shard_map.104 = (f32[4,256,256]{2,1,0:T(8,128)S(1)}, f32[5120,256]{1,0:T(8,128)S(1)}) custom-call(bf16[4,288,256]{2,1,0:T(8,128)(2,1)S(1)} %collective-permute-done.7.refs_0_, bf16[5120,256]{1,0:T(8,128)(2,1)S(1)} %get-tuple-element.29.refs_1_, f32[10,8,512]{2,1,0:T(8,128)S(1)} %get-tuple-element.30.refs_2_, f32[16,128]{1,0:T(8,128)S(1)} %get-tuple-element.31.refs_3_), custom_call_target="tpu_custom_call" | custom-call | tf_op jit(solution)/shard_map/pallas_call | solution.py:275
  52.5 5.2 %shard_map.106 = (f32[4,256,256]{2,1,0:T(8,128)S(1)}, f32[4,512,256]{2,1,0:T(8,128)S(1)}, f32[4,512,256]{2,1,0:T(8,128)S(1)}) custom-call(bf16[4,288,256]{2,1,0:T(8,128)(2,1)S(1)} %collective-permute-done.9.refs_0_, bf16[5120,256]{1,0:T(8,128)(2,1)S(1)} %get-tuple-element.29.refs_1_, f32[10,8,512]{2,1,0:T(8,128)S(1)} %get-tuple-element.30.refs_2_, ...), custom_call_target="tpu_custom_call" | custom-call | tf_op jit(solution)/shard_map/pallas_call | solution.py:275
  57.8 4.1 %collective-permute-start.16 = (f32[4,512,256]{2,1,0:T(8,128)S(1)}, f32[4,512,256]{2,1,0:T(8,128)S(1)}, u32[]{:S(2)}, u32[]{:S(2)}) collective-permute-start(f32[4,512,256]{2,1,0:T(8,128)S(1)} %get-tuple-element.40), channel_id=1, source_target_pairs={{0,4},{1,5},{2,6},{3,7},{4,0},{5,1},{6,2},{7,3},{8,12},{9,13},{10,... | collective-permute-start | bytes 6291464 | tf_op jit(solution)/shard_map/ppermute | solution.py:394
  62.8 2.1 %collective-permute-start.11 = (f32[4,256,256]{2,1,0:T(8,128)S(1)}, f32[4,256,256]{2,1,0:T(8,128)S(1)}, u32[]{:S(2)}, u32[]{:S(2)}) collective-permute-start(f32[4,256,256]{2,1,0:T(8,128)S(1)} %get-tuple-element.37), channel_id=1, source_target_pairs={{0,64},{1,65},{2,66},{3,67},{4,20},{5,21},{6,22},{7,23},{8,72},{9,... | collective-permute-start | bytes 3145736 | tf_op jit(solution)/shard_map/ppermute | solution.py:394
  65.0 10.9 %collective-permute-done.12 = f32[4,256,256]{2,1,0:T(8,128)S(1)} collective-permute-done((f32[4,256,256]{2,1,0:T(8,128)S(1)}, f32[4,256,256]{2,1,0:T(8,128)S(1)}, u32[]{:S(2)}, u32[]{:S(2)}) %collective-permute-start.12) | collective-permute-done | bytes 1048608 | tf_op jit(solution)/shard_map/ppermute | solution.py:394
  75.8 2.5 %collective-permute-done.11 = f32[4,256,256]{2,1,0:T(8,128)S(1)} collective-permute-done((f32[4,256,256]{2,1,0:T(8,128)S(1)}, f32[4,256,256]{2,1,0:T(8,128)S(1)}, u32[]{:S(2)}, u32[]{:S(2)}) %collective-permute-start.11) | collective-permute-done | bytes 1048608 | tf_op jit(solution)/shard_map/ppermute | solution.py:394
  78.3 11.2 %collective-permute-done.8 = f32[4,256,256]{2,1,0:T(8,128)S(1)} collective-permute-done((f32[4,256,256]{2,1,0:T(8,128)S(1)}, f32[4,256,256]{2,1,0:T(8,128)S(1)}, u32[]{:S(2)}, u32[]{:S(2)}) %collective-permute-start.8) | collective-permute-done | bytes 1048608 | tf_op jit(solution)/shard_map/ppermute | solution.py:394
  89.8 4.6 %collective-permute-start.13 = (f32[256,256]{1,0:T(8,128)S(1)}, f32[256,256]{1,0:T(8,128)S(1)}, u32[]{:S(2)}, u32[]{:S(2)}) collective-permute-start(f32[256,256]{1,0:T(8,128)S(1)} %get-tuple-element.55), channel_id=1, source_target_pairs={{0,8},{1,9},{2,10},{3,11},{4,36},{5,37},{6,38},{7,39},{8,16},{9,17... | collective-permute-start | bytes 786440 | tf_op jit(solution)/shard_map/ppermute | solution.py:394
  95.7 2.1 %collective-permute-start.18 = (f32[512,256]{1,0:T(8,128)S(1)}, f32[512,256]{1,0:T(8,128)S(1)}, u32[]{:S(2)}, u32[]{:S(2)}) collective-permute-start(f32[512,256]{1,0:T(8,128)S(1)} %get-tuple-element.50), channel_id=1, source_target_pairs={{0,2},{1,3},{2,0},{3,1},{4,6},{5,7},{6,4},{7,5},{8,10},{9,11},{10,... | collective-permute-start | bytes 1572872 | tf_op jit(solution)/shard_map/ppermute | solution.py:394
  99.1 2.2 %collective-permute-start.14 = (f32[256,256]{1,0:T(8,128)S(1)}, f32[256,256]{1,0:T(8,128)S(1)}, u32[]{:S(2)}, u32[]{:S(2)}) collective-permute-start(f32[256,256]{1,0:T(8,128)S(1)} %get-tuple-element.54), channel_id=1, source_target_pairs={{0,16},{1,17},{2,18},{3,19},{4,68},{5,69},{6,70},{7,71},{8,24},{9,... | collective-permute-start | bytes 786440 | tf_op jit(solution)/shard_map/ppermute | solution.py:394
  101.4 2.0 %collective-permute-start.15 = (f32[256,256]{1,0:T(8,128)S(1)}, f32[256,256]{1,0:T(8,128)S(1)}, u32[]{:S(2)}, u32[]{:S(2)}) collective-permute-start(f32[256,256]{1,0:T(8,128)S(1)} %get-tuple-element.53), channel_id=1, source_target_pairs={{0,24},{1,25},{2,26},{3,27},{4,100},{5,101},{6,102},{7,103},{8,0},... | collective-permute-start | bytes 786440 | tf_op jit(solution)/shard_map/ppermute | solution.py:394
  103.4 2.7 %collective-permute-done.14.refs_3_ = f32[256,256]{1,0:T(8,128)S(1)} collective-permute-done((f32[256,256]{1,0:T(8,128)S(1)}, f32[256,256]{1,0:T(8,128)S(1)}, u32[]{:S(2)}, u32[]{:S(2)}) %collective-permute-start.14) | collective-permute-done | bytes 262176 | tf_op jit(solution)/shard_map/ppermute | solution.py:394
  108.9 11.6 %collective-permute-done.18.refs_7_ = f32[512,256]{1,0:T(8,128)S(1)} collective-permute-done((f32[512,256]{1,0:T(8,128)S(1)}, f32[512,256]{1,0:T(8,128)S(1)}, u32[]{:S(2)}, u32[]{:S(2)}) %collective-permute-start.18) | collective-permute-done | bytes 524320 | tf_op jit(solution)/shard_map/ppermute | solution.py:394
  120.6 2.0 %shard_map.107 = (f32[256,256]{1,0:T(8,128)S(1)}, f32[512,256]{1,0:T(8,128)}, f32[3,128,256]{2,1,0:T(8,128)S(1)}, f32[3,128,256]{2,1,0:T(8,128)S(1)}) custom-call(s32[6]{0:T(128)S(1)} %copy-done.1, f32[256,256]{1,0:T(8,128)S(1)} %get-tuple-element.56.refs_1_, f32[256,256]{1,0:T(8,128)S(1)} %collective-permute-done.13.refs_2_, ...), custom_call_target="tpu_custom_call" | custom-call | tf_op jit(solution)/shard_map/pallas_call | solution.py:321
  135.9 3.7 %collective-permute-done.29 = f32[3,32,256]{2,1,0:T(8,128)S(1)} collective-permute-done((f32[3,32,256]{2,1,0:T(8,128)S(1)}, f32[3,32,256]{2,1,0:T(8,128)S(1)}, u32[]{:S(2)}, u32[]{:S(2)}) %collective-permute-start.29) | collective-permute-done | bytes 98336 | tf_op jit(solution)/shard_map/ppermute | solution.py:390
  139.7 2.4 %collective-permute-start.31 = (f32[3,32,256]{2,1,0:T(8,128)S(1)}, f32[3,32,256]{2,1,0:T(8,128)S(1)}, u32[]{:S(2)}, u32[]{:S(2)}) collective-permute-start(f32[3,32,256]{2,1,0:T(8,128)S(1)} %add_add_fusion.1), channel_id=1, source_target_pairs={{1,0},{2,1},{3,2},{0,3},{5,4},{6,5},{7,6},{4,7},{9,8},{10,9},{11,1... | collective-permute-start | bytes 294920 | tf_op jit(solution)/shard_map/ppermute | solution.py:390
  143.7 4.1 %collective-permute-done.32 = f32[3,32,256]{2,1,0:T(8,128)S(1)} collective-permute-done((f32[3,32,256]{2,1,0:T(8,128)S(1)}, f32[3,32,256]{2,1,0:T(8,128)S(1)}, u32[]{:S(2)}, u32[]{:S(2)}) %collective-permute-start.32) | collective-permute-done | bytes 98336 | tf_op jit(solution)/shard_map/ppermute | solution.py:390
  147.8 2.6 %collective-permute-start.33 = (f32[3,32,256]{2,1,0:T(8,128)S(1)}, f32[3,32,256]{2,1,0:T(8,128)S(1)}, u32[]{:S(2)}, u32[]{:S(2)}) collective-permute-start(f32[3,32,256]{2,1,0:T(8,128)S(1)} %add_add_fusion.refs_4_), channel_id=1, source_target_pairs={{8,0},{9,1},{10,2},{11,3},{36,4},{37,5},{38,6},{39,7},{16,8},{17,9... | collective-permute-start | bytes 294920 | tf_op jit(solution)/shard_map/ppermute | solution.py:390
  153.1 2.5 %collective-permute-done.34.refs_6_ = f32[3,32,256]{2,1,0:T(8,128)S(1)} collective-permute-done((f32[3,32,256]{2,1,0:T(8,128)S(1)}, f32[3,32,256]{2,1,0:T(8,128)S(1)}, u32[]{:S(2)}, u32[]{:S(2)}) %collective-permute-start.34) | collective-permute-done | bytes 98336 | tf_op jit(solution)/shard_map/ppermute | solution.py:390
  156.2 5.5 %collective-permute-start.36 = (f32[4,3,32,256]{3,2,1,0:T(8,128)S(1)}, f32[4,3,32,256]{3,2,1,0:T(8,128)S(1)}, u32[]{:S(2)}, u32[]{:S(2)}) collective-permute-start(f32[4,3,32,256]{3,2,1,0:T(8,128)S(1)} %pad_maximum_fusion.2), channel_id=1, source_target_pairs={{4,0},{5,1},{6,2},{7,3},{0,4},{1,5},{2,6},{3,7},{12,8},{13,9},{14,... | collective-permute-start | bytes 1179656 | tf_op jit(solution)/shard_map/ppermute | solution.py:390
  161.8 2.2 %collective-permute-start.20 = (f32[256,256]{1,0:T(8,128)S(1)}, f32[256,256]{1,0:T(8,128)S(1)}, u32[]{:S(2)}, u32[]{:S(2)}) collective-permute-start(f32[256,256]{1,0:T(8,128)S(1)} %get-tuple-element.41.refs_0_), channel_id=1, source_target_pairs={{1,0},{2,1},{3,2},{0,3},{5,4},{6,5},{7,6},{4,7},{9,8},{10,9},{11,1... | collective-permute-start | bytes 786440 | tf_op jit(solution)/shard_map/ppermute | solution.py:390
  164.5 10.5 %collective-permute-done.20.refs_1_ = f32[256,256]{1,0:T(8,128)S(1)} collective-permute-done((f32[256,256]{1,0:T(8,128)S(1)}, f32[256,256]{1,0:T(8,128)S(1)}, u32[]{:S(2)}, u32[]{:S(2)}) %collective-permute-start.20) | collective-permute-done | bytes 262176 | tf_op jit(solution)/shard_map/ppermute | solution.py:390
  175.0 3.7 %collective-permute-done.22.refs_3_ = f32[256,256]{1,0:T(8,128)S(1)} collective-permute-done((f32[256,256]{1,0:T(8,128)S(1)}, f32[256,256]{1,0:T(8,128)S(1)}, u32[]{:S(2)}, u32[]{:S(2)}) %collective-permute-start.22) | collective-permute-done | bytes 262176 | tf_op jit(solution)/shard_map/ppermute | solution.py:390
  (65 shorter events, 41.3 us)
Async XLA Ops:
  4.7 10.4 %collective-permute-start.5 = (bf16[576,256]{1,0:T(8,128)(2,1)}, bf16[576,256]{1,0:T(8,128)(2,1)S(1)}, u32[]{:S(2)}, u32[]{:S(2)}) collective-permute-start(bf16[576,256]{1,0:T(8,128)(2,1)} %get-tuple-element.28), channel_id=1, source_target_pairs={{3,0},{0,1},{1,2},{2,3},{7,4},{4,5},{5,6},{6,7},{11,8},{8,9},{9,10... | collective-permute-start | bytes 884744 | tf_op jit(solution)/shard_map/ppermute | solution.py:390
  6.8 15.6 %collective-permute-start.4 = (bf16[576,256]{1,0:T(8,128)(2,1)}, bf16[576,256]{1,0:T(8,128)(2,1)S(1)}, u32[]{:S(2)}, u32[]{:S(2)}) collective-permute-start(bf16[576,256]{1,0:T(8,128)(2,1)} %get-tuple-element.28), channel_id=1, source_target_pairs={{2,0},{3,1},{0,2},{1,3},{6,4},{7,5},{4,6},{5,7},{10,8},{11,9},{8,1... | collective-permute-start | bytes 884744 | tf_op jit(solution)/shard_map/ppermute | solution.py:390
  9.5 13.0 %collective-permute-start.3 = (bf16[576,256]{1,0:T(8,128)(2,1)}, bf16[576,256]{1,0:T(8,128)(2,1)S(1)}, u32[]{:S(2)}, u32[]{:S(2)}) collective-permute-start(bf16[576,256]{1,0:T(8,128)(2,1)} %get-tuple-element.28), channel_id=1, source_target_pairs={{1,0},{2,1},{3,2},{0,3},{5,4},{6,5},{7,6},{4,7},{9,8},{10,9},{11,1... | collective-permute-start | bytes 884744 | tf_op jit(solution)/shard_map/ppermute | solution.py:390
  23.5 15.0 %collective-permute-start.6 = (bf16[4,576,256]{2,1,0:T(8,128)(2,1)S(1)}, bf16[4,576,256]{2,1,0:T(8,128)(2,1)S(1)}, u32[]{:S(2)}, u32[]{:S(2)}) collective-permute-start(bf16[4,576,256]{2,1,0:T(8,128)(2,1)S(1)} %pad_maximum_fusion.s0), channel_id=1, source_target_pairs={{4,0},{5,1},{6,2},{7,3},{0,4},{1,5},{2,6},{3,7},{12,8},{13,9},{14,... | collective-permute-start | bytes 3538952 | tf_op jit(solution)/shard_map/ppermute | solution.py:390
  25.1 6.3 %collective-permute-start.2 = (bf16[288,256]{1,0:T(8,128)(2,1)S(1)}, bf16[288,256]{1,0:T(8,128)(2,1)S(1)}, u32[]{:S(2)}, u32[]{:S(2)}) collective-permute-start(bf16[288,256]{1,0:T(8,128)(2,1)S(1)} %copy-done), channel_id=1, source_target_pairs={{24,0},{25,1},{26,2},{27,3},{100,4},{101,5},{102,6},{103,7},{0,8},... | collective-permute-start | bytes 442376 | tf_op jit(solution)/shard_map/ppermute | solution.py:390
  26.8 7.4 %collective-permute-start.1 = (bf16[288,256]{1,0:T(8,128)(2,1)S(1)}, bf16[288,256]{1,0:T(8,128)(2,1)S(1)}, u32[]{:S(2)}, u32[]{:S(2)}) collective-permute-start(bf16[288,256]{1,0:T(8,128)(2,1)S(1)} %copy-done), channel_id=1, source_target_pairs={{16,0},{17,1},{18,2},{19,3},{68,4},{69,5},{70,6},{71,7},{24,8},{25... | collective-permute-start | bytes 442376 | tf_op jit(solution)/shard_map/ppermute | solution.py:390
  34.3 10.3 %collective-permute-start.10 = (bf16[4,288,256]{2,1,0:T(8,128)(2,1)S(1)}, bf16[4,288,256]{2,1,0:T(8,128)(2,1)S(1)}, u32[]{:S(2)}, u32[]{:S(2)}) collective-permute-start(bf16[4,288,256]{2,1,0:T(8,128)(2,1)S(1)} %pad_maximum_fusion.1.refs_0_), channel_id=1, source_target_pairs={{96,0},{97,1},{98,2},{99,3},{28,4},{29,5},{30,6},{31,7},{104,8},{1... | collective-permute-start | bytes 1769480 | tf_op jit(solution)/shard_map/ppermute | solution.py:390
  35.6 13.0 %collective-permute-start.7 = (bf16[4,288,256]{2,1,0:T(8,128)(2,1)S(1)}, bf16[4,288,256]{2,1,0:T(8,128)(2,1)S(1)}, u32[]{:S(2)}, u32[]{:S(2)}) collective-permute-start(bf16[4,288,256]{2,1,0:T(8,128)(2,1)S(1)} %pad_maximum_fusion.1.refs_0_), channel_id=1, source_target_pairs={{32,0},{33,1},{34,2},{35,3},{12,4},{13,5},{14,6},{15,7},{40,8},{41... | collective-permute-start | bytes 1769480 | tf_op jit(solution)/shard_map/ppermute | solution.py:390
  37.0 15.5 %collective-permute-start.9 = (bf16[4,288,256]{2,1,0:T(8,128)(2,1)S(1)}, bf16[4,288,256]{2,1,0:T(8,128)(2,1)S(1)}, u32[]{:S(2)}, u32[]{:S(2)}) collective-permute-start(bf16[4,288,256]{2,1,0:T(8,128)(2,1)S(1)} %pad_maximum_fusion.1.refs_0_), channel_id=1, source_target_pairs={{64,0},{65,1},{66,2},{67,3},{20,4},{21,5},{22,6},{23,7},{72,8},{73... | collective-permute-start | bytes 1769480 | tf_op jit(solution)/shard_map/ppermute | solution.py:390
  57.8 36.6 %collective-permute-start.16 = (f32[4,512,256]{2,1,0:T(8,128)S(1)}, f32[4,512,256]{2,1,0:T(8,128)S(1)}, u32[]{:S(2)}, u32[]{:S(2)}) collective-permute-start(f32[4,512,256]{2,1,0:T(8,128)S(1)} %get-tuple-element.40), channel_id=1, source_target_pairs={{0,4},{1,5},{2,6},{3,7},{4,0},{5,1},{6,2},{7,3},{8,12},{9,13},{10,... | collective-permute-start | bytes 6291464 | tf_op jit(solution)/shard_map/ppermute | solution.py:394
  61.9 13.9 %collective-permute-start.12 = (f32[4,256,256]{2,1,0:T(8,128)S(1)}, f32[4,256,256]{2,1,0:T(8,128)S(1)}, u32[]{:S(2)}, u32[]{:S(2)}) collective-permute-start(f32[4,256,256]{2,1,0:T(8,128)S(1)} %get-tuple-element.38), channel_id=1, source_target_pairs={{0,96},{1,97},{2,98},{3,99},{4,28},{5,29},{6,30},{7,31},{8,104},{9... | collective-permute-start | bytes 3145736 | tf_op jit(solution)/shard_map/ppermute | solution.py:394
  62.8 15.5 %collective-permute-start.11 = (f32[4,256,256]{2,1,0:T(8,128)S(1)}, f32[4,256,256]{2,1,0:T(8,128)S(1)}, u32[]{:S(2)}, u32[]{:S(2)}) collective-permute-start(f32[4,256,256]{2,1,0:T(8,128)S(1)} %get-tuple-element.37), channel_id=1, source_target_pairs={{0,64},{1,65},{2,66},{3,67},{4,20},{5,21},{6,22},{7,23},{8,72},{9,... | collective-permute-start | bytes 3145736 | tf_op jit(solution)/shard_map/ppermute | solution.py:394
  64.9 24.6 %collective-permute-start.8 = (f32[4,256,256]{2,1,0:T(8,128)S(1)}, f32[4,256,256]{2,1,0:T(8,128)S(1)}, u32[]{:S(2)}, u32[]{:S(2)}) collective-permute-start(f32[4,256,256]{2,1,0:T(8,128)S(1)} %get-tuple-element.33), channel_id=1, source_target_pairs={{0,32},{1,33},{2,34},{3,35},{4,12},{5,13},{6,14},{7,15},{8,40},{9,... | collective-permute-start | bytes 3145736 | tf_op jit(solution)/shard_map/ppermute | solution.py:394
  89.8 11.6 %collective-permute-start.13 = (f32[256,256]{1,0:T(8,128)S(1)}, f32[256,256]{1,0:T(8,128)S(1)}, u32[]{:S(2)}, u32[]{:S(2)}) collective-permute-start(f32[256,256]{1,0:T(8,128)S(1)} %get-tuple-element.55), channel_id=1, source_target_pairs={{0,8},{1,9},{2,10},{3,11},{4,36},{5,37},{6,38},{7,39},{8,16},{9,17... | collective-permute-start | bytes 786440 | tf_op jit(solution)/shard_map/ppermute | solution.py:394
  94.7 14.2 %collective-permute-start.17 = (f32[512,256]{1,0:T(8,128)S(1)}, f32[512,256]{1,0:T(8,128)S(1)}, u32[]{:S(2)}, u32[]{:S(2)}) collective-permute-start(f32[512,256]{1,0:T(8,128)S(1)} %get-tuple-element.51), channel_id=1, source_target_pairs={{0,1},{1,2},{2,3},{3,0},{4,5},{5,6},{6,7},{7,4},{8,9},{9,10},{10,1... | collective-permute-start | bytes 1572872 | tf_op jit(solution)/shard_map/ppermute | solution.py:394
  95.7 24.8 %collective-permute-start.18 = (f32[512,256]{1,0:T(8,128)S(1)}, f32[512,256]{1,0:T(8,128)S(1)}, u32[]{:S(2)}, u32[]{:S(2)}) collective-permute-start(f32[512,256]{1,0:T(8,128)S(1)} %get-tuple-element.50), channel_id=1, source_target_pairs={{0,2},{1,3},{2,0},{3,1},{4,6},{5,7},{6,4},{7,5},{8,10},{9,11},{10,... | collective-permute-start | bytes 1572872 | tf_op jit(solution)/shard_map/ppermute | solution.py:394
  97.8 22.8 %collective-permute-start.19 = (f32[512,256]{1,0:T(8,128)S(1)}, f32[512,256]{1,0:T(8,128)S(1)}, u32[]{:S(2)}, u32[]{:S(2)}) collective-permute-start(f32[512,256]{1,0:T(8,128)S(1)} %get-tuple-element.49), channel_id=1, source_target_pairs={{0,3},{1,0},{2,1},{3,2},{4,7},{5,4},{6,5},{7,6},{8,11},{9,8},{10,9... | collective-permute-start | bytes 1572872 | tf_op jit(solution)/shard_map/ppermute | solution.py:394
  99.1 7.0 %collective-permute-start.14 = (f32[256,256]{1,0:T(8,128)S(1)}, f32[256,256]{1,0:T(8,128)S(1)}, u32[]{:S(2)}, u32[]{:S(2)}) collective-permute-start(f32[256,256]{1,0:T(8,128)S(1)} %get-tuple-element.54), channel_id=1, source_target_pairs={{0,16},{1,17},{2,18},{3,19},{4,68},{5,69},{6,70},{7,71},{8,24},{9,... | collective-permute-start | bytes 786440 | tf_op jit(solution)/shard_map/ppermute | solution.py:394
  101.4 6.5 %collective-permute-start.15 = (f32[256,256]{1,0:T(8,128)S(1)}, f32[256,256]{1,0:T(8,128)S(1)}, u32[]{:S(2)}, u32[]{:S(2)}) collective-permute-start(f32[256,256]{1,0:T(8,128)S(1)} %get-tuple-element.53), channel_id=1, source_target_pairs={{0,24},{1,25},{2,26},{3,27},{4,100},{5,101},{6,102},{7,103},{8,0},... | collective-permute-start | bytes 786440 | tf_op jit(solution)/shard_map/ppermute | solution.py:394
  125.7 5.0 %collective-permute-start.24 = (f32[3,32,256]{2,1,0:T(8,128)S(1)}, f32[3,32,256]{2,1,0:T(8,128)S(1)}, u32[]{:S(2)}, u32[]{:S(2)}) collective-permute-start(f32[3,32,256]{2,1,0:T(8,128)S(1)} %get-tuple-element.59), channel_id=1, source_target_pairs={{0,8},{1,9},{2,10},{3,11},{4,36},{5,37},{6,38},{7,39},{8,16},{9,17... | collective-permute-start | bytes 294920 | tf_op jit(solution)/shard_map/ppermute | solution.py:394
  127.2 5.0 %collective-permute-start.25 = (f32[3,32,256]{2,1,0:T(8,128)S(1)}, f32[3,32,256]{2,1,0:T(8,128)S(1)}, u32[]{:S(2)}, u32[]{:S(2)}) collective-permute-start(f32[3,32,256]{2,1,0:T(8,128)S(1)} %get-tuple-element.58), channel_id=1, source_target_pairs={{0,16},{1,17},{2,18},{3,19},{4,68},{5,69},{6,70},{7,71},{8,24},{9,... | collective-permute-start | bytes 294920 | tf_op jit(solution)/shard_map/ppermute | solution.py:394
  133.9 5.7 %collective-permute-start.29 = (f32[3,32,256]{2,1,0:T(8,128)S(1)}, f32[3,32,256]{2,1,0:T(8,128)S(1)}, u32[]{:S(2)}, u32[]{:S(2)}) collective-permute-start(f32[3,32,256]{2,1,0:T(8,128)S(1)} %fusion.12), channel_id=1, source_target_pairs={{96,0},{97,1},{98,2},{99,3},{28,4},{29,5},{30,6},{31,7},{104,8},{1... | collective-permute-start | bytes 294920 | tf_op jit(solution)/shard_map/ppermute | solution.py:390
  133.9 5.7 %collective-permute-start.27 = (f32[3,32,256]{2,1,0:T(8,128)S(1)}, f32[3,32,256]{2,1,0:T(8,128)S(1)}, u32[]{:S(2)}, u32[]{:S(2)}) collective-permute-start(f32[3,32,256]{2,1,0:T(8,128)S(1)} %fusion.12), channel_id=1, source_target_pairs={{64,0},{65,1},{66,2},{67,3},{20,4},{21,5},{22,6},{23,7},{72,8},{73... | collective-permute-start | bytes 294920 | tf_op jit(solution)/shard_map/ppermute | solution.py:390
  142.1 5.7 %collective-permute-start.32 = (f32[3,32,256]{2,1,0:T(8,128)S(1)}, f32[3,32,256]{2,1,0:T(8,128)S(1)}, u32[]{:S(2)}, u32[]{:S(2)}) collective-permute-start(f32[3,32,256]{2,1,0:T(8,128)S(1)} %add_add_fusion.1), channel_id=1, source_target_pairs={{3,0},{0,1},{1,2},{2,3},{7,4},{4,5},{5,6},{6,7},{11,8},{8,9},{9,10... | collective-permute-start | bytes 294920 | tf_op jit(solution)/shard_map/ppermute | solution.py:390
  142.1 5.7 %collective-permute-start.30 = (f32[3,32,256]{2,1,0:T(8,128)S(1)}, f32[3,32,256]{2,1,0:T(8,128)S(1)}, u32[]{:S(2)}, u32[]{:S(2)}) collective-permute-start(f32[3,32,256]{2,1,0:T(8,128)S(1)} %add_add_fusion.1), channel_id=1, source_target_pairs={{2,0},{3,1},{0,2},{1,3},{6,4},{7,5},{4,6},{5,7},{10,8},{11,9},{8,1... | collective-permute-start | bytes 294920 | tf_op jit(solution)/shard_map/ppermute | solution.py:390
  147.8 5.2 %collective-permute-start.33 = (f32[3,32,256]{2,1,0:T(8,128)S(1)}, f32[3,32,256]{2,1,0:T(8,128)S(1)}, u32[]{:S(2)}, u32[]{:S(2)}) collective-permute-start(f32[3,32,256]{2,1,0:T(8,128)S(1)} %add_add_fusion.refs_4_), channel_id=1, source_target_pairs={{8,0},{9,1},{10,2},{11,3},{36,4},{37,5},{38,6},{39,7},{16,8},{17,9... | collective-permute-start | bytes 294920 | tf_op jit(solution)/shard_map/ppermute | solution.py:390
  150.5 5.1 %collective-permute-start.34 = (f32[3,32,256]{2,1,0:T(8,128)S(1)}, f32[3,32,256]{2,1,0:T(8,128)S(1)}, u32[]{:S(2)}, u32[]{:S(2)}) collective-permute-start(f32[3,32,256]{2,1,0:T(8,128)S(1)} %add_add_fusion.refs_4_), channel_id=1, source_target_pairs={{16,0},{17,1},{18,2},{19,3},{68,4},{69,5},{70,6},{71,7},{24,8},{25... | collective-permute-start | bytes 294920 | tf_op jit(solution)/shard_map/ppermute | solution.py:390
  150.5 5.7 %collective-permute-start.35 = (f32[3,32,256]{2,1,0:T(8,128)S(1)}, f32[3,32,256]{2,1,0:T(8,128)S(1)}, u32[]{:S(2)}, u32[]{:S(2)}) collective-permute-start(f32[3,32,256]{2,1,0:T(8,128)S(1)} %add_add_fusion.refs_4_), channel_id=1, source_target_pairs={{24,0},{25,1},{26,2},{27,3},{100,4},{101,5},{102,6},{103,7},{0,8},... | collective-permute-start | bytes 294920 | tf_op jit(solution)/shard_map/ppermute | solution.py:390
  156.2 22.5 %collective-permute-start.36 = (f32[4,3,32,256]{3,2,1,0:T(8,128)S(1)}, f32[4,3,32,256]{3,2,1,0:T(8,128)S(1)}, u32[]{:S(2)}, u32[]{:S(2)}) collective-permute-start(f32[4,3,32,256]{3,2,1,0:T(8,128)S(1)} %pad_maximum_fusion.2), channel_id=1, source_target_pairs={{4,0},{5,1},{6,2},{7,3},{0,4},{1,5},{2,6},{3,7},{12,8},{13,9},{14,... | collective-permute-start | bytes 1179656 | tf_op jit(solution)/shard_map/ppermute | solution.py:390
  161.8 13.3 %collective-permute-start.20 = (f32[256,256]{1,0:T(8,128)S(1)}, f32[256,256]{1,0:T(8,128)S(1)}, u32[]{:S(2)}, u32[]{:S(2)}) collective-permute-start(f32[256,256]{1,0:T(8,128)S(1)} %get-tuple-element.41.refs_0_), channel_id=1, source_target_pairs={{1,0},{2,1},{3,2},{0,3},{5,4},{6,5},{7,6},{4,7},{9,8},{10,9},{11,1... | collective-permute-start | bytes 786440 | tf_op jit(solution)/shard_map/ppermute | solution.py:390
  164.0 11.1 %collective-permute-start.21 = (f32[256,256]{1,0:T(8,128)S(1)}, f32[256,256]{1,0:T(8,128)S(1)}, u32[]{:S(2)}, u32[]{:S(2)}) collective-permute-start(f32[256,256]{1,0:T(8,128)S(1)} %get-tuple-element.41.refs_0_), channel_id=1, source_target_pairs={{2,0},{3,1},{0,2},{1,3},{6,4},{7,5},{4,6},{5,7},{10,8},{11,9},{8,1... | collective-permute-start | bytes 786440 | tf_op jit(solution)/shard_map/ppermute | solution.py:390
  164.0 14.8 %collective-permute-start.22 = (f32[256,256]{1,0:T(8,128)S(1)}, f32[256,256]{1,0:T(8,128)S(1)}, u32[]{:S(2)}, u32[]{:S(2)}) collective-permute-start(f32[256,256]{1,0:T(8,128)S(1)} %get-tuple-element.41.refs_0_), channel_id=1, source_target_pairs={{3,0},{0,1},{1,2},{2,3},{7,4},{4,5},{5,6},{6,7},{11,8},{8,9},{9,10... | collective-permute-start | bytes 786440 | tf_op jit(solution)/shard_map/ppermute | solution.py:390
  (7 other events, 65.5 us)

commit v5 on v4

--- a/solution.py
+++ b/solution.py
@@ -117,21 +117,20 @@
     return [pl.multiple_of(v, GRAN) for v in off]
 
 
-def sources_kernel(s0, s1, omc, srow, scnt, spos):
-    sin = (s0, s1)
+def sources_kernel(*refs):
+    sin, (omc, srow, scnt, spos) = refs[:NS], refs[NS:]
     counts = []
     for k in range(NS):
-        both = [join(sin[k // YN], k % YN, SCAP + 32 * h)[3:4, 0:128] for h in range(SCAP // R)]
+        both = [join(sin[k], SCAP + 32 * h)[3:4, 0:128] for h in range(SCAP // R)]
         scnt[k:k + 1, :] = sum(both)
         counts.append(first_lane(sum(both)))
     soff = offsets(counts)
     chunks = (soff[NS] + SC - 1) // SC
     scnt[NS:NS + 1, :] = jnp.full((1, 128), chunks.astype(F32))
     for k in range(NS):
-        ref, d = sin[k // YN], k % YN
-        omc[pl.ds(soff[k], SCAP), :] = ref[d, 0:SCAP, :]
+        omc[pl.ds(soff[k], SCAP), :] = sin[k][0:SCAP, :]
         for h in range(SCAP // R):
-            spos[pl.ds(soff[k] + h * R, R), :] = join(ref, d, SCAP + 32 * h).T
+            spos[pl.ds(soff[k] + h * R, R), :] = join(sin[k], SCAP + 32 * h).T
     omc[pl.ds(soff[NS], SC), :] = jnp.zeros((SC, R), BF16)
     spos[pl.ds(soff[NS], SC), :] = jnp.full((SC, 8), FAR, F32)
 
@@ -151,7 +150,7 @@
             jax.ShapeDtypeStruct((SROWS // SC, 8, SC), F32),
             jax.ShapeDtypeStruct((2 * NS, 128), F32),
         ),
-        in_specs=[vm] * 2,
+        in_specs=[vm] * NS,
         out_specs=(vm,) * 3,
         scratch_shapes=[
             pltpu.VMEM((SROWS, 8), F32),
@@ -420,9 +419,9 @@
     tin = [column]
     for d in (1, 2, 3):
         tin.append(fetch(column, LAST, d))
-    srep = jnp.stack(srow)
-    sfar = fetch(srep, SAME["c"], 1)
-    src = sources([srep, sfar])
+    sfar = [fetch(spay, SAME["c"], 1)]
+    sfar += [fetch(v, SAME["c"], 1) for v in srow[1:]]
+    src = sources([*srow, *sfar])
     y0, za = sketch(tin[0:1], src)
     y1, zb = sketch(tin[1:2], src)
     y3, zd = sketch(tin[3:4], src)
@@ -446,7 +445,8 @@
     ]
     p = returned(chunks, FIRST)
     mine = (p[0] + p[1]) + (p[2] + p[3])
-    mine = gathered_sum(gathered_sum(mine, LAST), SAME["y"])
+    mine = gathered_sum(mine, LAST)
+    mine = gathered_sum(mine, SAME["y"])
     own = ring(mine, FIRST)
     other = fetch(jnp.stack(own), SAME["c"], 1)
     y, g0, g1, g2 = place(where, ys, own, other)

time: 181 us -> 170 us (0.939)
  waiting for transfers between devices: 89.6 us -> 78.7 us
    ppermute x24 -> x27, waiting for transfers between devices: 45.6 us -> 35.6 us  [fetch(): return lax.ppermute(v, ALL, [(b, a) for a, b in shifted(axes, d)])]
    ppermute x13, starting transfers between devices: 24.9 us -> 21.4 us  [give(): return lax.ppermute(v, ALL, shifted(axes, d))]
    ppermute x24 -> x27, starting transfers between devices: 37.1 us -> 40.2 us  [fetch(): return lax.ppermute(v, ALL, [(b, a) for a, b in shifted(axes, d)])]
  transfers between devices with their start and end apart: 37 -> 40, of which waited for: 26 -> 26; matrix products, arithmetic and copies ran while one was open for 0% -> 1% of each run, Pallas kernels for 7% -> 8%
where the time goes in v5:
time: 170 us
  waiting for transfers between devices  78.7 us (46%)
  starting transfers between devices  61.7 us (36%)
  Pallas kernels  24.4 us (14%)
  between operations  2.08 us (1%)
    ppermute x13, waiting for transfers between devices, give(): return lax.ppermute(v, ALL, shifted(axes, d))  43.1 us
    ppermute x27, starting transfers between devices, fetch(): return lax.ppermute(v, ALL, [(b, a) for a, b in shifted(axes, d)])  40.2 us
    ppermute x27, waiting for transfers between devices, fetch(): return lax.ppermute(v, ALL, [(b, a) for a, b in shifted(axes, d)])  35.6 us
    ppermute x13, starting transfers between devices, give(): return lax.ppermute(v, ALL, shifted(axes, d))  21.4 us
    pallas_call x4, Pallas kernels, sketch(): pl.pallas_call(functools.partial(sketch_kernel, m, last), out_shape=tuple...  17.1 us
  transfers between devices with their start and end apart: 40, of which 26 were waited for; matrix products, arithmetic and copies ran while one was open for 1% of the time, Pallas kernels for 8%

profile of v5, /device:TPU:1, one launch (start us, length us, event | category | flops | bytes accessed | tf_op | source)
XLA Modules:
  0.0 170.2 jit_solution(15537753370160595484)
XLA Ops:
  2.5 2.2 %shard_map.101 = (bf16[288,256]{1,0:T(8,128)(2,1)}, bf16[576,256]{1,0:T(8,128)(2,1)}) custom-call(s32[6]{0:T(128)} %stack.49.where_ref.refs_0_, f32[3,1024]{1,0:T(4,128)} %txyz_ref.1, f32[3,512]{1,0:T(4,128)} %sxyz_ref.1, bf16[1024,256]{1,0:T(8,128)(2,1)} %psi_ref.1, bf16[512,256]{1,0:T(8,128)(2,1)} %omega_ref.1), custom_call_target="tpu_custom_call" | custom-call | tf_op jit(solution)/shard_map/pallas_call | solution.py:82
  4.7 3.6 %collective-permute-start.3 = (bf16[576,256]{1,0:T(8,128)(2,1)}, bf16[576,256]{1,0:T(8,128)(2,1)S(1)}, u32[]{:S(2)}, u32[]{:S(2)}) collective-permute-start(bf16[576,256]{1,0:T(8,128)(2,1)} %get-tuple-element.28.refs_0_), channel_id=1, source_target_pairs={{1,0},{2,1},{3,2},{0,3},{5,4},{6,5},{7,6},{4,7},{9,8},{10,9},{11,1... | collective-permute-start | bytes 884744 | tf_op jit(solution)/shard_map/ppermute | solution.py:389
  11.0 3.3 %collective-permute-start.1 = (bf16[288,256]{1,0:T(8,128)(2,1)}, bf16[288,256]{1,0:T(8,128)(2,1)S(1)}, u32[]{:S(2)}, u32[]{:S(2)}) collective-permute-start(bf16[288,256]{1,0:T(8,128)(2,1)} %get-tuple-element.27.refs_9_), channel_id=1, source_target_pairs={{16,0},{17,1},{18,2},{19,3},{68,4},{69,5},{70,6},{71,7},{24,8},{25... | collective-permute-start | bytes 442376 | tf_op jit(solution)/shard_map/ppermute | solution.py:389
  20.5 1.7 collective-permute-start.7
  26.9 2.7 %collective-permute-start.12 = (bf16[4,288,256]{2,1,0:T(8,128)(2,1)S(1)}, bf16[4,288,256]{2,1,0:T(8,128)(2,1)S(1)}, u32[]{:S(2)}, u32[]{:S(2)}) collective-permute-start(bf16[4,288,256]{2,1,0:T(8,128)(2,1)S(1)} %pad_maximum_fusion.refs_0_), channel_id=1, source_target_pairs={{64,0},{65,1},{66,2},{67,3},{20,4},{21,5},{22,6},{23,7},{72,8},{73... | collective-permute-start | bytes 1769480 | tf_op jit(solution)/shard_map/ppermute | solution.py:389
  34.7 4.0 %shard_map.103 = (f32[4,256,256]{2,1,0:T(8,128)S(1)}, f32[5120,256]{1,0:T(8,128)S(1)}) custom-call(bf16[4,288,256]{2,1,0:T(8,128)(2,1)S(1)} %pad_maximum_fusion.refs_0_, bf16[5120,256]{1,0:T(8,128)(2,1)S(1)} %get-tuple-element.29.refs_1_, f32[10,8,512]{2,1,0:T(8,128)S(1)} %get-tuple-element.30.refs_2_, f32[16,128]{1,0:T(8,128)S(1)} %get-tuple-element.31.refs_3_), custom_call_target="tpu_custom_call" | custom-call | tf_op jit(solution)/shard_map/pallas_call | solution.py:274
  38.7 4.0 %shard_map.105 = (f32[4,256,256]{2,1,0:T(8,128)S(1)}, f32[5120,256]{1,0:T(8,128)S(1)}) custom-call(bf16[4,288,256]{2,1,0:T(8,128)(2,1)S(1)} %collective-permute-done.13.refs_0_, bf16[5120,256]{1,0:T(8,128)(2,1)S(1)} %get-tuple-element.29.refs_1_, f32[10,8,512]{2,1,0:T(8,128)S(1)} %get-tuple-element.30.refs_2_, f32[16,128]{1,0:T(8,128)S(1)} %get-tuple-element.31.refs_3_), custom_call_target="tpu_custom_call" | custom-call | tf_op jit(solution)/shard_map/pallas_call | solution.py:274
  42.7 4.0 %shard_map.104 = (f32[4,256,256]{2,1,0:T(8,128)S(1)}, f32[5120,256]{1,0:T(8,128)S(1)}) custom-call(bf16[4,288,256]{2,1,0:T(8,128)(2,1)S(1)} %collective-permute-done.10.refs_0_, bf16[5120,256]{1,0:T(8,128)(2,1)S(1)} %get-tuple-element.29.refs_1_, f32[10,8,512]{2,1,0:T(8,128)S(1)} %get-tuple-element.30.refs_2_, f32[16,128]{1,0:T(8,128)S(1)} %get-tuple-element.31.refs_3_), custom_call_target="tpu_custom_call" | custom-call | tf_op jit(solution)/shard_map/pallas_call | solution.py:274
  46.7 5.2 %shard_map.106 = (f32[4,256,256]{2,1,0:T(8,128)S(1)}, f32[4,512,256]{2,1,0:T(8,128)S(1)}, f32[4,512,256]{2,1,0:T(8,128)S(1)}) custom-call(bf16[4,288,256]{2,1,0:T(8,128)(2,1)S(1)} %collective-permute-done.12.refs_0_, bf16[5120,256]{1,0:T(8,128)(2,1)S(1)} %get-tuple-element.29.refs_1_, f32[10,8,512]{2,1,0:T(8,128)S(1)} %get-tuple-element.30.refs_2_, ...), custom_call_target="tpu_custom_call" | custom-call | tf_op jit(solution)/shard_map/pallas_call | solution.py:274
  52.3 3.0 %collective-permute-start.14 = (f32[4,256,256]{2,1,0:T(8,128)S(1)}, f32[4,256,256]{2,1,0:T(8,128)S(1)}, u32[]{:S(2)}, u32[]{:S(2)}) collective-permute-start(f32[4,256,256]{2,1,0:T(8,128)S(1)} %get-tuple-element.37), channel_id=1, source_target_pairs={{0,64},{1,65},{2,66},{3,67},{4,20},{5,21},{6,22},{7,23},{8,72},{9,... | collective-permute-start | bytes 3145736 | tf_op jit(solution)/shard_map/ppermute | solution.py:393
  55.9 10.3 %collective-permute-done.15 = f32[4,256,256]{2,1,0:T(8,128)S(1)} collective-permute-done((f32[4,256,256]{2,1,0:T(8,128)S(1)}, f32[4,256,256]{2,1,0:T(8,128)S(1)}, u32[]{:S(2)}, u32[]{:S(2)}) %collective-permute-start.15) | collective-permute-done | bytes 1048608 | tf_op jit(solution)/shard_map/ppermute | solution.py:393
  67.9 11.2 %collective-permute-done.11 = f32[4,256,256]{2,1,0:T(8,128)S(1)} collective-permute-done((f32[4,256,256]{2,1,0:T(8,128)S(1)}, f32[4,256,256]{2,1,0:T(8,128)S(1)}, u32[]{:S(2)}, u32[]{:S(2)}) %collective-permute-start.11) | collective-permute-done | bytes 1048608 | tf_op jit(solution)/shard_map/ppermute | solution.py:393
  79.3 3.6 %collective-permute-start.16 = (f32[256,256]{1,0:T(8,128)S(1)}, f32[256,256]{1,0:T(8,128)S(1)}, u32[]{:S(2)}, u32[]{:S(2)}) collective-permute-start(f32[256,256]{1,0:T(8,128)S(1)} %get-tuple-element.55), channel_id=1, source_target_pairs={{0,8},{1,9},{2,10},{3,11},{4,36},{5,37},{6,38},{7,39},{8,16},{9,17... | collective-permute-start | bytes 786440 | tf_op jit(solution)/shard_map/ppermute | solution.py:393
  83.3 4.5 %collective-permute-start.21 = (f32[512,256]{1,0:T(8,128)S(1)}, f32[512,256]{1,0:T(8,128)S(1)}, u32[]{:S(2)}, u32[]{:S(2)}) collective-permute-start(f32[512,256]{1,0:T(8,128)S(1)} %get-tuple-element.50), channel_id=1, source_target_pairs={{0,2},{1,3},{2,0},{3,1},{4,6},{5,7},{6,4},{7,5},{8,10},{9,11},{10,... | collective-permute-start | bytes 1572872 | tf_op jit(solution)/shard_map/ppermute | solution.py:393
  87.8 2.5 %collective-permute-start.17 = (f32[256,256]{1,0:T(8,128)S(1)}, f32[256,256]{1,0:T(8,128)S(1)}, u32[]{:S(2)}, u32[]{:S(2)}) collective-permute-start(f32[256,256]{1,0:T(8,128)S(1)} %get-tuple-element.54), channel_id=1, source_target_pairs={{0,16},{1,17},{2,18},{3,19},{4,68},{5,69},{6,70},{7,71},{8,24},{9,... | collective-permute-start | bytes 786440 | tf_op jit(solution)/shard_map/ppermute | solution.py:393
  90.3 2.0 %collective-permute-start.18 = (f32[256,256]{1,0:T(8,128)S(1)}, f32[256,256]{1,0:T(8,128)S(1)}, u32[]{:S(2)}, u32[]{:S(2)}) collective-permute-start(f32[256,256]{1,0:T(8,128)S(1)} %get-tuple-element.53), channel_id=1, source_target_pairs={{0,24},{1,25},{2,26},{3,27},{4,100},{5,101},{6,102},{7,103},{8,0},... | collective-permute-start | bytes 786440 | tf_op jit(solution)/shard_map/ppermute | solution.py:393
  92.4 2.5 %collective-permute-done.17.refs_3_ = f32[256,256]{1,0:T(8,128)S(1)} collective-permute-done((f32[256,256]{1,0:T(8,128)S(1)}, f32[256,256]{1,0:T(8,128)S(1)}, u32[]{:S(2)}, u32[]{:S(2)}) %collective-permute-start.17) | collective-permute-done | bytes 262176 | tf_op jit(solution)/shard_map/ppermute | solution.py:393
  94.8 2.0 %collective-permute-done.18.refs_4_ = f32[256,256]{1,0:T(8,128)S(1)} collective-permute-done((f32[256,256]{1,0:T(8,128)S(1)}, f32[256,256]{1,0:T(8,128)S(1)}, u32[]{:S(2)}, u32[]{:S(2)}) %collective-permute-start.18) | collective-permute-done | bytes 262176 | tf_op jit(solution)/shard_map/ppermute | solution.py:393
  98.2 12.1 %collective-permute-done.21.refs_7_ = f32[512,256]{1,0:T(8,128)S(1)} collective-permute-done((f32[512,256]{1,0:T(8,128)S(1)}, f32[512,256]{1,0:T(8,128)S(1)}, u32[]{:S(2)}, u32[]{:S(2)}) %collective-permute-start.21) | collective-permute-done | bytes 524320 | tf_op jit(solution)/shard_map/ppermute | solution.py:393
  110.4 2.1 %shard_map.107 = (f32[256,256]{1,0:T(8,128)S(1)}, f32[512,256]{1,0:T(8,128)}, f32[3,128,256]{2,1,0:T(8,128)S(1)}, f32[3,128,256]{2,1,0:T(8,128)S(1)}) custom-call(s32[6]{0:T(128)S(1)} %copy-done.2, f32[256,256]{1,0:T(8,128)S(1)} %get-tuple-element.56.refs_1_, f32[256,256]{1,0:T(8,128)S(1)} %collective-permute-done.16.refs_2_, ...), custom_call_target="tpu_custom_call" | custom-call | tf_op jit(solution)/shard_map/pallas_call | solution.py:320
  118.1 2.0 %collective-permute-start.29 = (f32[3,32,256]{2,1,0:T(8,128)S(1)}, f32[3,32,256]{2,1,0:T(8,128)S(1)}, u32[]{:S(2)}, u32[]{:S(2)}) collective-permute-start(f32[3,32,256]{2,1,0:T(8,128)S(1)} %get-tuple-element.57), channel_id=1, source_target_pairs={{0,24},{1,25},{2,26},{3,27},{4,100},{5,101},{6,102},{7,103},{8,0},... | collective-permute-start | bytes 294920 | tf_op jit(solution)/shard_map/ppermute | solution.py:393
  125.7 3.7 %collective-permute-done.32 = f32[3,32,256]{2,1,0:T(8,128)S(1)} collective-permute-done((f32[3,32,256]{2,1,0:T(8,128)S(1)}, f32[3,32,256]{2,1,0:T(8,128)S(1)}, u32[]{:S(2)}, u32[]{:S(2)}) %collective-permute-start.32) | collective-permute-done | bytes 98336 | tf_op jit(solution)/shard_map/ppermute | solution.py:389
  129.4 1.9 %collective-permute-start.34 = (f32[3,32,256]{2,1,0:T(8,128)S(1)}, f32[3,32,256]{2,1,0:T(8,128)S(1)}, u32[]{:S(2)}, u32[]{:S(2)}) collective-permute-start(f32[3,32,256]{2,1,0:T(8,128)S(1)} %add_add_fusion.1), channel_id=1, source_target_pairs={{1,0},{2,1},{3,2},{0,3},{5,4},{6,5},{7,6},{4,7},{9,8},{10,9},{11,1... | collective-permute-start | bytes 294920 | tf_op jit(solution)/shard_map/ppermute | solution.py:389
  133.0 4.1 %collective-permute-done.35 = f32[3,32,256]{2,1,0:T(8,128)S(1)} collective-permute-done((f32[3,32,256]{2,1,0:T(8,128)S(1)}, f32[3,32,256]{2,1,0:T(8,128)S(1)}, u32[]{:S(2)}, u32[]{:S(2)}) %collective-permute-start.35) | collective-permute-done | bytes 98336 | tf_op jit(solution)/shard_map/ppermute | solution.py:389
  137.1 2.4 %collective-permute-start.36 = (f32[3,32,256]{2,1,0:T(8,128)S(1)}, f32[3,32,256]{2,1,0:T(8,128)S(1)}, u32[]{:S(2)}, u32[]{:S(2)}) collective-permute-start(f32[3,32,256]{2,1,0:T(8,128)S(1)} %add_add_fusion.refs_4_), channel_id=1, source_target_pairs={{8,0},{9,1},{10,2},{11,3},{36,4},{37,5},{38,6},{39,7},{16,8},{17,9... | collective-permute-start | bytes 294920 | tf_op jit(solution)/shard_map/ppermute | solution.py:389
  140.2 1.9 %collective-permute-done.36.refs_5_ = f32[3,32,256]{2,1,0:T(8,128)S(1)} collective-permute-done((f32[3,32,256]{2,1,0:T(8,128)S(1)}, f32[3,32,256]{2,1,0:T(8,128)S(1)}, u32[]{:S(2)}, u32[]{:S(2)}) %collective-permute-start.36) | collective-permute-done | bytes 98336 | tf_op jit(solution)/shard_map/ppermute | solution.py:389
  142.2 2.5 %collective-permute-done.37.refs_6_ = f32[3,32,256]{2,1,0:T(8,128)S(1)} collective-permute-done((f32[3,32,256]{2,1,0:T(8,128)S(1)}, f32[3,32,256]{2,1,0:T(8,128)S(1)}, u32[]{:S(2)}, u32[]{:S(2)}) %collective-permute-start.37) | collective-permute-done | bytes 98336 | tf_op jit(solution)/shard_map/ppermute | solution.py:389
  145.5 5.9 %collective-permute-start.39 = (f32[4,3,32,256]{3,2,1,0:T(8,128)S(1)}, f32[4,3,32,256]{3,2,1,0:T(8,128)S(1)}, u32[]{:S(2)}, u32[]{:S(2)}) collective-permute-start(f32[4,3,32,256]{3,2,1,0:T(8,128)S(1)} %pad_maximum_fusion.1), channel_id=1, source_target_pairs={{4,0},{5,1},{6,2},{7,3},{0,4},{1,5},{2,6},{3,7},{12,8},{13,9},{14,... | collective-permute-start | bytes 1179656 | tf_op jit(solution)/shard_map/ppermute | solution.py:389
  151.3 2.2 %collective-permute-start.23 = (f32[256,256]{1,0:T(8,128)S(1)}, f32[256,256]{1,0:T(8,128)S(1)}, u32[]{:S(2)}, u32[]{:S(2)}) collective-permute-start(f32[256,256]{1,0:T(8,128)S(1)} %get-tuple-element.41.refs_0_), channel_id=1, source_target_pairs={{1,0},{2,1},{3,2},{0,3},{5,4},{6,5},{7,6},{4,7},{9,8},{10,9},{11,1... | collective-permute-start | bytes 786440 | tf_op jit(solution)/shard_map/ppermute | solution.py:389
  154.1 10.5 %collective-permute-done.23.refs_1_ = f32[256,256]{1,0:T(8,128)S(1)} collective-permute-done((f32[256,256]{1,0:T(8,128)S(1)}, f32[256,256]{1,0:T(8,128)S(1)}, u32[]{:S(2)}, u32[]{:S(2)}) %collective-permute-start.23) | collective-permute-done | bytes 262176 | tf_op jit(solution)/shard_map/ppermute | solution.py:389
  164.6 3.7 %collective-permute-done.25.refs_3_ = f32[256,256]{1,0:T(8,128)S(1)} collective-permute-done((f32[256,256]{1,0:T(8,128)S(1)}, f32[256,256]{1,0:T(8,128)S(1)}, u32[]{:S(2)}, u32[]{:S(2)}) %collective-permute-start.25) | collective-permute-done | bytes 262176 | tf_op jit(solution)/shard_map/ppermute | solution.py:389
  168.3 1.9 %shard_map.108 = (f32[1024,256]{1,0:T(8,128)}, f32[256,256]{1,0:T(8,128)}, f32[256,256]{1,0:T(8,128)}, f32[256,256]{1,0:T(8,128)}) custom-call(s32[6]{0:T(128)S(1)} %copy-done.2, f32[256,256]{1,0:T(8,128)S(1)} %get-tuple-element.41.refs_0_, f32[256,256]{1,0:T(8,128)S(1)} %collective-permute-done.23.refs_1_, f32[256,256]{1,0:T(8,128)S(1)} %collective-permute-done.24.refs_2_, ...), custom_call_target="tpu_custom_call" | custom-call | tf_op jit(solution)/shard_map/pallas_call | solution.py:356
  (72 shorter events, 39.0 us)
Async XLA Ops:
  4.7 15.7 %collective-permute-start.3 = (bf16[576,256]{1,0:T(8,128)(2,1)}, bf16[576,256]{1,0:T(8,128)(2,1)S(1)}, u32[]{:S(2)}, u32[]{:S(2)}) collective-permute-start(bf16[576,256]{1,0:T(8,128)(2,1)} %get-tuple-element.28.refs_0_), channel_id=1, source_target_pairs={{1,0},{2,1},{3,2},{0,3},{5,4},{6,5},{7,6},{4,7},{9,8},{10,9},{11,1... | collective-permute-start | bytes 884744 | tf_op jit(solution)/shard_map/ppermute | solution.py:389
  8.3 6.8 %collective-permute-start.2 = (bf16[288,256]{1,0:T(8,128)(2,1)}, bf16[288,256]{1,0:T(8,128)(2,1)S(1)}, u32[]{:S(2)}, u32[]{:S(2)}) collective-permute-start(bf16[288,256]{1,0:T(8,128)(2,1)} %get-tuple-element.27.refs_9_), channel_id=1, source_target_pairs={{24,0},{25,1},{26,2},{27,3},{100,4},{101,5},{102,6},{103,7},{0,8},... | collective-permute-start | bytes 442376 | tf_op jit(solution)/shard_map/ppermute | solution.py:389
  9.9 14.5 %collective-permute-start.4 = (bf16[576,256]{1,0:T(8,128)(2,1)}, bf16[576,256]{1,0:T(8,128)(2,1)S(1)}, u32[]{:S(2)}, u32[]{:S(2)}) collective-permute-start(bf16[576,256]{1,0:T(8,128)(2,1)} %get-tuple-element.28.refs_0_), channel_id=1, source_target_pairs={{2,0},{3,1},{0,2},{1,3},{6,4},{7,5},{4,6},{5,7},{10,8},{11,9},{8,1... | collective-permute-start | bytes 884744 | tf_op jit(solution)/shard_map/ppermute | solution.py:389
  10.3 16.6 %collective-permute-start.5 = (bf16[576,256]{1,0:T(8,128)(2,1)}, bf16[576,256]{1,0:T(8,128)(2,1)S(1)}, u32[]{:S(2)}, u32[]{:S(2)}) collective-permute-start(bf16[576,256]{1,0:T(8,128)(2,1)} %get-tuple-element.28.refs_0_), channel_id=1, source_target_pairs={{3,0},{0,1},{1,2},{2,3},{7,4},{4,5},{5,6},{6,7},{11,8},{8,9},{9,10... | collective-permute-start | bytes 884744 | tf_op jit(solution)/shard_map/ppermute | solution.py:389
  11.0 6.9 %collective-permute-start.1 = (bf16[288,256]{1,0:T(8,128)(2,1)}, bf16[288,256]{1,0:T(8,128)(2,1)S(1)}, u32[]{:S(2)}, u32[]{:S(2)}) collective-permute-start(bf16[288,256]{1,0:T(8,128)(2,1)} %get-tuple-element.27.refs_9_), channel_id=1, source_target_pairs={{16,0},{17,1},{18,2},{19,3},{68,4},{69,5},{70,6},{71,7},{24,8},{25... | collective-permute-start | bytes 442376 | tf_op jit(solution)/shard_map/ppermute | solution.py:389
  15.1 7.1 %collective-permute-start = (bf16[288,256]{1,0:T(8,128)(2,1)}, bf16[288,256]{1,0:T(8,128)(2,1)S(1)}, u32[]{:S(2)}, u32[]{:S(2)}) collective-permute-start(bf16[288,256]{1,0:T(8,128)(2,1)} %get-tuple-element.27.refs_9_), channel_id=1, source_target_pairs={{8,0},{9,1},{10,2},{11,3},{36,4},{37,5},{38,6},{39,7},{16,8},{17,9... | collective-permute-start | bytes 442376 | tf_op jit(solution)/shard_map/ppermute | solution.py:389
  17.8 11.8 %collective-permute-start.6 = (bf16[576,256]{1,0:T(8,128)(2,1)}, bf16[576,256]{1,0:T(8,128)(2,1)S(1)}, u32[]{:S(2)}, u32[]{:S(2)}) collective-permute-start(bf16[576,256]{1,0:T(8,128)(2,1)} %get-tuple-element.28.refs_0_), channel_id=1, source_target_pairs={{4,0},{5,1},{6,2},{7,3},{0,4},{1,5},{2,6},{3,7},{12,8},{13,9},{14,... | collective-permute-start | bytes 884744 | tf_op jit(solution)/shard_map/ppermute | solution.py:389
  20.5 10.5 %collective-permute-start.7 = (bf16[576,256]{1,0:T(8,128)(2,1)S(1)}, bf16[576,256]{1,0:T(8,128)(2,1)S(1)}, u32[]{:S(2)}, u32[]{:S(2)}) collective-permute-start(bf16[576,256]{1,0:T(8,128)(2,1)S(1)} %collective-permute-done.3.refs_1_), channel_id=1, source_target_pairs={{4,0},{5,1},{6,2},{7,3},{0,4},{1,5},{2,6},{3,7},{12,8},{13,9},{14,... | collective-permute-start | bytes 884744 | tf_op jit(solution)/shard_map/ppermute | solution.py:389
  23.1 15.6 %collective-permute-start.13 = (bf16[4,288,256]{2,1,0:T(8,128)(2,1)S(1)}, bf16[4,288,256]{2,1,0:T(8,128)(2,1)S(1)}, u32[]{:S(2)}, u32[]{:S(2)}) collective-permute-start(bf16[4,288,256]{2,1,0:T(8,128)(2,1)S(1)} %pad_maximum_fusion.refs_0_), channel_id=1, source_target_pairs={{96,0},{97,1},{98,2},{99,3},{28,4},{29,5},{30,6},{31,7},{104,8},{1... | collective-permute-start | bytes 1769480 | tf_op jit(solution)/shard_map/ppermute | solution.py:389
  24.4 18.3 %collective-permute-start.10 = (bf16[4,288,256]{2,1,0:T(8,128)(2,1)S(1)}, bf16[4,288,256]{2,1,0:T(8,128)(2,1)S(1)}, u32[]{:S(2)}, u32[]{:S(2)}) collective-permute-start(bf16[4,288,256]{2,1,0:T(8,128)(2,1)S(1)} %pad_maximum_fusion.refs_0_), channel_id=1, source_target_pairs={{32,0},{33,1},{34,2},{35,3},{12,4},{13,5},{14,6},{15,7},{40,8},{41... | collective-permute-start | bytes 1769480 | tf_op jit(solution)/shard_map/ppermute | solution.py:389
  26.9 19.8 %collective-permute-start.12 = (bf16[4,288,256]{2,1,0:T(8,128)(2,1)S(1)}, bf16[4,288,256]{2,1,0:T(8,128)(2,1)S(1)}, u32[]{:S(2)}, u32[]{:S(2)}) collective-permute-start(bf16[4,288,256]{2,1,0:T(8,128)(2,1)S(1)} %pad_maximum_fusion.refs_0_), channel_id=1, source_target_pairs={{64,0},{65,1},{66,2},{67,3},{20,4},{21,5},{22,6},{23,7},{72,8},{73... | collective-permute-start | bytes 1769480 | tf_op jit(solution)/shard_map/ppermute | solution.py:389
  51.9 31.1 %collective-permute-start.19 = (f32[4,512,256]{2,1,0:T(8,128)S(1)}, f32[4,512,256]{2,1,0:T(8,128)S(1)}, u32[]{:S(2)}, u32[]{:S(2)}) collective-permute-start(f32[4,512,256]{2,1,0:T(8,128)S(1)} %get-tuple-element.40), channel_id=1, source_target_pairs={{0,4},{1,5},{2,6},{3,7},{4,0},{5,1},{6,2},{7,3},{8,12},{9,13},{10,... | collective-permute-start | bytes 6291464 | tf_op jit(solution)/shard_map/ppermute | solution.py:393
  52.3 13.9 %collective-permute-start.15 = (f32[4,256,256]{2,1,0:T(8,128)S(1)}, f32[4,256,256]{2,1,0:T(8,128)S(1)}, u32[]{:S(2)}, u32[]{:S(2)}) collective-permute-start(f32[4,256,256]{2,1,0:T(8,128)S(1)} %get-tuple-element.38), channel_id=1, source_target_pairs={{0,96},{1,97},{2,98},{3,99},{4,28},{5,29},{6,30},{7,31},{8,104},{9... | collective-permute-start | bytes 3145736 | tf_op jit(solution)/shard_map/ppermute | solution.py:393
  52.3 15.5 %collective-permute-start.14 = (f32[4,256,256]{2,1,0:T(8,128)S(1)}, f32[4,256,256]{2,1,0:T(8,128)S(1)}, u32[]{:S(2)}, u32[]{:S(2)}) collective-permute-start(f32[4,256,256]{2,1,0:T(8,128)S(1)} %get-tuple-element.37), channel_id=1, source_target_pairs={{0,64},{1,65},{2,66},{3,67},{4,20},{5,21},{6,22},{7,23},{8,72},{9,... | collective-permute-start | bytes 3145736 | tf_op jit(solution)/shard_map/ppermute | solution.py:393
  55.3 23.7 %collective-permute-start.11 = (f32[4,256,256]{2,1,0:T(8,128)S(1)}, f32[4,256,256]{2,1,0:T(8,128)S(1)}, u32[]{:S(2)}, u32[]{:S(2)}) collective-permute-start(f32[4,256,256]{2,1,0:T(8,128)S(1)} %get-tuple-element.33), channel_id=1, source_target_pairs={{0,32},{1,33},{2,34},{3,35},{4,12},{5,13},{6,14},{7,15},{8,40},{9,... | collective-permute-start | bytes 3145736 | tf_op jit(solution)/shard_map/ppermute | solution.py:393
  79.3 11.0 %collective-permute-start.16 = (f32[256,256]{1,0:T(8,128)S(1)}, f32[256,256]{1,0:T(8,128)S(1)}, u32[]{:S(2)}, u32[]{:S(2)}) collective-permute-start(f32[256,256]{1,0:T(8,128)S(1)} %get-tuple-element.55), channel_id=1, source_target_pairs={{0,8},{1,9},{2,10},{3,11},{4,36},{5,37},{6,38},{7,39},{8,16},{9,17... | collective-permute-start | bytes 786440 | tf_op jit(solution)/shard_map/ppermute | solution.py:393
  83.3 15.0 %collective-permute-start.20 = (f32[512,256]{1,0:T(8,128)S(1)}, f32[512,256]{1,0:T(8,128)S(1)}, u32[]{:S(2)}, u32[]{:S(2)}) collective-permute-start(f32[512,256]{1,0:T(8,128)S(1)} %get-tuple-element.51), channel_id=1, source_target_pairs={{0,1},{1,2},{2,3},{3,0},{4,5},{5,6},{6,7},{7,4},{8,9},{9,10},{10,1... | collective-permute-start | bytes 1572872 | tf_op jit(solution)/shard_map/ppermute | solution.py:393
  83.3 27.0 %collective-permute-start.21 = (f32[512,256]{1,0:T(8,128)S(1)}, f32[512,256]{1,0:T(8,128)S(1)}, u32[]{:S(2)}, u32[]{:S(2)}) collective-permute-start(f32[512,256]{1,0:T(8,128)S(1)} %get-tuple-element.50), channel_id=1, source_target_pairs={{0,2},{1,3},{2,0},{3,1},{4,6},{5,7},{6,4},{7,5},{8,10},{9,11},{10,... | collective-permute-start | bytes 1572872 | tf_op jit(solution)/shard_map/ppermute | solution.py:393
  87.8 22.6 %collective-permute-start.22 = (f32[512,256]{1,0:T(8,128)S(1)}, f32[512,256]{1,0:T(8,128)S(1)}, u32[]{:S(2)}, u32[]{:S(2)}) collective-permute-start(f32[512,256]{1,0:T(8,128)S(1)} %get-tuple-element.49), channel_id=1, source_target_pairs={{0,3},{1,0},{2,1},{3,2},{4,7},{5,4},{6,5},{7,6},{8,11},{9,8},{10,9... | collective-permute-start | bytes 1572872 | tf_op jit(solution)/shard_map/ppermute | solution.py:393
  87.8 7.0 %collective-permute-start.17 = (f32[256,256]{1,0:T(8,128)S(1)}, f32[256,256]{1,0:T(8,128)S(1)}, u32[]{:S(2)}, u32[]{:S(2)}) collective-permute-start(f32[256,256]{1,0:T(8,128)S(1)} %get-tuple-element.54), channel_id=1, source_target_pairs={{0,16},{1,17},{2,18},{3,19},{4,68},{5,69},{6,70},{7,71},{8,24},{9,... | collective-permute-start | bytes 786440 | tf_op jit(solution)/shard_map/ppermute | solution.py:393
  90.3 6.5 %collective-permute-start.18 = (f32[256,256]{1,0:T(8,128)S(1)}, f32[256,256]{1,0:T(8,128)S(1)}, u32[]{:S(2)}, u32[]{:S(2)}) collective-permute-start(f32[256,256]{1,0:T(8,128)S(1)} %get-tuple-element.53), channel_id=1, source_target_pairs={{0,24},{1,25},{2,26},{3,27},{4,100},{5,101},{6,102},{7,103},{8,0},... | collective-permute-start | bytes 786440 | tf_op jit(solution)/shard_map/ppermute | solution.py:393
  116.7 5.1 %collective-permute-start.28 = (f32[3,32,256]{2,1,0:T(8,128)S(1)}, f32[3,32,256]{2,1,0:T(8,128)S(1)}, u32[]{:S(2)}, u32[]{:S(2)}) collective-permute-start(f32[3,32,256]{2,1,0:T(8,128)S(1)} %get-tuple-element.58), channel_id=1, source_target_pairs={{0,16},{1,17},{2,18},{3,19},{4,68},{5,69},{6,70},{7,71},{8,24},{9,... | collective-permute-start | bytes 294920 | tf_op jit(solution)/shard_map/ppermute | solution.py:393
  123.7 5.7 %collective-permute-start.32 = (f32[3,32,256]{2,1,0:T(8,128)S(1)}, f32[3,32,256]{2,1,0:T(8,128)S(1)}, u32[]{:S(2)}, u32[]{:S(2)}) collective-permute-start(f32[3,32,256]{2,1,0:T(8,128)S(1)} %fusion.12), channel_id=1, source_target_pairs={{96,0},{97,1},{98,2},{99,3},{28,4},{29,5},{30,6},{31,7},{104,8},{1... | collective-permute-start | bytes 294920 | tf_op jit(solution)/shard_map/ppermute | solution.py:389
  123.7 5.7 %collective-permute-start.30 = (f32[3,32,256]{2,1,0:T(8,128)S(1)}, f32[3,32,256]{2,1,0:T(8,128)S(1)}, u32[]{:S(2)}, u32[]{:S(2)}) collective-permute-start(f32[3,32,256]{2,1,0:T(8,128)S(1)} %fusion.12), channel_id=1, source_target_pairs={{64,0},{65,1},{66,2},{67,3},{20,4},{21,5},{22,6},{23,7},{72,8},{73... | collective-permute-start | bytes 294920 | tf_op jit(solution)/shard_map/ppermute | solution.py:389
  131.4 5.7 %collective-permute-start.35 = (f32[3,32,256]{2,1,0:T(8,128)S(1)}, f32[3,32,256]{2,1,0:T(8,128)S(1)}, u32[]{:S(2)}, u32[]{:S(2)}) collective-permute-start(f32[3,32,256]{2,1,0:T(8,128)S(1)} %add_add_fusion.1), channel_id=1, source_target_pairs={{3,0},{0,1},{1,2},{2,3},{7,4},{4,5},{5,6},{6,7},{11,8},{8,9},{9,10... | collective-permute-start | bytes 294920 | tf_op jit(solution)/shard_map/ppermute | solution.py:389
  131.4 5.7 %collective-permute-start.33 = (f32[3,32,256]{2,1,0:T(8,128)S(1)}, f32[3,32,256]{2,1,0:T(8,128)S(1)}, u32[]{:S(2)}, u32[]{:S(2)}) collective-permute-start(f32[3,32,256]{2,1,0:T(8,128)S(1)} %add_add_fusion.1), channel_id=1, source_target_pairs={{2,0},{3,1},{0,2},{1,3},{6,4},{7,5},{4,6},{5,7},{10,8},{11,9},{8,1... | collective-permute-start | bytes 294920 | tf_op jit(solution)/shard_map/ppermute | solution.py:389
  139.6 5.1 %collective-permute-start.37 = (f32[3,32,256]{2,1,0:T(8,128)S(1)}, f32[3,32,256]{2,1,0:T(8,128)S(1)}, u32[]{:S(2)}, u32[]{:S(2)}) collective-permute-start(f32[3,32,256]{2,1,0:T(8,128)S(1)} %add_add_fusion.refs_4_), channel_id=1, source_target_pairs={{16,0},{17,1},{18,2},{19,3},{68,4},{69,5},{70,6},{71,7},{24,8},{25... | collective-permute-start | bytes 294920 | tf_op jit(solution)/shard_map/ppermute | solution.py:389
  139.7 5.7 %collective-permute-start.38 = (f32[3,32,256]{2,1,0:T(8,128)S(1)}, f32[3,32,256]{2,1,0:T(8,128)S(1)}, u32[]{:S(2)}, u32[]{:S(2)}) collective-permute-start(f32[3,32,256]{2,1,0:T(8,128)S(1)} %add_add_fusion.refs_4_), channel_id=1, source_target_pairs={{24,0},{25,1},{26,2},{27,3},{100,4},{101,5},{102,6},{103,7},{0,8},... | collective-permute-start | bytes 294920 | tf_op jit(solution)/shard_map/ppermute | solution.py:389
  145.5 22.8 %collective-permute-start.39 = (f32[4,3,32,256]{3,2,1,0:T(8,128)S(1)}, f32[4,3,32,256]{3,2,1,0:T(8,128)S(1)}, u32[]{:S(2)}, u32[]{:S(2)}) collective-permute-start(f32[4,3,32,256]{3,2,1,0:T(8,128)S(1)} %pad_maximum_fusion.1), channel_id=1, source_target_pairs={{4,0},{5,1},{6,2},{7,3},{0,4},{1,5},{2,6},{3,7},{12,8},{13,9},{14,... | collective-permute-start | bytes 1179656 | tf_op jit(solution)/shard_map/ppermute | solution.py:389
  151.3 13.3 %collective-permute-start.23 = (f32[256,256]{1,0:T(8,128)S(1)}, f32[256,256]{1,0:T(8,128)S(1)}, u32[]{:S(2)}, u32[]{:S(2)}) collective-permute-start(f32[256,256]{1,0:T(8,128)S(1)} %get-tuple-element.41.refs_0_), channel_id=1, source_target_pairs={{1,0},{2,1},{3,2},{0,3},{5,4},{6,5},{7,6},{4,7},{9,8},{10,9},{11,1... | collective-permute-start | bytes 786440 | tf_op jit(solution)/shard_map/ppermute | solution.py:389
  153.5 11.1 %collective-permute-start.24 = (f32[256,256]{1,0:T(8,128)S(1)}, f32[256,256]{1,0:T(8,128)S(1)}, u32[]{:S(2)}, u32[]{:S(2)}) collective-permute-start(f32[256,256]{1,0:T(8,128)S(1)} %get-tuple-element.41.refs_0_), channel_id=1, source_target_pairs={{2,0},{3,1},{0,2},{1,3},{6,4},{7,5},{4,6},{5,7},{10,8},{11,9},{8,1... | collective-permute-start | bytes 786440 | tf_op jit(solution)/shard_map/ppermute | solution.py:389
  153.5 14.8 %collective-permute-start.25 = (f32[256,256]{1,0:T(8,128)S(1)}, f32[256,256]{1,0:T(8,128)S(1)}, u32[]{:S(2)}, u32[]{:S(2)}) collective-permute-start(f32[256,256]{1,0:T(8,128)S(1)} %get-tuple-element.41.refs_0_), channel_id=1, source_target_pairs={{3,0},{0,1},{1,2},{2,3},{7,4},{4,5},{5,6},{6,7},{11,8},{8,9},{9,10... | collective-permute-start | bytes 786440 | tf_op jit(solution)/shard_map/ppermute | solution.py:389
  (11 other events, 84.1 us)

commit v6 on v5

--- a/solution.py
+++ b/solution.py
@@ -156,7 +156,7 @@
             pltpu.VMEM((SROWS, 8), F32),
         ],
         compiler_params=pltpu.CompilerParams(vmem_limit_bytes=5 << 20),
-    )(*inside(*sin))
+    )(pltpu.with_memory_space_constraint(sin[0], pltpu.HBM), *inside(*sin[1:]))
 
 
 def sketch_kernel(m, last, *refs):
@@ -165,7 +165,7 @@
     omc, srow, scnt = refs[:3]
     refs = refs[3:]
     if last:
-        earlier, refs = refs[:3], refs[3:]
+        earlier, refs = refs[0], refs[1:]
     youts, refs = refs[:m], refs[m:]
     if last:
         zouts, refs = refs[:2], refs[2:]
@@ -245,9 +245,7 @@
         soff = offsets([first_lane(scnt[k:k + 1, :]) for k in range(NS)])
         for k in range(NS):
             rows = pl.ds(soff[k], SCAP)
-            total = zc[rows, :] + earlier[2][rows, :]
-            total = total + (earlier[0][rows, :] + earlier[1][rows, :])
-            zouts[k // YN][k % YN] = total
+            zouts[k // YN][k % YN] = zc[rows, :] + earlier[rows, :]
 
 
 def sketch(tin, src, earlier=None):
@@ -259,7 +257,7 @@
     zhalf = jax.ShapeDtypeStruct((YN, SCAP, R), F32)
     zall = (SROWS, R)
     outs = [ypart] * m + ([zhalf] * CN if last else [jax.ShapeDtypeStruct(zall, F32)])
-    operands = [*tin, *src, *(earlier or ())]
+    operands = [*tin, *src] + ([earlier] if last else [])
     column = pltpu.VMEM((trows // TC, TC, 128), F32)
     scratch = [
         pltpu.VMEM((trows, R), BF16),
@@ -422,15 +420,13 @@
     sfar = [fetch(spay, SAME["c"], 1)]
     sfar += [fetch(v, SAME["c"], 1) for v in srow[1:]]
     src = sources([*srow, *sfar])
-    y0, za = sketch(tin[0:1], src)
-    y1, zb = sketch(tin[1:2], src)
-    y3, zd = sketch(tin[3:4], src)
-    y2, z0, z1 = sketch(tin[2:3], src, (za, zb, zd))
+    y0, y3, za = sketch([tin[0], tin[3]], src)
+    y2, y1, z0, z1 = sketch([tin[2], tin[1]], src, za)
     ys = [y0, y1, y2, y3]
     zfar = give(z1, SAME["c"], 1)
-    ys[1] = give(ys[1], LAST, 1)
     ys[3] = give(ys[3], LAST, 3)
     ys[2] = give(ys[2], LAST, 2)
+    ys[1] = give(ys[1], LAST, 1)
     zmine = [z0[d] + zfar[d] for d in range(YN)]
     zs = returned(zmine, SAME["y"])
     ys = [(ys[0][d] + ys[1][d]) + (ys[2][d] + ys[3][d]) for d in range(ZN)]

time: 170 us -> 170 us (level)
  waiting for transfers between devices: 78.7 us -> 81 us
    ppermute x13, waiting for transfers between devices: 43.1 us -> 45.7 us  [give(): return lax.ppermute(v, ALL, shifted(axes, d))]
    pallas_call x4 -> x2, Pallas kernels: 17.1 us -> 15.1 us  [sketch(): pl.pallas_call(functools.partial(sketch_kernel, m, last), out_shape=tuple...]
  transfers between devices with their start and end apart: 40 -> 40, of which waited for: 26 -> 26; matrix products, arithmetic and copies ran while one was open for 1% -> 1% of each run, Pallas kernels for 8% -> 6%
where the time goes in v6:
time: 170 us; the launch traced here: 169 us
  waiting for transfers between devices  81 us (48%)
  starting transfers between devices  60.7 us (36%)
  Pallas kernels  23.4 us (14%)
  between operations  2.04 us (1%)
  other arithmetic  1.76 us (1%)
    ppermute x13, waiting for transfers between devices, give(): return lax.ppermute(v, ALL, shifted(axes, d))  45.7 us
    ppermute x27, starting transfers between devices, fetch(): return lax.ppermute(v, ALL, [(b, a) for a, b in shifted(axes, d)])  39.6 us
    ppermute x27, waiting for transfers between devices, fetch(): return lax.ppermute(v, ALL, [(b, a) for a, b in shifted(axes, d)])  35.3 us
    ppermute x13, starting transfers between devices, give(): return lax.ppermute(v, ALL, shifted(axes, d))  21 us
    pallas_call x2, Pallas kernels, sketch(): pl.pallas_call(functools.partial(sketch_kernel, m, last), out_shape=tuple...  15.1 us
  transfers between devices with their start and end apart: 40, of which 26 were waited for; matrix products, arithmetic and copies ran while one was open for 1% of the time, Pallas kernels for 6%

profile of v6, /device:TPU:1, one launch (start us, length us, event | category | flops | bytes accessed | tf_op | source)
XLA Modules:
  0.0 169.5 jit_solution(3106037208873302465)
XLA Ops:
  2.5 2.2 %shard_map.101 = (bf16[288,256]{1,0:T(8,128)(2,1)}, bf16[576,256]{1,0:T(8,128)(2,1)}) custom-call(s32[6]{0:T(128)} %stack.49.where_ref.refs_0_, f32[3,1024]{1,0:T(4,128)} %txyz_ref.1, f32[3,512]{1,0:T(4,128)} %sxyz_ref.1, bf16[1024,256]{1,0:T(8,128)(2,1)} %psi_ref.1, bf16[512,256]{1,0:T(8,128)(2,1)} %omega_ref.1), custom_call_target="tpu_custom_call" | custom-call | tf_op jit(solution)/shard_map/pallas_call | solution.py:82
  4.7 2.1 %collective-permute-start.6 = (bf16[576,256]{1,0:T(8,128)(2,1)}, bf16[576,256]{1,0:T(8,128)(2,1)S(1)}, u32[]{:S(2)}, u32[]{:S(2)}) collective-permute-start(bf16[576,256]{1,0:T(8,128)(2,1)} %get-tuple-element.26.refs_0_), channel_id=1, source_target_pairs={{3,0},{0,1},{1,2},{2,3},{7,4},{4,5},{5,6},{6,7},{11,8},{8,9},{9,10... | collective-permute-start | bytes 884744 | tf_op jit(solution)/shard_map/ppermute | solution.py:387
  6.8 3.8 %collective-permute-start = (bf16[288,256]{1,0:T(8,128)(2,1)}, bf16[288,256]{1,0:T(8,128)(2,1)S(1)}, u32[]{:S(2)}, u32[]{:S(2)}) collective-permute-start(bf16[288,256]{1,0:T(8,128)(2,1)} %get-tuple-element.25.refs_9_), channel_id=1, source_target_pairs={{8,0},{9,1},{10,2},{11,3},{36,4},{37,5},{38,6},{39,7},{16,8},{17,9... | collective-permute-start | bytes 442376 | tf_op jit(solution)/shard_map/ppermute | solution.py:387
  12.0 1.6 collective-permute-start.5
  14.4 5.3 %collective-permute-done.1 = bf16[288,256]{1,0:T(8,128)(2,1)S(1)} collective-permute-done((bf16[288,256]{1,0:T(8,128)(2,1)}, bf16[288,256]{1,0:T(8,128)(2,1)S(1)}, u32[]{:S(2)}, u32[]{:S(2)}) %collective-permute-start.1) | collective-permute-done | bytes 147488 | tf_op jit(solution)/shard_map/ppermute | solution.py:387
  23.2 2.5 %collective-permute-start.11 = (bf16[4,288,256]{2,1,0:T(8,128)(2,1)S(1)}, bf16[4,288,256]{2,1,0:T(8,128)(2,1)S(1)}, u32[]{:S(2)}, u32[]{:S(2)}) collective-permute-start(bf16[4,288,256]{2,1,0:T(8,128)(2,1)S(1)} %pad_maximum_fusion.refs_0_), channel_id=1, source_target_pairs={{64,0},{65,1},{66,2},{67,3},{20,4},{21,5},{22,6},{23,7},{72,8},{73... | collective-permute-start | bytes 1769480 | tf_op jit(solution)/shard_map/ppermute | solution.py:387
  26.9 3.4 %collective-permute-start.8 = (bf16[576,256]{1,0:T(8,128)(2,1)S(1)}, bf16[576,256]{1,0:T(8,128)(2,1)S(1)}, u32[]{:S(2)}, u32[]{:S(2)}) collective-permute-start(bf16[576,256]{1,0:T(8,128)(2,1)S(1)} %collective-permute-done.4.refs_1_), channel_id=1, source_target_pairs={{4,0},{5,1},{6,2},{7,3},{0,4},{1,5},{2,6},{3,7},{12,8},{13,9},{14,... | collective-permute-start | bytes 884744 | tf_op jit(solution)/shard_map/ppermute | solution.py:387
  31.8 2.1 %shard_map.102 = (bf16[5120,256]{1,0:T(8,128)(2,1)S(1)}, f32[10,8,512]{2,1,0:T(8,128)S(1)}, f32[16,128]{1,0:T(8,128)S(1)}) custom-call(bf16[576,256]{1,0:T(8,128)(2,1)} %get-tuple-element.26.refs_0_, bf16[576,256]{1,0:T(8,128)(2,1)S(1)} %collective-permute-done.4.refs_1_, bf16[576,256]{1,0:T(8,128)(2,1)S(1)} %collective-permute-done.5.refs_2_, ...), custom_call_target="tpu_custom_call" | custom-call | tf_op jit(solution)/shard_map/pallas_call | solution.py:146
  34.0 7.3 %shard_map.103 = (f32[4,256,256]{2,1,0:T(8,128)S(1)}, f32[4,256,256]{2,1,0:T(8,128)S(1)}, f32[5120,256]{1,0:T(8,128)S(1)}) custom-call(bf16[4,288,256]{2,1,0:T(8,128)(2,1)S(1)} %pad_maximum_fusion.refs_0_, bf16[4,288,256]{2,1,0:T(8,128)(2,1)S(1)} %collective-permute-done.3.refs_1_, bf16[5120,256]{1,0:T(8,128)(2,1)S(1)} %get-tuple-element.27.refs_2_, ...), custom_call_target="tpu_custom_call" | custom-call | tf_op jit(solution)/shard_map/pallas_call | solution.py:272
  41.3 7.8 %shard_map.104 = (f32[4,256,256]{2,1,0:T(8,128)S(1)}, f32[4,256,256]{2,1,0:T(8,128)S(1)}, f32[4,512,256]{2,1,0:T(8,128)S(1)}, f32[4,512,256]{2,1,0:T(8,128)S(1)}) custom-call(bf16[4,288,256]{2,1,0:T(8,128)(2,1)S(1)} %collective-permute-done.11.refs_0_, bf16[4,288,256]{2,1,0:T(8,128)(2,1)S(1)} %collective-permute-done.12.refs_1_, ...), custom_call_target="tpu_custom_call" | custom-call | tf_op jit(solution)/shard_map/pallas_call | solution.py:272
  50.4 1.9 %collective-permute-start.15 = (f32[4,256,256]{2,1,0:T(8,128)S(1)}, f32[4,256,256]{2,1,0:T(8,128)S(1)}, u32[]{:S(2)}, u32[]{:S(2)}) collective-permute-start(f32[4,256,256]{2,1,0:T(8,128)S(1)} %get-tuple-element.34), channel_id=1, source_target_pairs={{0,96},{1,97},{2,98},{3,99},{4,28},{5,29},{6,30},{7,31},{8,104},{9... | collective-permute-start | bytes 3145736 | tf_op jit(solution)/shard_map/ppermute | solution.py:391
  52.3 23.7 %collective-permute-done.13 = f32[4,256,256]{2,1,0:T(8,128)S(1)} collective-permute-done((f32[4,256,256]{2,1,0:T(8,128)S(1)}, f32[4,256,256]{2,1,0:T(8,128)S(1)}, u32[]{:S(2)}, u32[]{:S(2)}) %collective-permute-start.13) | collective-permute-done | bytes 1048608 | tf_op jit(solution)/shard_map/ppermute | solution.py:391
  77.0 5.8 %collective-permute-start.16 = (f32[256,256]{1,0:T(8,128)S(1)}, f32[256,256]{1,0:T(8,128)S(1)}, u32[]{:S(2)}, u32[]{:S(2)}) collective-permute-start(f32[256,256]{1,0:T(8,128)S(1)} %get-tuple-element.51), channel_id=1, source_target_pairs={{0,8},{1,9},{2,10},{3,11},{4,36},{5,37},{6,38},{7,39},{8,16},{9,17... | collective-permute-start | bytes 786440 | tf_op jit(solution)/shard_map/ppermute | solution.py:391
  86.3 3.3 %collective-permute-start.17 = (f32[256,256]{1,0:T(8,128)S(1)}, f32[256,256]{1,0:T(8,128)S(1)}, u32[]{:S(2)}, u32[]{:S(2)}) collective-permute-start(f32[256,256]{1,0:T(8,128)S(1)} %get-tuple-element.50), channel_id=1, source_target_pairs={{0,16},{1,17},{2,18},{3,19},{4,68},{5,69},{6,70},{7,71},{8,24},{9,... | collective-permute-start | bytes 786440 | tf_op jit(solution)/shard_map/ppermute | solution.py:391
  90.9 2.8 %collective-permute-done.17.refs_3_ = f32[256,256]{1,0:T(8,128)S(1)} collective-permute-done((f32[256,256]{1,0:T(8,128)S(1)}, f32[256,256]{1,0:T(8,128)S(1)}, u32[]{:S(2)}, u32[]{:S(2)}) %collective-permute-start.17) | collective-permute-done | bytes 262176 | tf_op jit(solution)/shard_map/ppermute | solution.py:391
  93.7 2.2 %collective-permute-done.18.refs_4_ = f32[256,256]{1,0:T(8,128)S(1)} collective-permute-done((f32[256,256]{1,0:T(8,128)S(1)}, f32[256,256]{1,0:T(8,128)S(1)}, u32[]{:S(2)}, u32[]{:S(2)}) %collective-permute-start.18) | collective-permute-done | bytes 262176 | tf_op jit(solution)/shard_map/ppermute | solution.py:391
  96.9 9.8 %collective-permute-done.21.refs_7_ = f32[512,256]{1,0:T(8,128)S(1)} collective-permute-done((f32[512,256]{1,0:T(8,128)S(1)}, f32[512,256]{1,0:T(8,128)S(1)}, u32[]{:S(2)}, u32[]{:S(2)}) %collective-permute-start.21) | collective-permute-done | bytes 524320 | tf_op jit(solution)/shard_map/ppermute | solution.py:391
  106.8 2.2 %collective-permute-done.22.refs_8_ = f32[512,256]{1,0:T(8,128)S(1)} collective-permute-done((f32[512,256]{1,0:T(8,128)S(1)}, f32[512,256]{1,0:T(8,128)S(1)}, u32[]{:S(2)}, u32[]{:S(2)}) %collective-permute-start.22) | collective-permute-done | bytes 524320 | tf_op jit(solution)/shard_map/ppermute | solution.py:391
  109.0 2.0 %shard_map.105 = (f32[256,256]{1,0:T(8,128)S(1)}, f32[512,256]{1,0:T(8,128)}, f32[3,128,256]{2,1,0:T(8,128)S(1)}, f32[3,128,256]{2,1,0:T(8,128)S(1)}) custom-call(s32[6]{0:T(128)S(1)} %copy-done.1, f32[256,256]{1,0:T(8,128)S(1)} %get-tuple-element.52.refs_1_, f32[256,256]{1,0:T(8,128)S(1)} %collective-permute-done.16.refs_2_, ...), custom_call_target="tpu_custom_call" | custom-call | tf_op jit(solution)/shard_map/pallas_call | solution.py:318
  114.2 3.6 %collective-permute-start.28 = (f32[3,32,256]{2,1,0:T(8,128)S(1)}, f32[3,32,256]{2,1,0:T(8,128)S(1)}, u32[]{:S(2)}, u32[]{:S(2)}) collective-permute-start(f32[3,32,256]{2,1,0:T(8,128)S(1)} %get-tuple-element.54), channel_id=1, source_target_pairs={{0,16},{1,17},{2,18},{3,19},{4,68},{5,69},{6,70},{7,71},{8,24},{9,... | collective-permute-start | bytes 294920 | tf_op jit(solution)/shard_map/ppermute | solution.py:391
  119.1 2.0 %collective-permute-done.28 = f32[3,32,256]{2,1,0:T(8,128)S(1)} collective-permute-done((f32[3,32,256]{2,1,0:T(8,128)S(1)}, f32[3,32,256]{2,1,0:T(8,128)S(1)}, u32[]{:S(2)}, u32[]{:S(2)}) %collective-permute-start.28) | collective-permute-done | bytes 98336 | tf_op jit(solution)/shard_map/ppermute | solution.py:391
  124.0 2.6 %collective-permute-done.30 = f32[3,32,256]{2,1,0:T(8,128)S(1)} collective-permute-done((f32[3,32,256]{2,1,0:T(8,128)S(1)}, f32[3,32,256]{2,1,0:T(8,128)S(1)}, u32[]{:S(2)}, u32[]{:S(2)}) %collective-permute-start.30) | collective-permute-done | bytes 98336 | tf_op jit(solution)/shard_map/ppermute | solution.py:387
  128.6 1.9 %collective-permute-start.33 = (f32[3,32,256]{2,1,0:T(8,128)S(1)}, f32[3,32,256]{2,1,0:T(8,128)S(1)}, u32[]{:S(2)}, u32[]{:S(2)}) collective-permute-start(f32[3,32,256]{2,1,0:T(8,128)S(1)} %add_add_fusion.1), channel_id=1, source_target_pairs={{2,0},{3,1},{0,2},{1,3},{6,4},{7,5},{4,6},{5,7},{10,8},{11,9},{8,1... | collective-permute-start | bytes 294920 | tf_op jit(solution)/shard_map/ppermute | solution.py:387
  132.0 1.7 collective-permute-done.33
  134.7 1.6 collective-permute-done.35
  136.4 3.2 %collective-permute-start.36 = (f32[3,32,256]{2,1,0:T(8,128)S(1)}, f32[3,32,256]{2,1,0:T(8,128)S(1)}, u32[]{:S(2)}, u32[]{:S(2)}) collective-permute-start(f32[3,32,256]{2,1,0:T(8,128)S(1)} %add_add_fusion.refs_4_), channel_id=1, source_target_pairs={{8,0},{9,1},{10,2},{11,3},{36,4},{37,5},{38,6},{39,7},{16,8},{17,9... | collective-permute-start | bytes 294920 | tf_op jit(solution)/shard_map/ppermute | solution.py:387
  141.2 3.4 %collective-permute-done.37.refs_6_ = f32[3,32,256]{2,1,0:T(8,128)S(1)} collective-permute-done((f32[3,32,256]{2,1,0:T(8,128)S(1)}, f32[3,32,256]{2,1,0:T(8,128)S(1)}, u32[]{:S(2)}, u32[]{:S(2)}) %collective-permute-start.37) | collective-permute-done | bytes 98336 | tf_op jit(solution)/shard_map/ppermute | solution.py:387
  145.6 6.6 %collective-permute-start.39 = (f32[4,3,32,256]{3,2,1,0:T(8,128)S(1)}, f32[4,3,32,256]{3,2,1,0:T(8,128)S(1)}, u32[]{:S(2)}, u32[]{:S(2)}) collective-permute-start(f32[4,3,32,256]{3,2,1,0:T(8,128)S(1)} %pad_maximum_fusion.1), channel_id=1, source_target_pairs={{4,0},{5,1},{6,2},{7,3},{0,4},{1,5},{2,6},{3,7},{12,8},{13,9},{14,... | collective-permute-start | bytes 1179656 | tf_op jit(solution)/shard_map/ppermute | solution.py:387
  152.2 1.8 %collective-permute-start.24 = (f32[256,256]{1,0:T(8,128)S(1)}, f32[256,256]{1,0:T(8,128)S(1)}, u32[]{:S(2)}, u32[]{:S(2)}) collective-permute-start(f32[256,256]{1,0:T(8,128)S(1)} %get-tuple-element.37.refs_0_), channel_id=1, source_target_pairs={{2,0},{3,1},{0,2},{1,3},{6,4},{7,5},{4,6},{5,7},{10,8},{11,9},{8,1... | collective-permute-start | bytes 786440 | tf_op jit(solution)/shard_map/ppermute | solution.py:387
  154.0 6.0 %collective-permute-done.23.refs_1_ = f32[256,256]{1,0:T(8,128)S(1)} collective-permute-done((f32[256,256]{1,0:T(8,128)S(1)}, f32[256,256]{1,0:T(8,128)S(1)}, u32[]{:S(2)}, u32[]{:S(2)}) %collective-permute-start.23) | collective-permute-done | bytes 262176 | tf_op jit(solution)/shard_map/ppermute | solution.py:387
  161.4 6.1 %collective-permute-done.25.refs_3_ = f32[256,256]{1,0:T(8,128)S(1)} collective-permute-done((f32[256,256]{1,0:T(8,128)S(1)}, f32[256,256]{1,0:T(8,128)S(1)}, u32[]{:S(2)}, u32[]{:S(2)}) %collective-permute-start.25) | collective-permute-done | bytes 262176 | tf_op jit(solution)/shard_map/ppermute | solution.py:387
  167.5 1.9 %shard_map.106 = (f32[1024,256]{1,0:T(8,128)}, f32[256,256]{1,0:T(8,128)}, f32[256,256]{1,0:T(8,128)}, f32[256,256]{1,0:T(8,128)}) custom-call(s32[6]{0:T(128)S(1)} %copy-done.1, f32[256,256]{1,0:T(8,128)S(1)} %get-tuple-element.37.refs_0_, f32[256,256]{1,0:T(8,128)S(1)} %collective-permute-done.23.refs_1_, f32[256,256]{1,0:T(8,128)S(1)} %collective-permute-done.24.refs_2_, ...), custom_call_target="tpu_custom_call" | custom-call | tf_op jit(solution)/shard_map/pallas_call | solution.py:354
  (68 shorter events, 33.0 us)
Async XLA Ops:
  4.7 16.4 %collective-permute-start.6 = (bf16[576,256]{1,0:T(8,128)(2,1)}, bf16[576,256]{1,0:T(8,128)(2,1)S(1)}, u32[]{:S(2)}, u32[]{:S(2)}) collective-permute-start(bf16[576,256]{1,0:T(8,128)(2,1)} %get-tuple-element.26.refs_0_), channel_id=1, source_target_pairs={{3,0},{0,1},{1,2},{2,3},{7,4},{4,5},{5,6},{6,7},{11,8},{8,9},{9,10... | collective-permute-start | bytes 884744 | tf_op jit(solution)/shard_map/ppermute | solution.py:387
  6.8 6.8 %collective-permute-start = (bf16[288,256]{1,0:T(8,128)(2,1)}, bf16[288,256]{1,0:T(8,128)(2,1)S(1)}, u32[]{:S(2)}, u32[]{:S(2)}) collective-permute-start(bf16[288,256]{1,0:T(8,128)(2,1)} %get-tuple-element.25.refs_9_), channel_id=1, source_target_pairs={{8,0},{9,1},{10,2},{11,3},{36,4},{37,5},{38,6},{39,7},{16,8},{17,9... | collective-permute-start | bytes 442376 | tf_op jit(solution)/shard_map/ppermute | solution.py:387
  10.6 12.7 %collective-permute-start.4 = (bf16[576,256]{1,0:T(8,128)(2,1)}, bf16[576,256]{1,0:T(8,128)(2,1)S(1)}, u32[]{:S(2)}, u32[]{:S(2)}) collective-permute-start(bf16[576,256]{1,0:T(8,128)(2,1)} %get-tuple-element.26.refs_0_), channel_id=1, source_target_pairs={{1,0},{2,1},{3,2},{0,3},{5,4},{6,5},{7,6},{4,7},{9,8},{10,9},{11,1... | collective-permute-start | bytes 884744 | tf_op jit(solution)/shard_map/ppermute | solution.py:387
  12.0 13.7 %collective-permute-start.5 = (bf16[576,256]{1,0:T(8,128)(2,1)}, bf16[576,256]{1,0:T(8,128)(2,1)S(1)}, u32[]{:S(2)}, u32[]{:S(2)}) collective-permute-start(bf16[576,256]{1,0:T(8,128)(2,1)} %get-tuple-element.26.refs_0_), channel_id=1, source_target_pairs={{2,0},{3,1},{0,2},{1,3},{6,4},{7,5},{4,6},{5,7},{10,8},{11,9},{8,1... | collective-permute-start | bytes 884744 | tf_op jit(solution)/shard_map/ppermute | solution.py:387
  13.7 6.1 %collective-permute-start.1 = (bf16[288,256]{1,0:T(8,128)(2,1)}, bf16[288,256]{1,0:T(8,128)(2,1)S(1)}, u32[]{:S(2)}, u32[]{:S(2)}) collective-permute-start(bf16[288,256]{1,0:T(8,128)(2,1)} %get-tuple-element.25.refs_9_), channel_id=1, source_target_pairs={{16,0},{17,1},{18,2},{19,3},{68,4},{69,5},{70,6},{71,7},{24,8},{25... | collective-permute-start | bytes 442376 | tf_op jit(solution)/shard_map/ppermute | solution.py:387
  13.7 7.5 %collective-permute-start.2 = (bf16[288,256]{1,0:T(8,128)(2,1)}, bf16[288,256]{1,0:T(8,128)(2,1)S(1)}, u32[]{:S(2)}, u32[]{:S(2)}) collective-permute-start(bf16[288,256]{1,0:T(8,128)(2,1)} %get-tuple-element.25.refs_9_), channel_id=1, source_target_pairs={{24,0},{25,1},{26,2},{27,3},{100,4},{101,5},{102,6},{103,7},{0,8},... | collective-permute-start | bytes 442376 | tf_op jit(solution)/shard_map/ppermute | solution.py:387
  19.7 7.1 %collective-permute-start.7 = (bf16[576,256]{1,0:T(8,128)(2,1)}, bf16[576,256]{1,0:T(8,128)(2,1)S(1)}, u32[]{:S(2)}, u32[]{:S(2)}) collective-permute-start(bf16[576,256]{1,0:T(8,128)(2,1)} %get-tuple-element.26.refs_0_), channel_id=1, source_target_pairs={{4,0},{5,1},{6,2},{7,3},{0,4},{1,5},{2,6},{3,7},{12,8},{13,9},{14,... | collective-permute-start | bytes 884744 | tf_op jit(solution)/shard_map/ppermute | solution.py:387
  21.2 9.1 %collective-permute-start.10 = (bf16[576,256]{1,0:T(8,128)(2,1)S(1)}, bf16[576,256]{1,0:T(8,128)(2,1)S(1)}, u32[]{:S(2)}, u32[]{:S(2)}) collective-permute-start(bf16[576,256]{1,0:T(8,128)(2,1)S(1)} %collective-permute-done.6.refs_3_), channel_id=1, source_target_pairs={{4,0},{5,1},{6,2},{7,3},{0,4},{1,5},{2,6},{3,7},{12,8},{13,9},{14,... | collective-permute-start | bytes 884744 | tf_op jit(solution)/shard_map/ppermute | solution.py:387
  22.2 11.8 %collective-permute-start.3 = (bf16[4,288,256]{2,1,0:T(8,128)(2,1)S(1)}, bf16[4,288,256]{2,1,0:T(8,128)(2,1)S(1)}, u32[]{:S(2)}, u32[]{:S(2)}) collective-permute-start(bf16[4,288,256]{2,1,0:T(8,128)(2,1)S(1)} %pad_maximum_fusion.refs_0_), channel_id=1, source_target_pairs={{96,0},{97,1},{98,2},{99,3},{28,4},{29,5},{30,6},{31,7},{104,8},{1... | collective-permute-start | bytes 1769480 | tf_op jit(solution)/shard_map/ppermute | solution.py:387
  23.2 18.1 %collective-permute-start.11 = (bf16[4,288,256]{2,1,0:T(8,128)(2,1)S(1)}, bf16[4,288,256]{2,1,0:T(8,128)(2,1)S(1)}, u32[]{:S(2)}, u32[]{:S(2)}) collective-permute-start(bf16[4,288,256]{2,1,0:T(8,128)(2,1)S(1)} %pad_maximum_fusion.refs_0_), channel_id=1, source_target_pairs={{64,0},{65,1},{66,2},{67,3},{20,4},{21,5},{22,6},{23,7},{72,8},{73... | collective-permute-start | bytes 1769480 | tf_op jit(solution)/shard_map/ppermute | solution.py:387
  25.7 15.6 %collective-permute-start.12 = (bf16[4,288,256]{2,1,0:T(8,128)(2,1)S(1)}, bf16[4,288,256]{2,1,0:T(8,128)(2,1)S(1)}, u32[]{:S(2)}, u32[]{:S(2)}) collective-permute-start(bf16[4,288,256]{2,1,0:T(8,128)(2,1)S(1)} %pad_maximum_fusion.refs_0_), channel_id=1, source_target_pairs={{32,0},{33,1},{34,2},{35,3},{12,4},{13,5},{14,6},{15,7},{40,8},{41... | collective-permute-start | bytes 1769480 | tf_op jit(solution)/shard_map/ppermute | solution.py:387
  49.1 33.7 %collective-permute-start.19 = (f32[4,512,256]{2,1,0:T(8,128)S(1)}, f32[4,512,256]{2,1,0:T(8,128)S(1)}, u32[]{:S(2)}, u32[]{:S(2)}) collective-permute-start(f32[4,512,256]{2,1,0:T(8,128)S(1)} %get-tuple-element.36), channel_id=1, source_target_pairs={{0,4},{1,5},{2,6},{3,7},{4,0},{5,1},{6,2},{7,3},{8,12},{9,13},{10,... | collective-permute-start | bytes 6291464 | tf_op jit(solution)/shard_map/ppermute | solution.py:391
  49.7 26.4 %collective-permute-start.13 = (f32[4,256,256]{2,1,0:T(8,128)S(1)}, f32[4,256,256]{2,1,0:T(8,128)S(1)}, u32[]{:S(2)}, u32[]{:S(2)}) collective-permute-start(f32[4,256,256]{2,1,0:T(8,128)S(1)} %get-tuple-element.32), channel_id=1, source_target_pairs={{0,32},{1,33},{2,34},{3,35},{4,12},{5,13},{6,14},{7,15},{8,40},{9,... | collective-permute-start | bytes 3145736 | tf_op jit(solution)/shard_map/ppermute | solution.py:391
  49.7 26.4 %collective-permute-start.14 = (f32[4,256,256]{2,1,0:T(8,128)S(1)}, f32[4,256,256]{2,1,0:T(8,128)S(1)}, u32[]{:S(2)}, u32[]{:S(2)}) collective-permute-start(f32[4,256,256]{2,1,0:T(8,128)S(1)} %get-tuple-element.33), channel_id=1, source_target_pairs={{0,64},{1,65},{2,66},{3,67},{4,20},{5,21},{6,22},{7,23},{8,72},{9,... | collective-permute-start | bytes 3145736 | tf_op jit(solution)/shard_map/ppermute | solution.py:391
  50.4 26.3 %collective-permute-start.15 = (f32[4,256,256]{2,1,0:T(8,128)S(1)}, f32[4,256,256]{2,1,0:T(8,128)S(1)}, u32[]{:S(2)}, u32[]{:S(2)}) collective-permute-start(f32[4,256,256]{2,1,0:T(8,128)S(1)} %get-tuple-element.34), channel_id=1, source_target_pairs={{0,96},{1,97},{2,98},{3,99},{4,28},{5,29},{6,30},{7,31},{8,104},{9... | collective-permute-start | bytes 3145736 | tf_op jit(solution)/shard_map/ppermute | solution.py:391
  77.0 12.6 %collective-permute-start.16 = (f32[256,256]{1,0:T(8,128)S(1)}, f32[256,256]{1,0:T(8,128)S(1)}, u32[]{:S(2)}, u32[]{:S(2)}) collective-permute-start(f32[256,256]{1,0:T(8,128)S(1)} %get-tuple-element.51), channel_id=1, source_target_pairs={{0,8},{1,9},{2,10},{3,11},{4,36},{5,37},{6,38},{7,39},{8,16},{9,17... | collective-permute-start | bytes 786440 | tf_op jit(solution)/shard_map/ppermute | solution.py:391
  83.1 13.8 %collective-permute-start.20 = (f32[512,256]{1,0:T(8,128)S(1)}, f32[512,256]{1,0:T(8,128)S(1)}, u32[]{:S(2)}, u32[]{:S(2)}) collective-permute-start(f32[512,256]{1,0:T(8,128)S(1)} %get-tuple-element.47), channel_id=1, source_target_pairs={{0,1},{1,2},{2,3},{3,0},{4,5},{5,6},{6,7},{7,4},{8,9},{9,10},{10,1... | collective-permute-start | bytes 1572872 | tf_op jit(solution)/shard_map/ppermute | solution.py:391
  83.6 23.2 %collective-permute-start.21 = (f32[512,256]{1,0:T(8,128)S(1)}, f32[512,256]{1,0:T(8,128)S(1)}, u32[]{:S(2)}, u32[]{:S(2)}) collective-permute-start(f32[512,256]{1,0:T(8,128)S(1)} %get-tuple-element.46), channel_id=1, source_target_pairs={{0,2},{1,3},{2,0},{3,1},{4,6},{5,7},{6,4},{7,5},{8,10},{9,11},{10,... | collective-permute-start | bytes 1572872 | tf_op jit(solution)/shard_map/ppermute | solution.py:391
  85.1 23.9 %collective-permute-start.22 = (f32[512,256]{1,0:T(8,128)S(1)}, f32[512,256]{1,0:T(8,128)S(1)}, u32[]{:S(2)}, u32[]{:S(2)}) collective-permute-start(f32[512,256]{1,0:T(8,128)S(1)} %get-tuple-element.45), channel_id=1, source_target_pairs={{0,3},{1,0},{2,1},{3,2},{4,7},{5,4},{6,5},{7,6},{8,11},{9,8},{10,9... | collective-permute-start | bytes 1572872 | tf_op jit(solution)/shard_map/ppermute | solution.py:391
  86.3 7.4 %collective-permute-start.17 = (f32[256,256]{1,0:T(8,128)S(1)}, f32[256,256]{1,0:T(8,128)S(1)}, u32[]{:S(2)}, u32[]{:S(2)}) collective-permute-start(f32[256,256]{1,0:T(8,128)S(1)} %get-tuple-element.50), channel_id=1, source_target_pairs={{0,16},{1,17},{2,18},{3,19},{4,68},{5,69},{6,70},{7,71},{8,24},{9,... | collective-permute-start | bytes 786440 | tf_op jit(solution)/shard_map/ppermute | solution.py:391
  89.7 6.3 %collective-permute-start.18 = (f32[256,256]{1,0:T(8,128)S(1)}, f32[256,256]{1,0:T(8,128)S(1)}, u32[]{:S(2)}, u32[]{:S(2)}) collective-permute-start(f32[256,256]{1,0:T(8,128)S(1)} %get-tuple-element.49), channel_id=1, source_target_pairs={{0,24},{1,25},{2,26},{3,27},{4,100},{5,101},{6,102},{7,103},{8,0},... | collective-permute-start | bytes 786440 | tf_op jit(solution)/shard_map/ppermute | solution.py:391
  114.1 5.0 %collective-permute-start.27 = (f32[3,32,256]{2,1,0:T(8,128)S(1)}, f32[3,32,256]{2,1,0:T(8,128)S(1)}, u32[]{:S(2)}, u32[]{:S(2)}) collective-permute-start(f32[3,32,256]{2,1,0:T(8,128)S(1)} %get-tuple-element.55), channel_id=1, source_target_pairs={{0,8},{1,9},{2,10},{3,11},{4,36},{5,37},{6,38},{7,39},{8,16},{9,17... | collective-permute-start | bytes 294920 | tf_op jit(solution)/shard_map/ppermute | solution.py:391
  114.2 7.0 %collective-permute-start.28 = (f32[3,32,256]{2,1,0:T(8,128)S(1)}, f32[3,32,256]{2,1,0:T(8,128)S(1)}, u32[]{:S(2)}, u32[]{:S(2)}) collective-permute-start(f32[3,32,256]{2,1,0:T(8,128)S(1)} %get-tuple-element.54), channel_id=1, source_target_pairs={{0,16},{1,17},{2,18},{3,19},{4,68},{5,69},{6,70},{7,71},{8,24},{9,... | collective-permute-start | bytes 294920 | tf_op jit(solution)/shard_map/ppermute | solution.py:391
  121.6 5.1 %collective-permute-start.30 = (f32[3,32,256]{2,1,0:T(8,128)S(1)}, f32[3,32,256]{2,1,0:T(8,128)S(1)}, u32[]{:S(2)}, u32[]{:S(2)}) collective-permute-start(f32[3,32,256]{2,1,0:T(8,128)S(1)} %fusion.12), channel_id=1, source_target_pairs={{64,0},{65,1},{66,2},{67,3},{20,4},{21,5},{22,6},{23,7},{72,8},{73... | collective-permute-start | bytes 294920 | tf_op jit(solution)/shard_map/ppermute | solution.py:387
  122.0 5.1 %collective-permute-start.31 = (f32[3,32,256]{2,1,0:T(8,128)S(1)}, f32[3,32,256]{2,1,0:T(8,128)S(1)}, u32[]{:S(2)}, u32[]{:S(2)}) collective-permute-start(f32[3,32,256]{2,1,0:T(8,128)S(1)} %fusion.12), channel_id=1, source_target_pairs={{32,0},{33,1},{34,2},{35,3},{12,4},{13,5},{14,6},{15,7},{40,8},{41... | collective-permute-start | bytes 294920 | tf_op jit(solution)/shard_map/ppermute | solution.py:387
  123.6 5.0 %collective-permute-start.32 = (f32[3,32,256]{2,1,0:T(8,128)S(1)}, f32[3,32,256]{2,1,0:T(8,128)S(1)}, u32[]{:S(2)}, u32[]{:S(2)}) collective-permute-start(f32[3,32,256]{2,1,0:T(8,128)S(1)} %fusion.12), channel_id=1, source_target_pairs={{96,0},{97,1},{98,2},{99,3},{28,4},{29,5},{30,6},{31,7},{104,8},{1... | collective-permute-start | bytes 294920 | tf_op jit(solution)/shard_map/ppermute | solution.py:387
  128.6 5.1 %collective-permute-start.33 = (f32[3,32,256]{2,1,0:T(8,128)S(1)}, f32[3,32,256]{2,1,0:T(8,128)S(1)}, u32[]{:S(2)}, u32[]{:S(2)}) collective-permute-start(f32[3,32,256]{2,1,0:T(8,128)S(1)} %add_add_fusion.1), channel_id=1, source_target_pairs={{2,0},{3,1},{0,2},{1,3},{6,4},{7,5},{4,6},{5,7},{10,8},{11,9},{8,1... | collective-permute-start | bytes 294920 | tf_op jit(solution)/shard_map/ppermute | solution.py:387
  139.5 5.0 %collective-permute-start.37 = (f32[3,32,256]{2,1,0:T(8,128)S(1)}, f32[3,32,256]{2,1,0:T(8,128)S(1)}, u32[]{:S(2)}, u32[]{:S(2)}) collective-permute-start(f32[3,32,256]{2,1,0:T(8,128)S(1)} %add_add_fusion.refs_4_), channel_id=1, source_target_pairs={{16,0},{17,1},{18,2},{19,3},{68,4},{69,5},{70,6},{71,7},{24,8},{25... | collective-permute-start | bytes 294920 | tf_op jit(solution)/shard_map/ppermute | solution.py:387
  145.6 21.9 %collective-permute-start.39 = (f32[4,3,32,256]{3,2,1,0:T(8,128)S(1)}, f32[4,3,32,256]{3,2,1,0:T(8,128)S(1)}, u32[]{:S(2)}, u32[]{:S(2)}) collective-permute-start(f32[4,3,32,256]{3,2,1,0:T(8,128)S(1)} %pad_maximum_fusion.1), channel_id=1, source_target_pairs={{4,0},{5,1},{6,2},{7,3},{0,4},{1,5},{2,6},{3,7},{12,8},{13,9},{14,... | collective-permute-start | bytes 1179656 | tf_op jit(solution)/shard_map/ppermute | solution.py:387
  152.2 7.8 %collective-permute-start.23 = (f32[256,256]{1,0:T(8,128)S(1)}, f32[256,256]{1,0:T(8,128)S(1)}, u32[]{:S(2)}, u32[]{:S(2)}) collective-permute-start(f32[256,256]{1,0:T(8,128)S(1)} %get-tuple-element.37.refs_0_), channel_id=1, source_target_pairs={{1,0},{2,1},{3,2},{0,3},{5,4},{6,5},{7,6},{4,7},{9,8},{10,9},{11,1... | collective-permute-start | bytes 786440 | tf_op jit(solution)/shard_map/ppermute | solution.py:387
  152.2 9.2 %collective-permute-start.24 = (f32[256,256]{1,0:T(8,128)S(1)}, f32[256,256]{1,0:T(8,128)S(1)}, u32[]{:S(2)}, u32[]{:S(2)}) collective-permute-start(f32[256,256]{1,0:T(8,128)S(1)} %get-tuple-element.37.refs_0_), channel_id=1, source_target_pairs={{2,0},{3,1},{0,2},{1,3},{6,4},{7,5},{4,6},{5,7},{10,8},{11,9},{8,1... | collective-permute-start | bytes 786440 | tf_op jit(solution)/shard_map/ppermute | solution.py:387
  154.0 13.6 %collective-permute-start.25 = (f32[256,256]{1,0:T(8,128)S(1)}, f32[256,256]{1,0:T(8,128)S(1)}, u32[]{:S(2)}, u32[]{:S(2)}) collective-permute-start(f32[256,256]{1,0:T(8,128)S(1)} %get-tuple-element.37.refs_0_), channel_id=1, source_target_pairs={{3,0},{0,1},{1,2},{2,3},{7,4},{4,5},{5,6},{6,7},{11,8},{8,9},{9,10... | collective-permute-start | bytes 786440 | tf_op jit(solution)/shard_map/ppermute | solution.py:387
  (10 other events, 83.9 us)

commit v7 on v5

--- a/solution.py
+++ b/solution.py
@@ -156,7 +156,7 @@
             pltpu.VMEM((SROWS, 8), F32),
         ],
         compiler_params=pltpu.CompilerParams(vmem_limit_bytes=5 << 20),
-    )(*inside(*sin))
+    )(pltpu.with_memory_space_constraint(sin[0], pltpu.HBM), *inside(*sin[1:]))
 
 
 def sketch_kernel(m, last, *refs):
@@ -332,8 +332,8 @@
 
 
 def place_kernel(where_ref, *refs):
-    ys, own, other = refs[0:YN], refs[YN:YN + ZN], refs[YN + ZN]
-    yout, outs = refs[YN + ZN + 1], refs[YN + ZN + 2:]
+    ys, own, other = refs[0:YN], refs[YN:YN + ZN], refs[YN + ZN:YN + 2 * ZN]
+    yout, outs = refs[YN + 2 * ZN], refs[YN + 2 * ZN + 1:]
     yq, core = where_ref[0], where_ref[3]
     for d in range(YN):
         q = lax.rem(yq + d, YN)
@@ -348,7 +348,7 @@
         far = pl.multiple_of(((1 - core) * ZN + q) * share, share)
         for k in range(3):
             outs[k][pl.ds(at, share), :] = own[d][k]
-            outs[k][pl.ds(far, share), :] = other[d, k]
+            outs[k][pl.ds(far, share), :] = other[d][k]
 
 
 def place(where, ys, own, other):
@@ -359,10 +359,10 @@
             jax.ShapeDtypeStruct((TCAP, R), F32),
             *[jax.ShapeDtypeStruct((R, R), F32)] * 3,
         ),
-        in_specs=[pl.BlockSpec(memory_space=pltpu.SMEM)] + [vm] * (YN + ZN + 1),
+        in_specs=[pl.BlockSpec(memory_space=pltpu.SMEM)] + [vm] * (YN + 2 * ZN),
         out_specs=(vm,) * 4,
         compiler_params=pltpu.CompilerParams(vmem_limit_bytes=10 << 20),
-    )(where, *inside(*ys, *own, other))
+    )(where, *inside(*ys, *own, *other))
 
 
 FIRST = ("x", "z")
@@ -448,7 +448,7 @@
     mine = gathered_sum(mine, LAST)
     mine = gathered_sum(mine, SAME["y"])
     own = ring(mine, FIRST)
-    other = fetch(jnp.stack(own), SAME["c"], 1)
+    other = [fetch(v, SAME["c"], 1) for v in own]
     y, g0, g1, g2 = place(where, ys, own, other)
     return (y, zfin, g0, g1, g2)
 

time: 170 us -> 159 us (0.935)
  waiting for transfers between devices: 78.7 us -> 59.6 us
  starting transfers between devices: 61.7 us -> 69.3 us
    ppermute x27 -> x30, waiting for transfers between devices: 35.6 us -> 16.3 us  [fetch(): return lax.ppermute(v, ALL, [(b, a) for a, b in shifted(axes, d)])]
    ppermute x27 -> x30, starting transfers between devices: 40.2 us -> 47.9 us  [fetch(): return lax.ppermute(v, ALL, [(b, a) for a, b in shifted(axes, d)])]
  transfers between devices with their start and end apart: 40 -> 43, of which waited for: 26 -> 23; matrix products, arithmetic and copies ran while one was open for 1% -> 1% of each run, Pallas kernels for 8% -> 9%
where the time goes in v7:
time: 159 us
  starting transfers between devices  69.3 us (44%)
  waiting for transfers between devices  59.6 us (37%)
  Pallas kernels  25.4 us (16%)
  between operations  2.08 us (1%)
  other arithmetic  1.66 us (1%)
    ppermute x30, starting transfers between devices, fetch(): return lax.ppermute(v, ALL, [(b, a) for a, b in shifted(axes, d)])  47.9 us
    ppermute x13, waiting for transfers between devices, give(): return lax.ppermute(v, ALL, shifted(axes, d))  43.3 us
    ppermute x13, starting transfers between devices, give(): return lax.ppermute(v, ALL, shifted(axes, d))  21.5 us
    pallas_call x4, Pallas kernels, sketch(): pl.pallas_call(functools.partial(sketch_kernel, m, last), out_shape=tuple...  17.1 us
    ppermute x30, waiting for transfers between devices, fetch(): return lax.ppermute(v, ALL, [(b, a) for a, b in shifted(axes, d)])  16.3 us
  transfers between devices with their start and end apart: 43, of which 23 were waited for; matrix products, arithmetic and copies ran while one was open for 1% of the time, Pallas kernels for 9%

profile of v7, /device:TPU:1, one launch (start us, length us, event | category | flops | bytes accessed | tf_op | source)
XLA Modules:
  0.0 158.7 jit_solution(9318687160019973408)
XLA Ops:
  2.5 2.2 %shard_map.101 = (bf16[288,256]{1,0:T(8,128)(2,1)}, bf16[576,256]{1,0:T(8,128)(2,1)}) custom-call(s32[6]{0:T(128)} %stack.34.where_ref.refs_0_, f32[3,1024]{1,0:T(4,128)} %txyz_ref.1, f32[3,512]{1,0:T(4,128)} %sxyz_ref.1, bf16[1024,256]{1,0:T(8,128)(2,1)} %psi_ref.1, bf16[512,256]{1,0:T(8,128)(2,1)} %omega_ref.1), custom_call_target="tpu_custom_call" | custom-call | tf_op jit(solution)/shard_map/pallas_call | solution.py:82
  4.7 3.6 %collective-permute-start.3 = (bf16[576,256]{1,0:T(8,128)(2,1)}, bf16[576,256]{1,0:T(8,128)(2,1)S(1)}, u32[]{:S(2)}, u32[]{:S(2)}) collective-permute-start(bf16[576,256]{1,0:T(8,128)(2,1)} %get-tuple-element.28.refs_0_), channel_id=1, source_target_pairs={{1,0},{2,1},{3,2},{0,3},{5,4},{6,5},{7,6},{4,7},{9,8},{10,9},{11,1... | collective-permute-start | bytes 884744 | tf_op jit(solution)/shard_map/ppermute | solution.py:389
  8.3 1.6 %collective-permute-start.2 = (bf16[288,256]{1,0:T(8,128)(2,1)}, bf16[288,256]{1,0:T(8,128)(2,1)S(1)}, u32[]{:S(2)}, u32[]{:S(2)}) collective-permute-start(bf16[288,256]{1,0:T(8,128)(2,1)} %get-tuple-element.27.refs_9_), channel_id=1, source_target_pairs={{24,0},{25,1},{26,2},{27,3},{100,4},{101,5},{102,6},{103,7},{0,8},... | collective-permute-start | bytes 442376 | tf_op jit(solution)/shard_map/ppermute | solution.py:389
  11.0 3.3 %collective-permute-start.1 = (bf16[288,256]{1,0:T(8,128)(2,1)}, bf16[288,256]{1,0:T(8,128)(2,1)S(1)}, u32[]{:S(2)}, u32[]{:S(2)}) collective-permute-start(bf16[288,256]{1,0:T(8,128)(2,1)} %get-tuple-element.27.refs_9_), channel_id=1, source_target_pairs={{16,0},{17,1},{18,2},{19,3},{68,4},{69,5},{70,6},{71,7},{24,8},{25... | collective-permute-start | bytes 442376 | tf_op jit(solution)/shard_map/ppermute | solution.py:389
  20.5 1.7 %collective-permute-start.7 = (bf16[576,256]{1,0:T(8,128)(2,1)S(1)}, bf16[576,256]{1,0:T(8,128)(2,1)S(1)}, u32[]{:S(2)}, u32[]{:S(2)}) collective-permute-start(bf16[576,256]{1,0:T(8,128)(2,1)S(1)} %collective-permute-done.3.refs_1_), channel_id=1, source_target_pairs={{4,0},{5,1},{6,2},{7,3},{0,4},{1,5},{2,6},{3,7},{12,8},{13,9},{14,... | collective-permute-start | bytes 884744 | tf_op jit(solution)/shard_map/ppermute | solution.py:389
  26.9 2.7 %collective-permute-start.12 = (bf16[4,288,256]{2,1,0:T(8,128)(2,1)S(1)}, bf16[4,288,256]{2,1,0:T(8,128)(2,1)S(1)}, u32[]{:S(2)}, u32[]{:S(2)}) collective-permute-start(bf16[4,288,256]{2,1,0:T(8,128)(2,1)S(1)} %pad_maximum_fusion.refs_0_), channel_id=1, source_target_pairs={{64,0},{65,1},{66,2},{67,3},{20,4},{21,5},{22,6},{23,7},{72,8},{73... | collective-permute-start | bytes 1769480 | tf_op jit(solution)/shard_map/ppermute | solution.py:389
  32.6 2.1 %shard_map.102 = (bf16[5120,256]{1,0:T(8,128)(2,1)S(1)}, f32[10,8,512]{2,1,0:T(8,128)S(1)}, f32[16,128]{1,0:T(8,128)S(1)}) custom-call(bf16[576,256]{1,0:T(8,128)(2,1)} %get-tuple-element.28.refs_0_, bf16[576,256]{1,0:T(8,128)(2,1)S(1)} %collective-permute-done.3.refs_1_, bf16[576,256]{1,0:T(8,128)(2,1)S(1)} %collective-permute-done.4.refs_2_, ...), custom_call_target="tpu_custom_call" | custom-call | tf_op jit(solution)/shard_map/pallas_call | solution.py:146
  34.7 4.0 %shard_map.103 = (f32[4,256,256]{2,1,0:T(8,128)S(1)}, f32[5120,256]{1,0:T(8,128)S(1)}) custom-call(bf16[4,288,256]{2,1,0:T(8,128)(2,1)S(1)} %pad_maximum_fusion.refs_0_, bf16[5120,256]{1,0:T(8,128)(2,1)S(1)} %get-tuple-element.29.refs_1_, f32[10,8,512]{2,1,0:T(8,128)S(1)} %get-tuple-element.30.refs_2_, f32[16,128]{1,0:T(8,128)S(1)} %get-tuple-element.31.refs_3_), custom_call_target="tpu_custom_call" | custom-call | tf_op jit(solution)/shard_map/pallas_call | solution.py:274
  38.7 4.0 %shard_map.105 = (f32[4,256,256]{2,1,0:T(8,128)S(1)}, f32[5120,256]{1,0:T(8,128)S(1)}) custom-call(bf16[4,288,256]{2,1,0:T(8,128)(2,1)S(1)} %collective-permute-done.13.refs_0_, bf16[5120,256]{1,0:T(8,128)(2,1)S(1)} %get-tuple-element.29.refs_1_, f32[10,8,512]{2,1,0:T(8,128)S(1)} %get-tuple-element.30.refs_2_, f32[16,128]{1,0:T(8,128)S(1)} %get-tuple-element.31.refs_3_), custom_call_target="tpu_custom_call" | custom-call | tf_op jit(solution)/shard_map/pallas_call | solution.py:274
  42.7 4.0 %shard_map.104 = (f32[4,256,256]{2,1,0:T(8,128)S(1)}, f32[5120,256]{1,0:T(8,128)S(1)}) custom-call(bf16[4,288,256]{2,1,0:T(8,128)(2,1)S(1)} %collective-permute-done.10.refs_0_, bf16[5120,256]{1,0:T(8,128)(2,1)S(1)} %get-tuple-element.29.refs_1_, f32[10,8,512]{2,1,0:T(8,128)S(1)} %get-tuple-element.30.refs_2_, f32[16,128]{1,0:T(8,128)S(1)} %get-tuple-element.31.refs_3_), custom_call_target="tpu_custom_call" | custom-call | tf_op jit(solution)/shard_map/pallas_call | solution.py:274
  46.6 5.2 %shard_map.106 = (f32[4,256,256]{2,1,0:T(8,128)S(1)}, f32[4,512,256]{2,1,0:T(8,128)S(1)}, f32[4,512,256]{2,1,0:T(8,128)S(1)}) custom-call(bf16[4,288,256]{2,1,0:T(8,128)(2,1)S(1)} %collective-permute-done.12.refs_0_, bf16[5120,256]{1,0:T(8,128)(2,1)S(1)} %get-tuple-element.29.refs_1_, f32[10,8,512]{2,1,0:T(8,128)S(1)} %get-tuple-element.30.refs_2_, ...), custom_call_target="tpu_custom_call" | custom-call | tf_op jit(solution)/shard_map/pallas_call | solution.py:274
  52.3 3.0 %collective-permute-start.14 = (f32[4,256,256]{2,1,0:T(8,128)S(1)}, f32[4,256,256]{2,1,0:T(8,128)S(1)}, u32[]{:S(2)}, u32[]{:S(2)}) collective-permute-start(f32[4,256,256]{2,1,0:T(8,128)S(1)} %get-tuple-element.37), channel_id=1, source_target_pairs={{0,64},{1,65},{2,66},{3,67},{4,20},{5,21},{6,22},{7,23},{8,72},{9,... | collective-permute-start | bytes 3145736 | tf_op jit(solution)/shard_map/ppermute | solution.py:393
  55.9 10.3 %collective-permute-done.15 = f32[4,256,256]{2,1,0:T(8,128)S(1)} collective-permute-done((f32[4,256,256]{2,1,0:T(8,128)S(1)}, f32[4,256,256]{2,1,0:T(8,128)S(1)}, u32[]{:S(2)}, u32[]{:S(2)}) %collective-permute-start.15) | collective-permute-done | bytes 1048608 | tf_op jit(solution)/shard_map/ppermute | solution.py:393
  67.8 11.2 %collective-permute-done.11 = f32[4,256,256]{2,1,0:T(8,128)S(1)} collective-permute-done((f32[4,256,256]{2,1,0:T(8,128)S(1)}, f32[4,256,256]{2,1,0:T(8,128)S(1)}, u32[]{:S(2)}, u32[]{:S(2)}) %collective-permute-start.11) | collective-permute-done | bytes 1048608 | tf_op jit(solution)/shard_map/ppermute | solution.py:393
  79.3 3.7 %collective-permute-start.16 = (f32[256,256]{1,0:T(8,128)S(1)}, f32[256,256]{1,0:T(8,128)S(1)}, u32[]{:S(2)}, u32[]{:S(2)}) collective-permute-start(f32[256,256]{1,0:T(8,128)S(1)} %get-tuple-element.55), channel_id=1, source_target_pairs={{0,8},{1,9},{2,10},{3,11},{4,36},{5,37},{6,38},{7,39},{8,16},{9,17... | collective-permute-start | bytes 786440 | tf_op jit(solution)/shard_map/ppermute | solution.py:393
  83.3 4.5 %collective-permute-start.21 = (f32[512,256]{1,0:T(8,128)S(1)}, f32[512,256]{1,0:T(8,128)S(1)}, u32[]{:S(2)}, u32[]{:S(2)}) collective-permute-start(f32[512,256]{1,0:T(8,128)S(1)} %get-tuple-element.50), channel_id=1, source_target_pairs={{0,2},{1,3},{2,0},{3,1},{4,6},{5,7},{6,4},{7,5},{8,10},{9,11},{10,... | collective-permute-start | bytes 1572872 | tf_op jit(solution)/shard_map/ppermute | solution.py:393
  87.8 2.5 %collective-permute-start.17 = (f32[256,256]{1,0:T(8,128)S(1)}, f32[256,256]{1,0:T(8,128)S(1)}, u32[]{:S(2)}, u32[]{:S(2)}) collective-permute-start(f32[256,256]{1,0:T(8,128)S(1)} %get-tuple-element.54), channel_id=1, source_target_pairs={{0,16},{1,17},{2,18},{3,19},{4,68},{5,69},{6,70},{7,71},{8,24},{9,... | collective-permute-start | bytes 786440 | tf_op jit(solution)/shard_map/ppermute | solution.py:393
  90.3 2.0 %collective-permute-start.18 = (f32[256,256]{1,0:T(8,128)S(1)}, f32[256,256]{1,0:T(8,128)S(1)}, u32[]{:S(2)}, u32[]{:S(2)}) collective-permute-start(f32[256,256]{1,0:T(8,128)S(1)} %get-tuple-element.53), channel_id=1, source_target_pairs={{0,24},{1,25},{2,26},{3,27},{4,100},{5,101},{6,102},{7,103},{8,0},... | collective-permute-start | bytes 786440 | tf_op jit(solution)/shard_map/ppermute | solution.py:393
  92.4 2.5 %collective-permute-done.17.refs_3_ = f32[256,256]{1,0:T(8,128)S(1)} collective-permute-done((f32[256,256]{1,0:T(8,128)S(1)}, f32[256,256]{1,0:T(8,128)S(1)}, u32[]{:S(2)}, u32[]{:S(2)}) %collective-permute-start.17) | collective-permute-done | bytes 262176 | tf_op jit(solution)/shard_map/ppermute | solution.py:393
  94.8 2.0 %collective-permute-done.18.refs_4_ = f32[256,256]{1,0:T(8,128)S(1)} collective-permute-done((f32[256,256]{1,0:T(8,128)S(1)}, f32[256,256]{1,0:T(8,128)S(1)}, u32[]{:S(2)}, u32[]{:S(2)}) %collective-permute-start.18) | collective-permute-done | bytes 262176 | tf_op jit(solution)/shard_map/ppermute | solution.py:393
  98.4 12.1 %collective-permute-done.21.refs_7_ = f32[512,256]{1,0:T(8,128)S(1)} collective-permute-done((f32[512,256]{1,0:T(8,128)S(1)}, f32[512,256]{1,0:T(8,128)S(1)}, u32[]{:S(2)}, u32[]{:S(2)}) %collective-permute-start.21) | collective-permute-done | bytes 524320 | tf_op jit(solution)/shard_map/ppermute | solution.py:393
  110.6 2.0 %shard_map.107 = (f32[256,256]{1,0:T(8,128)S(1)}, f32[512,256]{1,0:T(8,128)}, f32[3,128,256]{2,1,0:T(8,128)S(1)}, f32[3,128,256]{2,1,0:T(8,128)S(1)}) custom-call(s32[6]{0:T(128)S(1)} %copy-done.1, f32[256,256]{1,0:T(8,128)S(1)} %get-tuple-element.56.refs_1_, f32[256,256]{1,0:T(8,128)S(1)} %collective-permute-done.16.refs_2_, ...), custom_call_target="tpu_custom_call" | custom-call | tf_op jit(solution)/shard_map/pallas_call | solution.py:320
  118.1 2.0 %collective-permute-start.29 = (f32[3,32,256]{2,1,0:T(8,128)S(1)}, f32[3,32,256]{2,1,0:T(8,128)S(1)}, u32[]{:S(2)}, u32[]{:S(2)}) collective-permute-start(f32[3,32,256]{2,1,0:T(8,128)S(1)} %get-tuple-element.57), channel_id=1, source_target_pairs={{0,24},{1,25},{2,26},{3,27},{4,100},{5,101},{6,102},{7,103},{8,0},... | collective-permute-start | bytes 294920 | tf_op jit(solution)/shard_map/ppermute | solution.py:393
  125.7 3.7 %collective-permute-done.32 = f32[3,32,256]{2,1,0:T(8,128)S(1)} collective-permute-done((f32[3,32,256]{2,1,0:T(8,128)S(1)}, f32[3,32,256]{2,1,0:T(8,128)S(1)}, u32[]{:S(2)}, u32[]{:S(2)}) %collective-permute-start.32) | collective-permute-done | bytes 98336 | tf_op jit(solution)/shard_map/ppermute | solution.py:389
  129.4 1.9 %collective-permute-start.34 = (f32[3,32,256]{2,1,0:T(8,128)S(1)}, f32[3,32,256]{2,1,0:T(8,128)S(1)}, u32[]{:S(2)}, u32[]{:S(2)}) collective-permute-start(f32[3,32,256]{2,1,0:T(8,128)S(1)} %add_add_fusion.1), channel_id=1, source_target_pairs={{1,0},{2,1},{3,2},{0,3},{5,4},{6,5},{7,6},{4,7},{9,8},{10,9},{11,1... | collective-permute-start | bytes 294920 | tf_op jit(solution)/shard_map/ppermute | solution.py:389
  134.0 2.4 %collective-permute-start.24 = (f32[256,256]{1,0:T(8,128)S(1)}, f32[256,256]{1,0:T(8,128)S(1)}, u32[]{:S(2)}, u32[]{:S(2)}) collective-permute-start(f32[256,256]{1,0:T(8,128)S(1)} %get-tuple-element.41.refs_0_), channel_id=1, source_target_pairs={{2,0},{3,1},{0,2},{1,3},{6,4},{7,5},{4,6},{5,7},{10,8},{11,9},{8,1... | collective-permute-start | bytes 786440 | tf_op jit(solution)/shard_map/ppermute | solution.py:389
  137.1 2.4 %collective-permute-start.36 = (f32[3,32,256]{2,1,0:T(8,128)S(1)}, f32[3,32,256]{2,1,0:T(8,128)S(1)}, u32[]{:S(2)}, u32[]{:S(2)}) collective-permute-start(f32[3,32,256]{2,1,0:T(8,128)S(1)} %add_add_fusion.refs_4_), channel_id=1, source_target_pairs={{8,0},{9,1},{10,2},{11,3},{36,4},{37,5},{38,6},{39,7},{16,8},{17,9... | collective-permute-start | bytes 294920 | tf_op jit(solution)/shard_map/ppermute | solution.py:389
  139.7 2.9 %collective-permute-done.23.refs_1_ = f32[256,256]{1,0:T(8,128)S(1)} collective-permute-done((f32[256,256]{1,0:T(8,128)S(1)}, f32[256,256]{1,0:T(8,128)S(1)}, u32[]{:S(2)}, u32[]{:S(2)}) %collective-permute-start.23) | collective-permute-done | bytes 262176 | tf_op jit(solution)/shard_map/ppermute | solution.py:389
  142.6 7.2 %collective-permute-start.39 = (f32[3,32,256]{2,1,0:T(8,128)S(1)}, f32[3,32,256]{2,1,0:T(8,128)S(1)}, u32[]{:S(2)}, u32[]{:S(2)}) collective-permute-start(f32[3,32,256]{2,1,0:T(8,128)S(1)} %add_add_fusion.refs_4_), channel_id=1, source_target_pairs={{4,0},{5,1},{6,2},{7,3},{0,4},{1,5},{2,6},{3,7},{12,8},{13,9},{14,... | collective-permute-start | bytes 294920 | tf_op jit(solution)/shard_map/ppermute | solution.py:389
  149.8 2.3 %collective-permute-start.40 = (f32[3,32,256]{2,1,0:T(8,128)S(1)}, f32[3,32,256]{2,1,0:T(8,128)S(1)}, u32[]{:S(2)}, u32[]{:S(2)}) collective-permute-start(f32[3,32,256]{2,1,0:T(8,128)S(1)} %collective-permute-done.36.refs_5_), channel_id=1, source_target_pairs={{4,0},{5,1},{6,2},{7,3},{0,4},{1,5},{2,6},{3,7},{12,8},{13,9},{14,... | collective-permute-start | bytes 294920 | tf_op jit(solution)/shard_map/ppermute | solution.py:389
  152.1 3.0 %collective-permute-start.41 = (f32[3,32,256]{2,1,0:T(8,128)S(1)}, f32[3,32,256]{2,1,0:T(8,128)S(1)}, u32[]{:S(2)}, u32[]{:S(2)}) collective-permute-start(f32[3,32,256]{2,1,0:T(8,128)S(1)} %collective-permute-done.37.refs_6_), channel_id=1, source_target_pairs={{4,0},{5,1},{6,2},{7,3},{0,4},{1,5},{2,6},{3,7},{12,8},{13,9},{14,... | collective-permute-start | bytes 294920 | tf_op jit(solution)/shard_map/ppermute | solution.py:389
  156.8 1.9 %shard_map.108 = (f32[1024,256]{1,0:T(8,128)}, f32[256,256]{1,0:T(8,128)}, f32[256,256]{1,0:T(8,128)}, f32[256,256]{1,0:T(8,128)}) custom-call(s32[6]{0:T(128)S(1)} %copy-done.1, f32[256,256]{1,0:T(8,128)S(1)} %get-tuple-element.41.refs_0_, f32[256,256]{1,0:T(8,128)S(1)} %collective-permute-done.23.refs_1_, f32[256,256]{1,0:T(8,128)S(1)} %collective-permute-done.24.refs_2_, ...), custom_call_target="tpu_custom_call" | custom-call | tf_op jit(solution)/shard_map/pallas_call | solution.py:356
  (75 shorter events, 36.8 us)
Async XLA Ops:
  4.7 15.7 %collective-permute-start.3 = (bf16[576,256]{1,0:T(8,128)(2,1)}, bf16[576,256]{1,0:T(8,128)(2,1)S(1)}, u32[]{:S(2)}, u32[]{:S(2)}) collective-permute-start(bf16[576,256]{1,0:T(8,128)(2,1)} %get-tuple-element.28.refs_0_), channel_id=1, source_target_pairs={{1,0},{2,1},{3,2},{0,3},{5,4},{6,5},{7,6},{4,7},{9,8},{10,9},{11,1... | collective-permute-start | bytes 884744 | tf_op jit(solution)/shard_map/ppermute | solution.py:389
  8.3 6.8 %collective-permute-start.2 = (bf16[288,256]{1,0:T(8,128)(2,1)}, bf16[288,256]{1,0:T(8,128)(2,1)S(1)}, u32[]{:S(2)}, u32[]{:S(2)}) collective-permute-start(bf16[288,256]{1,0:T(8,128)(2,1)} %get-tuple-element.27.refs_9_), channel_id=1, source_target_pairs={{24,0},{25,1},{26,2},{27,3},{100,4},{101,5},{102,6},{103,7},{0,8},... | collective-permute-start | bytes 442376 | tf_op jit(solution)/shard_map/ppermute | solution.py:389
  9.9 14.5 %collective-permute-start.4 = (bf16[576,256]{1,0:T(8,128)(2,1)}, bf16[576,256]{1,0:T(8,128)(2,1)S(1)}, u32[]{:S(2)}, u32[]{:S(2)}) collective-permute-start(bf16[576,256]{1,0:T(8,128)(2,1)} %get-tuple-element.28.refs_0_), channel_id=1, source_target_pairs={{2,0},{3,1},{0,2},{1,3},{6,4},{7,5},{4,6},{5,7},{10,8},{11,9},{8,1... | collective-permute-start | bytes 884744 | tf_op jit(solution)/shard_map/ppermute | solution.py:389
  10.3 16.6 %collective-permute-start.5 = (bf16[576,256]{1,0:T(8,128)(2,1)}, bf16[576,256]{1,0:T(8,128)(2,1)S(1)}, u32[]{:S(2)}, u32[]{:S(2)}) collective-permute-start(bf16[576,256]{1,0:T(8,128)(2,1)} %get-tuple-element.28.refs_0_), channel_id=1, source_target_pairs={{3,0},{0,1},{1,2},{2,3},{7,4},{4,5},{5,6},{6,7},{11,8},{8,9},{9,10... | collective-permute-start | bytes 884744 | tf_op jit(solution)/shard_map/ppermute | solution.py:389
  11.0 6.9 %collective-permute-start.1 = (bf16[288,256]{1,0:T(8,128)(2,1)}, bf16[288,256]{1,0:T(8,128)(2,1)S(1)}, u32[]{:S(2)}, u32[]{:S(2)}) collective-permute-start(bf16[288,256]{1,0:T(8,128)(2,1)} %get-tuple-element.27.refs_9_), channel_id=1, source_target_pairs={{16,0},{17,1},{18,2},{19,3},{68,4},{69,5},{70,6},{71,7},{24,8},{25... | collective-permute-start | bytes 442376 | tf_op jit(solution)/shard_map/ppermute | solution.py:389
  15.1 7.1 %collective-permute-start = (bf16[288,256]{1,0:T(8,128)(2,1)}, bf16[288,256]{1,0:T(8,128)(2,1)S(1)}, u32[]{:S(2)}, u32[]{:S(2)}) collective-permute-start(bf16[288,256]{1,0:T(8,128)(2,1)} %get-tuple-element.27.refs_9_), channel_id=1, source_target_pairs={{8,0},{9,1},{10,2},{11,3},{36,4},{37,5},{38,6},{39,7},{16,8},{17,9... | collective-permute-start | bytes 442376 | tf_op jit(solution)/shard_map/ppermute | solution.py:389
  17.8 11.8 %collective-permute-start.6 = (bf16[576,256]{1,0:T(8,128)(2,1)}, bf16[576,256]{1,0:T(8,128)(2,1)S(1)}, u32[]{:S(2)}, u32[]{:S(2)}) collective-permute-start(bf16[576,256]{1,0:T(8,128)(2,1)} %get-tuple-element.28.refs_0_), channel_id=1, source_target_pairs={{4,0},{5,1},{6,2},{7,3},{0,4},{1,5},{2,6},{3,7},{12,8},{13,9},{14,... | collective-permute-start | bytes 884744 | tf_op jit(solution)/shard_map/ppermute | solution.py:389
  20.5 10.5 %collective-permute-start.7 = (bf16[576,256]{1,0:T(8,128)(2,1)S(1)}, bf16[576,256]{1,0:T(8,128)(2,1)S(1)}, u32[]{:S(2)}, u32[]{:S(2)}) collective-permute-start(bf16[576,256]{1,0:T(8,128)(2,1)S(1)} %collective-permute-done.3.refs_1_), channel_id=1, source_target_pairs={{4,0},{5,1},{6,2},{7,3},{0,4},{1,5},{2,6},{3,7},{12,8},{13,9},{14,... | collective-permute-start | bytes 884744 | tf_op jit(solution)/shard_map/ppermute | solution.py:389
  23.1 15.6 %collective-permute-start.13 = (bf16[4,288,256]{2,1,0:T(8,128)(2,1)S(1)}, bf16[4,288,256]{2,1,0:T(8,128)(2,1)S(1)}, u32[]{:S(2)}, u32[]{:S(2)}) collective-permute-start(bf16[4,288,256]{2,1,0:T(8,128)(2,1)S(1)} %pad_maximum_fusion.refs_0_), channel_id=1, source_target_pairs={{96,0},{97,1},{98,2},{99,3},{28,4},{29,5},{30,6},{31,7},{104,8},{1... | collective-permute-start | bytes 1769480 | tf_op jit(solution)/shard_map/ppermute | solution.py:389
  24.4 18.2 %collective-permute-start.10 = (bf16[4,288,256]{2,1,0:T(8,128)(2,1)S(1)}, bf16[4,288,256]{2,1,0:T(8,128)(2,1)S(1)}, u32[]{:S(2)}, u32[]{:S(2)}) collective-permute-start(bf16[4,288,256]{2,1,0:T(8,128)(2,1)S(1)} %pad_maximum_fusion.refs_0_), channel_id=1, source_target_pairs={{32,0},{33,1},{34,2},{35,3},{12,4},{13,5},{14,6},{15,7},{40,8},{41... | collective-permute-start | bytes 1769480 | tf_op jit(solution)/shard_map/ppermute | solution.py:389
  26.9 19.8 %collective-permute-start.12 = (bf16[4,288,256]{2,1,0:T(8,128)(2,1)S(1)}, bf16[4,288,256]{2,1,0:T(8,128)(2,1)S(1)}, u32[]{:S(2)}, u32[]{:S(2)}) collective-permute-start(bf16[4,288,256]{2,1,0:T(8,128)(2,1)S(1)} %pad_maximum_fusion.refs_0_), channel_id=1, source_target_pairs={{64,0},{65,1},{66,2},{67,3},{20,4},{21,5},{22,6},{23,7},{72,8},{73... | collective-permute-start | bytes 1769480 | tf_op jit(solution)/shard_map/ppermute | solution.py:389
  51.9 31.1 %collective-permute-start.19 = (f32[4,512,256]{2,1,0:T(8,128)S(1)}, f32[4,512,256]{2,1,0:T(8,128)S(1)}, u32[]{:S(2)}, u32[]{:S(2)}) collective-permute-start(f32[4,512,256]{2,1,0:T(8,128)S(1)} %get-tuple-element.40), channel_id=1, source_target_pairs={{0,4},{1,5},{2,6},{3,7},{4,0},{5,1},{6,2},{7,3},{8,12},{9,13},{10,... | collective-permute-start | bytes 6291464 | tf_op jit(solution)/shard_map/ppermute | solution.py:393
  52.3 13.9 %collective-permute-start.15 = (f32[4,256,256]{2,1,0:T(8,128)S(1)}, f32[4,256,256]{2,1,0:T(8,128)S(1)}, u32[]{:S(2)}, u32[]{:S(2)}) collective-permute-start(f32[4,256,256]{2,1,0:T(8,128)S(1)} %get-tuple-element.38), channel_id=1, source_target_pairs={{0,96},{1,97},{2,98},{3,99},{4,28},{5,29},{6,30},{7,31},{8,104},{9... | collective-permute-start | bytes 3145736 | tf_op jit(solution)/shard_map/ppermute | solution.py:393
  52.3 15.5 %collective-permute-start.14 = (f32[4,256,256]{2,1,0:T(8,128)S(1)}, f32[4,256,256]{2,1,0:T(8,128)S(1)}, u32[]{:S(2)}, u32[]{:S(2)}) collective-permute-start(f32[4,256,256]{2,1,0:T(8,128)S(1)} %get-tuple-element.37), channel_id=1, source_target_pairs={{0,64},{1,65},{2,66},{3,67},{4,20},{5,21},{6,22},{7,23},{8,72},{9,... | collective-permute-start | bytes 3145736 | tf_op jit(solution)/shard_map/ppermute | solution.py:393
  55.3 23.7 %collective-permute-start.11 = (f32[4,256,256]{2,1,0:T(8,128)S(1)}, f32[4,256,256]{2,1,0:T(8,128)S(1)}, u32[]{:S(2)}, u32[]{:S(2)}) collective-permute-start(f32[4,256,256]{2,1,0:T(8,128)S(1)} %get-tuple-element.33), channel_id=1, source_target_pairs={{0,32},{1,33},{2,34},{3,35},{4,12},{5,13},{6,14},{7,15},{8,40},{9,... | collective-permute-start | bytes 3145736 | tf_op jit(solution)/shard_map/ppermute | solution.py:393
  79.3 11.0 %collective-permute-start.16 = (f32[256,256]{1,0:T(8,128)S(1)}, f32[256,256]{1,0:T(8,128)S(1)}, u32[]{:S(2)}, u32[]{:S(2)}) collective-permute-start(f32[256,256]{1,0:T(8,128)S(1)} %get-tuple-element.55), channel_id=1, source_target_pairs={{0,8},{1,9},{2,10},{3,11},{4,36},{5,37},{6,38},{7,39},{8,16},{9,17... | collective-permute-start | bytes 786440 | tf_op jit(solution)/shard_map/ppermute | solution.py:393
  83.3 15.2 %collective-permute-start.20 = (f32[512,256]{1,0:T(8,128)S(1)}, f32[512,256]{1,0:T(8,128)S(1)}, u32[]{:S(2)}, u32[]{:S(2)}) collective-permute-start(f32[512,256]{1,0:T(8,128)S(1)} %get-tuple-element.51), channel_id=1, source_target_pairs={{0,1},{1,2},{2,3},{3,0},{4,5},{5,6},{6,7},{7,4},{8,9},{9,10},{10,1... | collective-permute-start | bytes 1572872 | tf_op jit(solution)/shard_map/ppermute | solution.py:393
  83.3 27.2 %collective-permute-start.21 = (f32[512,256]{1,0:T(8,128)S(1)}, f32[512,256]{1,0:T(8,128)S(1)}, u32[]{:S(2)}, u32[]{:S(2)}) collective-permute-start(f32[512,256]{1,0:T(8,128)S(1)} %get-tuple-element.50), channel_id=1, source_target_pairs={{0,2},{1,3},{2,0},{3,1},{4,6},{5,7},{6,4},{7,5},{8,10},{9,11},{10,... | collective-permute-start | bytes 1572872 | tf_op jit(solution)/shard_map/ppermute | solution.py:393
  87.8 22.7 %collective-permute-start.22 = (f32[512,256]{1,0:T(8,128)S(1)}, f32[512,256]{1,0:T(8,128)S(1)}, u32[]{:S(2)}, u32[]{:S(2)}) collective-permute-start(f32[512,256]{1,0:T(8,128)S(1)} %get-tuple-element.49), channel_id=1, source_target_pairs={{0,3},{1,0},{2,1},{3,2},{4,7},{5,4},{6,5},{7,6},{8,11},{9,8},{10,9... | collective-permute-start | bytes 1572872 | tf_op jit(solution)/shard_map/ppermute | solution.py:393
  87.8 7.0 %collective-permute-start.17 = (f32[256,256]{1,0:T(8,128)S(1)}, f32[256,256]{1,0:T(8,128)S(1)}, u32[]{:S(2)}, u32[]{:S(2)}) collective-permute-start(f32[256,256]{1,0:T(8,128)S(1)} %get-tuple-element.54), channel_id=1, source_target_pairs={{0,16},{1,17},{2,18},{3,19},{4,68},{5,69},{6,70},{7,71},{8,24},{9,... | collective-permute-start | bytes 786440 | tf_op jit(solution)/shard_map/ppermute | solution.py:393
  90.3 6.5 %collective-permute-start.18 = (f32[256,256]{1,0:T(8,128)S(1)}, f32[256,256]{1,0:T(8,128)S(1)}, u32[]{:S(2)}, u32[]{:S(2)}) collective-permute-start(f32[256,256]{1,0:T(8,128)S(1)} %get-tuple-element.53), channel_id=1, source_target_pairs={{0,24},{1,25},{2,26},{3,27},{4,100},{5,101},{6,102},{7,103},{8,0},... | collective-permute-start | bytes 786440 | tf_op jit(solution)/shard_map/ppermute | solution.py:393
  123.7 5.7 %collective-permute-start.32 = (f32[3,32,256]{2,1,0:T(8,128)S(1)}, f32[3,32,256]{2,1,0:T(8,128)S(1)}, u32[]{:S(2)}, u32[]{:S(2)}) collective-permute-start(f32[3,32,256]{2,1,0:T(8,128)S(1)} %fusion.12), channel_id=1, source_target_pairs={{96,0},{97,1},{98,2},{99,3},{28,4},{29,5},{30,6},{31,7},{104,8},{1... | collective-permute-start | bytes 294920 | tf_op jit(solution)/shard_map/ppermute | solution.py:389
  129.4 7.0 %collective-permute-start.34 = (f32[3,32,256]{2,1,0:T(8,128)S(1)}, f32[3,32,256]{2,1,0:T(8,128)S(1)}, u32[]{:S(2)}, u32[]{:S(2)}) collective-permute-start(f32[3,32,256]{2,1,0:T(8,128)S(1)} %add_add_fusion.1), channel_id=1, source_target_pairs={{1,0},{2,1},{3,2},{0,3},{5,4},{6,5},{7,6},{4,7},{9,8},{10,9},{11,1... | collective-permute-start | bytes 294920 | tf_op jit(solution)/shard_map/ppermute | solution.py:389
  131.4 5.7 %collective-permute-start.35 = (f32[3,32,256]{2,1,0:T(8,128)S(1)}, f32[3,32,256]{2,1,0:T(8,128)S(1)}, u32[]{:S(2)}, u32[]{:S(2)}) collective-permute-start(f32[3,32,256]{2,1,0:T(8,128)S(1)} %add_add_fusion.1), channel_id=1, source_target_pairs={{3,0},{0,1},{1,2},{2,3},{7,4},{4,5},{5,6},{6,7},{11,8},{8,9},{9,10... | collective-permute-start | bytes 294920 | tf_op jit(solution)/shard_map/ppermute | solution.py:389
  132.6 10.0 %collective-permute-start.23 = (f32[256,256]{1,0:T(8,128)S(1)}, f32[256,256]{1,0:T(8,128)S(1)}, u32[]{:S(2)}, u32[]{:S(2)}) collective-permute-start(f32[256,256]{1,0:T(8,128)S(1)} %get-tuple-element.41.refs_0_), channel_id=1, source_target_pairs={{1,0},{2,1},{3,2},{0,3},{5,4},{6,5},{7,6},{4,7},{9,8},{10,9},{11,1... | collective-permute-start | bytes 786440 | tf_op jit(solution)/shard_map/ppermute | solution.py:389
  134.0 8.6 %collective-permute-start.24 = (f32[256,256]{1,0:T(8,128)S(1)}, f32[256,256]{1,0:T(8,128)S(1)}, u32[]{:S(2)}, u32[]{:S(2)}) collective-permute-start(f32[256,256]{1,0:T(8,128)S(1)} %get-tuple-element.41.refs_0_), channel_id=1, source_target_pairs={{2,0},{3,1},{0,2},{1,3},{6,4},{7,5},{4,6},{5,7},{10,8},{11,9},{8,1... | collective-permute-start | bytes 786440 | tf_op jit(solution)/shard_map/ppermute | solution.py:389
  136.4 19.5 %collective-permute-start.25 = (f32[256,256]{1,0:T(8,128)S(1)}, f32[256,256]{1,0:T(8,128)S(1)}, u32[]{:S(2)}, u32[]{:S(2)}) collective-permute-start(f32[256,256]{1,0:T(8,128)S(1)} %get-tuple-element.41.refs_0_), channel_id=1, source_target_pairs={{3,0},{0,1},{1,2},{2,3},{7,4},{4,5},{5,6},{6,7},{11,8},{8,9},{9,10... | collective-permute-start | bytes 786440 | tf_op jit(solution)/shard_map/ppermute | solution.py:389
  137.1 12.7 %collective-permute-start.36 = (f32[3,32,256]{2,1,0:T(8,128)S(1)}, f32[3,32,256]{2,1,0:T(8,128)S(1)}, u32[]{:S(2)}, u32[]{:S(2)}) collective-permute-start(f32[3,32,256]{2,1,0:T(8,128)S(1)} %add_add_fusion.refs_4_), channel_id=1, source_target_pairs={{8,0},{9,1},{10,2},{11,3},{36,4},{37,5},{38,6},{39,7},{16,8},{17,9... | collective-permute-start | bytes 294920 | tf_op jit(solution)/shard_map/ppermute | solution.py:389
  139.6 12.5 %collective-permute-start.37 = (f32[3,32,256]{2,1,0:T(8,128)S(1)}, f32[3,32,256]{2,1,0:T(8,128)S(1)}, u32[]{:S(2)}, u32[]{:S(2)}) collective-permute-start(f32[3,32,256]{2,1,0:T(8,128)S(1)} %add_add_fusion.refs_4_), channel_id=1, source_target_pairs={{16,0},{17,1},{18,2},{19,3},{68,4},{69,5},{70,6},{71,7},{24,8},{25... | collective-permute-start | bytes 294920 | tf_op jit(solution)/shard_map/ppermute | solution.py:389
  142.6 12.5 %collective-permute-start.38 = (f32[3,32,256]{2,1,0:T(8,128)S(1)}, f32[3,32,256]{2,1,0:T(8,128)S(1)}, u32[]{:S(2)}, u32[]{:S(2)}) collective-permute-start(f32[3,32,256]{2,1,0:T(8,128)S(1)} %add_add_fusion.refs_4_), channel_id=1, source_target_pairs={{24,0},{25,1},{26,2},{27,3},{100,4},{101,5},{102,6},{103,7},{0,8},... | collective-permute-start | bytes 294920 | tf_op jit(solution)/shard_map/ppermute | solution.py:389
  142.6 13.3 %collective-permute-start.39 = (f32[3,32,256]{2,1,0:T(8,128)S(1)}, f32[3,32,256]{2,1,0:T(8,128)S(1)}, u32[]{:S(2)}, u32[]{:S(2)}) collective-permute-start(f32[3,32,256]{2,1,0:T(8,128)S(1)} %add_add_fusion.refs_4_), channel_id=1, source_target_pairs={{4,0},{5,1},{6,2},{7,3},{0,4},{1,5},{2,6},{3,7},{12,8},{13,9},{14,... | collective-permute-start | bytes 294920 | tf_op jit(solution)/shard_map/ppermute | solution.py:389
  149.8 6.0 %collective-permute-start.40 = (f32[3,32,256]{2,1,0:T(8,128)S(1)}, f32[3,32,256]{2,1,0:T(8,128)S(1)}, u32[]{:S(2)}, u32[]{:S(2)}) collective-permute-start(f32[3,32,256]{2,1,0:T(8,128)S(1)} %collective-permute-done.36.refs_5_), channel_id=1, source_target_pairs={{4,0},{5,1},{6,2},{7,3},{0,4},{1,5},{2,6},{3,7},{12,8},{13,9},{14,... | collective-permute-start | bytes 294920 | tf_op jit(solution)/shard_map/ppermute | solution.py:389
  (13 other events, 97.0 us)
